TPU v7x, 128 devices: a whole 4x4x4 slice. The times are simulated.
128 devices in a mesh: row: 8 (over z_hi, x), col: 16 (over y, z_lo, core).
Axes of the slice: x: 4, y: 4, z: 4 (z_hi: 2, z_lo: 2; z = z_hi * 2 + z_lo), core: 2. Of those that a mesh axis runs over, the one named last changes fastest.
Arguments:
- traces: bfloat16 [64, 16384], P(None, ('row', 'col')), may hold values from -6 to 6
- incident: bfloat16 [64, 16384], P(None, ('row', 'col')), may hold values from -6 to 6
- points: float32 [3, 16384], P(None, ('row', 'col')), may hold values from 0 to 1
- coupling: int32 [16384], P(('row', 'col')), may hold values from 0 to 2047, as said below
- volume_tiles: bfloat16 [32, 64, 4, 128, 128], P('row', 'col'), may hold values from -0.125 to 0.125
- tile_columns: int32 [32, 64, 4], P('row', 'col'), may hold values from 0 to 8, as said below
Outputs:
- traces_out: bfloat16 [64, 16384], P(None, ('row', 'col'))
- volume_out: float32 [64, 32, 64, 128], P(None, 'row', 'col')
Inputs may be any that keep to these rules, and one draw needn't show every extreme that they name: `coupling`: within each aligned block of 128 unknowns the values are distinct. `tile_columns`: the 4 entries of one tile are distinct, and one of them is 4.
All inputs are finite; a program needn't handle non-finite values.
Results may differ from a plain program's by a relative error of at most 0.0154.
Values may be sent and summed in bfloat16 or wider, within the bound.
No kernel may reach another device: no remote copies, remote signals or barrier semaphores. Data moves between devices by JAX's collectives and lax.ppermute only.
A program may use at most 64 MiB of HBM per device.

v0:
```python
import math

import jax
import jax.numpy as jnp
from jax import lax
from jax.experimental import pallas as pl
from jax.experimental.pallas import tpu as pltpu
from jax.sharding import PartitionSpec as P

E, U, S = 64, 128, 128
NR, NC = 8, 16
TOTAL = U * NR * NC
MB = 1 << 20
BF, F32 = jnp.bfloat16, jnp.float32
COS = (0.99999922, -19.73898252, 64.92872661, -85.27239691, 58.79403824, -21.07678136)
NT = (((1,), (1,)), ((), ()))
TN = (((0,), (0,)), ((), ()))

SPACING = float(TOTAL) ** (-1.0 / 3.0)
TURNS = 2.0 / SPACING / (2.0 * math.pi)
SMOOTH = (0.5 * SPACING) ** 2 * TURNS * TURNS
FACTOR = TURNS / math.sqrt(2.0 * TOTAL)


def dot(a, b, dims=(((1,), (0,)), ((), ()))):
    return lax.dot_general(a, b, dims, preferred_element_type=F32)


def call(body, out_shape, *, limit=24 * MB, flops=0, moved=0, **kwargs):
    return pl.pallas_call(
        body,
        out_shape=out_shape,
        compiler_params=pltpu.CompilerParams(vmem_limit_bytes=limit),
        cost_estimate=pl.CostEstimate(flops=flops, bytes_accessed=moved, transcendentals=0),
        **kwargs,
    )


def shape(dims, dtype):
    return jax.ShapeDtypeStruct(dims, dtype)


def split3(x):
    a = x.astype(BF).astype(F32)
    b = (x - a).astype(BF).astype(F32)
    return a, b, (x - a - b).astype(BF).astype(F32)


def rows_at(line, pieces):
    out = jnp.zeros((16, U), F32)
    for at, value in pieces:
        out = jnp.where(line == at, value, out)
    return out


def pack_body(traces, points, row_out, col_out):
    p = (points[...] - 0.5) * TURNS
    parts = split3(p)
    norm = jnp.sum(p * p, axis=0, keepdims=True)
    line = lax.broadcasted_iota(jnp.int32, (16, U), 0)
    source = [(3 * i + d, parts[i][d : d + 1]) for i in range(3) for d in range(3)]
    source += [(9 + i, v) for i, v in enumerate(split3(norm))] + [(12, 1.0)]
    source = rows_at(line, source).astype(BF)
    shifted = split3(norm + SMOOTH)
    target = []
    for j in range(3):
        pieces = [(3 * i + d, -2.0 * parts[j][d : d + 1]) for i in range(3) for d in range(3)]
        if j == 0:
            pieces += [(9 + i, 1.0) for i in range(3)]
        target.append(rows_at(line, pieces + [(12, shifted[j])]).astype(BF))
    for r in range(NR):
        for j in range(3):
            row_out[r, 16 * j : 16 * j + 16] = target[j]
    for c in range(NC):
        col_out[c, :E] = traces[...]
        col_out[c, E:] = source


def pack(traces, points):
    return call(pack_body, (shape((NR, 48, U), BF), shape((NC, E + 16, U), BF)))(traces, points)


def write_partials(acc, out):
    for d in range(NR):
        for j in range(3):
            b = d - 1 + j
            if 0 <= b < NR:
                out[d, j] = acc[:, b * U : b * U + U].astype(BF)
            else:
                out[d, j] = jnp.zeros((E, U), BF)


def kernel_body(col_ref, row_ref, k_ref, out_ref, acc, feats, dist):
    step = pl.program_id(0)

    @pl.when(step == 0)
    def _():
        for r in range(NR):
            feats[:, r * U : r * U + U] = row_ref[r]
        acc[...] = jnp.zeros_like(acc)

    for i in range(2):
        own = col_ref[i, E:]
        dist[i * U : i * U + U] = dot(jnp.concatenate([own, own, own], axis=0), feats[...], TN)

    def chunk(n, carry):
        at = pl.multiple_of(n * 16, 16)
        for h in range(2):
            d2 = dist[pl.ds(at, 16), h * 512 : h * 512 + 512]
            inv = lax.rsqrt(d2)
            turns = d2 * inv
            f = turns - jnp.round(turns)
            u = f * f
            value = COS[5] * FACTOR * u + COS[4] * FACTOR
            for c in COS[3::-1]:
                value = value * u + c * FACTOR
            k_ref[pl.ds(at, 16), h * 512 : h * 512 + 512] = (value * inv).astype(BF)
        return carry

    lax.fori_loop(0, 16, chunk, 0, unroll=2)
    p = jnp.concatenate([col_ref[0, :E], col_ref[1, :E]], axis=1)
    acc[...] += dot(p, k_ref[...])

    @pl.when(step == pl.num_programs(0) - 1)
    def _():
        write_partials(acc, out_ref)


def make_kernel(cols, rows):
    return call(
        kernel_body,
        (shape((NC * U, NR * U), BF), shape((NR, 3, E, U), BF)),
        flops=40 * 2 * MB,
        moved=6 * MB,
        grid=(NC // 2,),
        in_specs=[
            pl.BlockSpec((2, E + 16, U), lambda i: (i, 0, 0)),
            pl.BlockSpec((NR, 48, U), lambda i: (0, 0, 0)),
        ],
        out_specs=(
            pl.BlockSpec((2 * U, NR * U), lambda i: (i, 0)),
            pl.BlockSpec((NR, 3, E, U), lambda i: (0, 0, 0, 0)),
        ),
        scratch_shapes=[
            pltpu.VMEM((E, NR * U), F32),
            pltpu.VMEM((48, NR * U), BF),
            pltpu.VMEM((2 * U, NR * U), F32),
        ],
    )(cols, rows)


def product_body(p_ref, k_ref, out_ref, acc):
    step = pl.program_id(0)

    @pl.when(step == 0)
    def _():
        acc[...] = jnp.zeros_like(acc)

    p = jnp.concatenate([p_ref[i] for i in range(4)], axis=1)
    acc[...] += dot(p, k_ref[...])

    @pl.when(step == pl.num_programs(0) - 1)
    def _():
        write_partials(acc, out_ref)


def product(present, kernel):
    return call(
        product_body,
        shape((NR, 3, E, U), BF),
        flops=2 * E * 2 * MB,
        moved=5 * MB,
        grid=(NC // 4,),
        in_specs=[
            pl.BlockSpec((4, E, U), lambda i: (i, 0, 0)),
            pl.BlockSpec((4 * U, NR * U), lambda i: (i, 0)),
        ],
        out_specs=pl.BlockSpec((NR, 3, E, U), lambda i: (0, 0, 0, 0)),
        scratch_shapes=[pltpu.VMEM((E, NR * U), F32)],
    )(present, kernel)


def span(b):
    return ((0, 2), (1, 3)) if b == 0 else ((6, 0), (7, 1)) if b == 2 else tuple((2 + i, i) for i in range(4))


def sweep_body(last, own_ref, mid, left, right, inc, tiles, prev, nxt, lefts, rights, meta, moves, *rest):
    if last:
        present_out, field_out, src, srcf, f1 = rest
    else:
        present_out, src, srcf, f1 = rest
        field_out = None
    line = lax.broadcasted_iota(jnp.int32, (S, U), 0).astype(F32)

    def coupling(b):
        m = meta[b].astype(F32)
        return m[0:1], jnp.where(m[1:2] == line, 1.0, 0.0).astype(BF)

    def masked(c, hi, ids):
        return jnp.concatenate([c * jnp.where(hi == float(t), 1.0, 0.0).astype(BF) for t in ids], axis=0)

    for br in range(3):
        for bc in range(3):
            if br == 1 and bc == 1:
                continue
            hi, lo = coupling(3 * br + bc)
            c = (left, mid, right)[bc][br]
            places = [(R * 8 + C, i * 4 + j) for R, i in span(br) for C, j in span(bc)]
            out = dot(masked(c, hi, [t for _, t in places]), lo, NT).astype(BF)
            for n, (w, _) in enumerate(places):
                src[w] = out[n * E : n * E + E]
    hi, lo = coupling(4)
    own = own_ref[...]
    top = own.astype(BF)
    low = (own - top.astype(F32)).astype(BF)
    both = jnp.concatenate([masked(top, hi, range(16)), masked(low, hi, range(16))], axis=0)
    out = dot(both, lo, NT)
    out = out[: 16 * E] + out[16 * E :]
    for t in range(16):
        srcf[t] = out[t * E : t * E + E]
        src[(2 + t // 4) * 8 + 2 + t % 4] = out[t * E : t * E + E].astype(BF)

    def apply(values, base, block, tile, matrix):
        total = None
        for h in range(2):
            ks = (2 * h, 2 * h + 1)
            x = jnp.concatenate([values[base + moves[block, tile * 4 + k]] for k in ks], axis=1)
            a = jnp.concatenate([matrix(k) for k in ks], axis=1)
            y = dot(x, a, NT)
            total = y if total is None else total + y
        return total

    def own_tile(t, carry):
        i, j = t // 4, t % 4
        w = (2 + i) * 8 + 2 + j
        f1[w] = (srcf[t] + apply(src, w - 9, 4, t, lambda k: tiles[t * 4 + k])).astype(BF)
        return carry

    lax.fori_loop(0, 16, own_tile, 0, unroll=2)

    def halo(w, block, tile, ref, start):
        y = apply(src, w - 9, block, tile, lambda k: ref[pl.ds(pl.multiple_of(start + k * S, S), S), :])
        f1[w] = (src[w].astype(F32) + y).astype(BF)

    def edge_row(j, carry):
        halo(8 + 2 + j, 1, 12 + j, prev, j * 4 * S)
        halo(48 + 2 + j, 7, j, nxt, j * 4 * S)
        return carry

    lax.fori_loop(0, 4, edge_row, 0)

    def edge_col(i, carry):
        w = (2 + i) * 8
        halo(w + 1, 3, i * 4 + 3, lefts, (1 + i) * 4 * S)
        halo(w + 6, 5, i * 4, rights, (1 + i) * 4 * S)
        return carry

    lax.fori_loop(0, 4, edge_col, 0)
    halo(9, 0, 15, lefts, 0)
    halo(14, 2, 12, rights, 0)
    halo(49, 6, 3, lefts, 5 * 4 * S)
    halo(54, 8, 0, rights, 5 * 4 * S)

    def final_tile(t, read):
        i, j = t // 4, t % 4
        w = (2 + i) * 8 + 2 + j
        field = srcf[t] + apply(f1, w - 9, 4, t, lambda k: tiles[t * 4 + k])
        if last:
            field_out[t] = field
        a = field.astype(BF)
        b = (field - a.astype(F32)).astype(BF)
        y = dot(jnp.concatenate([a, b], axis=0), lo)
        return read + jnp.where(hi == t.astype(F32), y[:E] + y[E:], 0.0)

    read = lax.fori_loop(0, 16, final_tile, jnp.zeros((E, U), F32), unroll=2)
    present = (inc[...].astype(F32) + read).astype(BF)
    if last:
        present_out[...] = present
    else:
        for c in range(NC):
            present_out[c] = present


def sweep(last, own, mid, left, right, inc, tiles, prev, nxt, lefts, rights, meta, moves):
    vmem = pl.BlockSpec(memory_space=pltpu.VMEM)
    smem = pl.BlockSpec(memory_space=pltpu.SMEM)
    if last:
        out = (shape((E, U), BF), shape((16, E, S), F32))
    else:
        out = shape((NC, E, U), BF)

    def body(*refs):
        sweep_body(last, *refs)

    return call(
        body,
        out,
        flops=2 * E * S * S * 4 * 52,
        moved=6 * MB,
        in_specs=[vmem] * 11 + [smem],
        out_specs=(vmem, vmem) if last else vmem,
        scratch_shapes=[pltpu.VMEM((64, E, S), BF), pltpu.VMEM((16, E, S), F32), pltpu.VMEM((64, E, S), BF)],
    )(own, mid, left, right, inc, tiles, prev, nxt, lefts, rights, meta, moves)


def shift(value, axis):
    size = lax.axis_size(axis)
    up = [(i, i + 1) for i in range(size - 1)]
    return up, [(j, i) for i, j in up]


def per_device(traces, incident, points, coupling, volume_tiles, tile_columns):
    row_up, row_down = shift(None, "row")
    col_up, col_down = shift(None, "col")
    tiles = volume_tiles.reshape(64, S, S)
    rows, cols = pack(traces, points)
    rows = lax.all_to_all(rows, "row", 0, 0, tiled=True)
    cols = lax.all_to_all(cols, "col", 0, 0, tiled=True)

    own_meta = jnp.zeros((16, U), F32)
    own_meta = own_meta.at[0].set((coupling // S).astype(F32)).at[1].set((coupling % S).astype(F32))
    own_meta = own_meta.at[2, :64].set(tile_columns.reshape(64).astype(F32)).astype(BF)
    flat = tiles.reshape(16, 4 * S, S)
    prev = lax.ppermute(jnp.concatenate([flat[12:16].reshape(16 * S, S), own_meta]), "row", row_up)
    nxt = lax.ppermute(jnp.concatenate([flat[0:4].reshape(16 * S, S), own_meta]), "row", row_down)

    def column(j):
        pieces = [prev[j * 4 * S : (j + 1) * 4 * S]] + [flat[4 * i + j] for i in range(4)]
        pieces += [nxt[j * 4 * S : (j + 1) * 4 * S], prev[16 * S :], own_meta, nxt[16 * S :]]
        return jnp.concatenate(pieces)

    lefts = lax.ppermute(column(3), "col", col_up)
    rights = lax.ppermute(column(0), "col", col_down)
    metas = []
    for br in range(3):
        for bc in range(3):
            if bc == 1:
                metas.append((prev[16 * S :], own_meta, nxt[16 * S :])[br])
            else:
                metas.append((lefts if bc == 0 else rights)[24 * S + 16 * br : 24 * S + 16 * br + 16])
    meta = jnp.stack(metas)
    offset = meta[:, 2, :64].astype(jnp.int32)
    moves = offset + 5 * (offset // 3)

    kernel, partials = make_kernel(cols, rows)
    for outer in range(2):
        last = outer == 1
        got = lax.all_to_all(partials, "row", 0, 0, tiled=True)
        sums = jnp.sum(got.astype(F32), axis=0)
        mid = sums.astype(BF)
        left = lax.ppermute(mid, "col", col_up)
        right = lax.ppermute(mid, "col", col_down)
        out = sweep(last, sums[1], mid, left, right, incident, tiles, prev, nxt, lefts, rights, meta, moves)
        if not last:
            partials = product(lax.all_to_all(out, "col", 0, 0, tiled=True), kernel)
    present, field = out
    return present, field.transpose(1, 0, 2).reshape(E, 4, 4, S)


def solution(mesh):
    in_specs = (
        P(None, ("row", "col")),
        P(None, ("row", "col")),
        P(None, ("row", "col")),
        P(("row", "col")),
        P("row", "col", None, None, None),
        P("row", "col", None),
    )
    out_specs = (P(None, ("row", "col")), P(None, "row", "col", None))
    return jax.shard_map(per_device, mesh=mesh, in_specs=in_specs, out_specs=out_specs, check_vma=False)
```

profile of v0, /device:TPU:8, one launch (start us, length us, event | category | flops | bytes accessed | tf_op | source)
XLA Modules:
  0.0 151.3 jit_solution(10322334667382449081)
XLA Ops:
  2.1 1.4 fusion.14
  4.8 3.4 %collective-permute-start.2 = (bf16[2064,128]{1,0:T(8,128)(2,1)}, bf16[2064,128]{1,0:T(8,128)(2,1)S(1)}, u32[]{:S(2)}, u32[]{:S(2)}) collective-permute-start(bf16[2064,128]{1,0:T(8,128)(2,1)} %get-tuple-element.97), channel_id=1, source_target_pairs={{0,16},{16,32},{32,48},{48,64},{64,80},{80,96},{96,112},{1,17},{17... | collective-permute-start | bytes 1585160 | tf_op jit(solution)/shard_map/ppermute | solution.py:324
  9.7 7.3 %all-to-all-start.1 = ((bf16[8,48,128]{2,1,0:T(8,128)(2,1)}), bf16[8,48,128]{2,1,0:T(8,128)(2,1)S(1)}, u32[]{:S(2)}, u32[]{:S(2)}) async-start(bf16[8,48,128]{2,1,0:T(8,128)(2,1)} %get-tuple-element.45), calls=%async_computation.1 | async-start | bytes 196608 | tf_op jit(solution)/shard_map/all_to_all | solution.py:317
  18.3 2.0 %collective-permute-done.2.refs_6_ = bf16[2064,128]{1,0:T(8,128)(2,1)S(1)} collective-permute-done((bf16[2064,128]{1,0:T(8,128)(2,1)}, bf16[2064,128]{1,0:T(8,128)(2,1)S(1)}, u32[]{:S(2)}, u32[]{:S(2)}) %collective-permute-start.2) | collective-permute-done | bytes 528416 | tf_op jit(solution)/shard_map/ppermute | solution.py:324
  23.9 8.6 %collective-permute-done.3.refs_7_ = bf16[2064,128]{1,0:T(8,128)(2,1)S(1)} collective-permute-done((bf16[2064,128]{1,0:T(8,128)(2,1)}, bf16[2064,128]{1,0:T(8,128)(2,1)S(1)}, u32[]{:S(2)}, u32[]{:S(2)}) %collective-permute-start.3) | collective-permute-done | bytes 528416 | tf_op jit(solution)/shard_map/ppermute | solution.py:325
  35.2 5.4 %all-to-all-start = ((bf16[16,80,128]{2,1,0:T(8,128)(2,1)}), bf16[16,80,128]{2,1,0:T(8,128)(2,1)S(1)}, u32[]{:S(2)}, u32[]{:S(2)}) async-start(bf16[16,80,128]{2,1,0:T(8,128)(2,1)} %copy-done.6), calls=%async_computation | async-start | bytes 655360 | tf_op jit(solution)/shard_map/all_to_all | solution.py:318
  41.1 3.1 %collective-permute-start.5 = (bf16[3120,128]{1,0:T(8,128)(2,1)}, bf16[3120,128]{1,0:T(8,128)(2,1)}, u32[]{:S(2)}, u32[]{:S(2)}) collective-permute-start(bf16[3120,128]{1,0:T(8,128)(2,1)} %get-tuple-element.85), channel_id=1, source_target_pairs={{1,0},{2,1},{3,2},{4,3},{5,4},{6,5},{7,6},{8,7},{9,8},{10,9},{11,1... | collective-permute-start | bytes 2396168 | tf_op jit(solution)/shard_map/ppermute | solution.py:333
  44.2 2.5 %all-to-all-done.col_ref = bf16[16,80,128]{2,1,0:T(8,128)(2,1)S(1)} async-done(((bf16[16,80,128]{2,1,0:T(8,128)(2,1)}), bf16[16,80,128]{2,1,0:T(8,128)(2,1)S(1)}, u32[]{:S(2)}, u32[]{:S(2)}) %all-to-all-start) | async-done | bytes 327712 | tf_op jit(solution)/shard_map/all_to_all | solution.py:318
  47.6 9.8 %shard_map.78 = (bf16[2048,1024]{1,0:T(8,128)(2,1)S(1)}, bf16[8,3,64,128]{3,2,1,0:T(8,128)(2,1)S(1)}) custom-call(bf16[16,80,128]{2,1,0:T(8,128)(2,1)S(1)} %all-to-all-done.col_ref, bf16[8,48,128]{2,1,0:T(8,128)(2,1)S(1)} %copy-done.5), custom_call_target="tpu_custom_call" | custom-call | flops 83886080 | bytes 6291456 | tf_op jit(solution)/shard_map/pallas_call | solution.py:130
  57.4 2.0 %copy-done.1 = bf16[2048,1024]{1,0:T(8,128)(2,1)} copy-done((bf16[2048,1024]{1,0:T(8,128)(2,1)}, bf16[2048,1024]{1,0:T(8,128)(2,1)S(1)}, u32[]{:S(2)}) %copy-start.1) | copy-done | bytes 4194328
  60.1 7.6 %all-to-all-start.2 = ((bf16[8,3,64,128]{3,2,1,0:T(8,128)(2,1)}), bf16[8,3,64,128]{3,2,1,0:T(8,128)(2,1)}, u32[]{:S(2)}, u32[]{:S(2)}) async-start(bf16[8,3,64,128]{3,2,1,0:T(8,128)(2,1)} %copy-done.3), calls=%async_computation.2 | async-start | bytes 786432 | tf_op jit(solution)/shard_map/all_to_all | solution.py:348
  67.8 2.2 %collective-permute-start.4 = (bf16[3120,128]{1,0:T(8,128)(2,1)}, bf16[3120,128]{1,0:T(8,128)(2,1)}, u32[]{:S(2)}, u32[]{:S(2)}) collective-permute-start(bf16[3120,128]{1,0:T(8,128)(2,1)} %get-tuple-element.86), channel_id=1, source_target_pairs={{0,1},{1,2},{2,3},{3,4},{4,5},{5,6},{6,7},{7,8},{8,9},{9,10},{10,1... | collective-permute-start | bytes 2396168 | tf_op jit(solution)/shard_map/ppermute | solution.py:332
  70.0 8.8 %all-to-all-done.2 = bf16[8,3,64,128]{3,2,1,0:T(8,128)(2,1)} async-done(((bf16[8,3,64,128]{3,2,1,0:T(8,128)(2,1)}), bf16[8,3,64,128]{3,2,1,0:T(8,128)(2,1)}, u32[]{:S(2)}, u32[]{:S(2)}) %all-to-all-start.2) | async-done | bytes 393248 | tf_op jit(solution)/shard_map/all_to_all | solution.py:348
  79.9 3.7 %collective-permute-start.1 = (bf16[3,64,128]{2,1,0:T(8,128)(2,1)S(1)}, bf16[3,64,128]{2,1,0:T(8,128)(2,1)S(1)}, u32[]{:S(2)}, u32[]{:S(2)}) collective-permute-start(bf16[3,64,128]{2,1,0:T(8,128)(2,1)S(1)} %convert_element_type.39.refs_1_), channel_id=1, source_target_pairs={{1,0},{2,1},{3,2},{4,3},{5,4},{6,5},{7,6},{8,7},{9,8},{10,9},{11,1... | collective-permute-start | bytes 147464 | tf_op jit(solution)/shard_map/ppermute | solution.py:352
  83.6 1.9 %collective-permute-start = (bf16[3,64,128]{2,1,0:T(8,128)(2,1)S(1)}, bf16[3,64,128]{2,1,0:T(8,128)(2,1)S(1)}, u32[]{:S(2)}, u32[]{:S(2)}) collective-permute-start(bf16[3,64,128]{2,1,0:T(8,128)(2,1)S(1)} %convert_element_type.39.refs_1_), channel_id=1, source_target_pairs={{0,1},{1,2},{2,3},{3,4},{4,5},{5,6},{6,7},{7,8},{8,9},{9,10},{10,1... | collective-permute-start | bytes 147464 | tf_op jit(solution)/shard_map/ppermute | solution.py:351
  87.3 2.7 %collective-permute-done.refs_2_ = bf16[3,64,128]{2,1,0:T(8,128)(2,1)S(1)} collective-permute-done((bf16[3,64,128]{2,1,0:T(8,128)(2,1)S(1)}, bf16[3,64,128]{2,1,0:T(8,128)(2,1)S(1)}, u32[]{:S(2)}, u32[]{:S(2)}) %collective-permute-start) | collective-permute-done | bytes 49184 | tf_op jit(solution)/shard_map/ppermute | solution.py:351
  90.0 9.4 %shard_map.79 = bf16[16,64,128]{2,1,0:T(8,128)(2,1)S(1)} custom-call(f32[64,128]{1,0:T(8,128)S(1)} %slice_bitcast_fusion.9.refs_0_, bf16[3,64,128]{2,1,0:T(8,128)(2,1)S(1)} %convert_element_type.39.refs_1_, bf16[3,64,128]{2,1,0:T(8,128)(2,1)S(1)} %collective-permute-done.refs_2_, bf16[3,64,128]{2,1,0:T(8,128)(2,1)S(1)} %collective-permute-done.1.refs_3_, ...), custom_call_target="tpu_custom_call" | custom-call | flops 436207616 | bytes 6291456 | tf_op jit(solution)/shard_map/pallas_call | solution.py:295
  99.4 9.1 %all_to_all.25.p_ref = bf16[16,64,128]{2,1,0:T(8,128)(2,1)S(1)} all-to-all(bf16[16,64,128]{2,1,0:T(8,128)(2,1)S(1)} %shard_map.79), channel_id=1, replica_groups=mesh['row'=8,'col'=16] {'col'}, dimensions={0} | all-to-all | bytes 524288 | tf_op jit(solution)/shard_map/all_to_all | solution.py:355
  108.5 1.3 shard_map.80
  109.8 21.3 %all_to_all.26 = bf16[8,3,64,128]{3,2,1,0:T(8,128)(2,1)S(1)} all-to-all(bf16[8,3,64,128]{3,2,1,0:T(8,128)(2,1)S(1)} %shard_map.80), channel_id=1, replica_groups=mesh['row'=8,'col'=16] {'row'}, dimensions={0} | all-to-all | bytes 786432 | tf_op jit(solution)/shard_map/all_to_all | solution.py:348
  131.2 2.9 %collective-permute-start.7 = (bf16[3,64,128]{2,1,0:T(8,128)(2,1)S(1)}, bf16[3,64,128]{2,1,0:T(8,128)(2,1)S(1)}, u32[]{:S(2)}, u32[]{:S(2)}) collective-permute-start(bf16[3,64,128]{2,1,0:T(8,128)(2,1)S(1)} %convert_element_type.48.refs_1_), channel_id=1, source_target_pairs={{1,0},{2,1},{3,2},{4,3},{5,4},{6,5},{7,6},{8,7},{9,8},{10,9},{11,1... | collective-permute-start | bytes 147464 | tf_op jit(solution)/shard_map/ppermute | solution.py:352
  134.0 1.9 %collective-permute-start.6 = (bf16[3,64,128]{2,1,0:T(8,128)(2,1)S(1)}, bf16[3,64,128]{2,1,0:T(8,128)(2,1)S(1)}, u32[]{:S(2)}, u32[]{:S(2)}) collective-permute-start(bf16[3,64,128]{2,1,0:T(8,128)(2,1)S(1)} %convert_element_type.48.refs_1_), channel_id=1, source_target_pairs={{0,1},{1,2},{2,3},{3,4},{4,5},{5,6},{6,7},{7,8},{8,9},{9,10},{10,1... | collective-permute-start | bytes 147464 | tf_op jit(solution)/shard_map/ppermute | solution.py:351
  136.0 4.4 %collective-permute-done.6.refs_2_ = bf16[3,64,128]{2,1,0:T(8,128)(2,1)S(1)} collective-permute-done((bf16[3,64,128]{2,1,0:T(8,128)(2,1)S(1)}, bf16[3,64,128]{2,1,0:T(8,128)(2,1)S(1)}, u32[]{:S(2)}, u32[]{:S(2)}) %collective-permute-start.6) | collective-permute-done | bytes 49184 | tf_op jit(solution)/shard_map/ppermute | solution.py:351
  140.3 9.9 %shard_map.81 = (bf16[64,128]{1,0:T(8,128)(2,1)}, f32[16,64,128]{2,1,0:T(8,128)S(1)}) custom-call(f32[64,128]{1,0:T(8,128)S(1)} %slice_bitcast_fusion.8.refs_0_, bf16[3,64,128]{2,1,0:T(8,128)(2,1)S(1)} %convert_element_type.48.refs_1_, bf16[3,64,128]{2,1,0:T(8,128)(2,1)S(1)} %collective-permute-done.6.refs_2_, ...), custom_call_target="tpu_custom_call" | custom-call | flops 436207616 | bytes 6291456 | tf_op jit(solution)/shard_map/pallas_call | solution.py:295
  (63 shorter events, 17.8 us)
Async XLA Ops:
  2.1 6.2 %copy-start.8 = (bf16[64,128]{1,0:T(8,128)(2,1)S(1)}, bf16[64,128]{1,0:T(8,128)(2,1)}, u32[]{:S(2)}) copy-start(bf16[64,128]{1,0:T(8,128)(2,1)} %traces.1) | copy-start | bytes 49156
  2.1 6.2 %copy-start.9 = (f32[3,128]{1,0:T(4,128)S(1)}, f32[3,128]{1,0:T(4,128)}, u32[]{:S(2)}) copy-start(f32[3,128]{1,0:T(4,128)} %points.1) | copy-start | bytes 4612
  2.1 18.9 %copy-start = (bf16[4,4,4,128,128]{4,3,2,1,0:T(8,128)(2,1)S(1)}, bf16[4,4,4,128,128]{4,3,2,1,0:T(8,128)(2,1)}, u32[]{:S(2)}) copy-start(bf16[4,4,4,128,128]{4,3,2,1,0:T(8,128)(2,1)} %param.16) | copy-start | bytes 6291460
  4.8 15.5 %collective-permute-start.2 = (bf16[2064,128]{1,0:T(8,128)(2,1)}, bf16[2064,128]{1,0:T(8,128)(2,1)S(1)}, u32[]{:S(2)}, u32[]{:S(2)}) collective-permute-start(bf16[2064,128]{1,0:T(8,128)(2,1)} %get-tuple-element.97), channel_id=1, source_target_pairs={{0,16},{16,32},{32,48},{48,64},{64,80},{80,96},{96,112},{1,17},{17... | collective-permute-start | bytes 1585160 | tf_op jit(solution)/shard_map/ppermute | solution.py:324
  9.0 0.7 copy-start.6
  9.7 24.8 %all-to-all-start.1 = ((bf16[8,48,128]{2,1,0:T(8,128)(2,1)}), bf16[8,48,128]{2,1,0:T(8,128)(2,1)S(1)}, u32[]{:S(2)}, u32[]{:S(2)}) async-start(bf16[8,48,128]{2,1,0:T(8,128)(2,1)} %get-tuple-element.45), calls=%async_computation.1 | async-start | bytes 196608 | tf_op jit(solution)/shard_map/all_to_all | solution.py:317
  17.0 15.6 %collective-permute-start.3 = (bf16[2064,128]{1,0:T(8,128)(2,1)}, bf16[2064,128]{1,0:T(8,128)(2,1)S(1)}, u32[]{:S(2)}, u32[]{:S(2)}) collective-permute-start(bf16[2064,128]{1,0:T(8,128)(2,1)} %get-tuple-element.96), channel_id=1, source_target_pairs={{16,0},{32,16},{48,32},{64,48},{80,64},{96,80},{112,96},{17,1},{33... | collective-permute-start | bytes 1585160 | tf_op jit(solution)/shard_map/ppermute | solution.py:325
  23.2 66.7 %copy-start.7 = (bf16[64,128]{1,0:T(8,128)(2,1)S(1)}, bf16[64,128]{1,0:T(8,128)(2,1)}, u32[]{:S(2)}) copy-start(bf16[64,128]{1,0:T(8,128)(2,1)} %refs_4_.3) | copy-start | bytes 49156
  34.5 0.6 copy-start.4
  35.2 11.5 %all-to-all-start = ((bf16[16,80,128]{2,1,0:T(8,128)(2,1)}), bf16[16,80,128]{2,1,0:T(8,128)(2,1)S(1)}, u32[]{:S(2)}, u32[]{:S(2)}) async-start(bf16[16,80,128]{2,1,0:T(8,128)(2,1)} %copy-done.6), calls=%async_computation | async-start | bytes 655360 | tf_op jit(solution)/shard_map/all_to_all | solution.py:318
  41.1 44.5 %collective-permute-start.5 = (bf16[3120,128]{1,0:T(8,128)(2,1)}, bf16[3120,128]{1,0:T(8,128)(2,1)}, u32[]{:S(2)}, u32[]{:S(2)}) collective-permute-start(bf16[3120,128]{1,0:T(8,128)(2,1)} %get-tuple-element.85), channel_id=1, source_target_pairs={{1,0},{2,1},{3,2},{4,3},{5,4},{6,5},{7,6},{8,7},{9,8},{10,9},{11,1... | collective-permute-start | bytes 2396168 | tf_op jit(solution)/shard_map/ppermute | solution.py:333
  46.7 0.9 copy-start.5
  57.4 2.0 %copy-start.1 = (bf16[2048,1024]{1,0:T(8,128)(2,1)}, bf16[2048,1024]{1,0:T(8,128)(2,1)S(1)}, u32[]{:S(2)}) copy-start(bf16[2048,1024]{1,0:T(8,128)(2,1)S(1)} %get-tuple-element.47.k_ref) | copy-start | bytes 12582916
  59.4 0.7 copy-start.3
  60.1 18.7 %all-to-all-start.2 = ((bf16[8,3,64,128]{3,2,1,0:T(8,128)(2,1)}), bf16[8,3,64,128]{3,2,1,0:T(8,128)(2,1)}, u32[]{:S(2)}, u32[]{:S(2)}) async-start(bf16[8,3,64,128]{3,2,1,0:T(8,128)(2,1)} %copy-done.3), calls=%async_computation.2 | async-start | bytes 786432 | tf_op jit(solution)/shard_map/all_to_all | solution.py:348
  67.8 18.6 %collective-permute-start.4 = (bf16[3120,128]{1,0:T(8,128)(2,1)}, bf16[3120,128]{1,0:T(8,128)(2,1)}, u32[]{:S(2)}, u32[]{:S(2)}) collective-permute-start(bf16[3120,128]{1,0:T(8,128)(2,1)} %get-tuple-element.86), channel_id=1, source_target_pairs={{0,1},{1,2},{2,3},{3,4},{4,5},{5,6},{6,7},{7,8},{8,9},{9,10},{10,1... | collective-permute-start | bytes 2396168 | tf_op jit(solution)/shard_map/ppermute | solution.py:332
  79.9 7.4 %collective-permute-start.1 = (bf16[3,64,128]{2,1,0:T(8,128)(2,1)S(1)}, bf16[3,64,128]{2,1,0:T(8,128)(2,1)S(1)}, u32[]{:S(2)}, u32[]{:S(2)}) collective-permute-start(bf16[3,64,128]{2,1,0:T(8,128)(2,1)S(1)} %convert_element_type.39.refs_1_), channel_id=1, source_target_pairs={{1,0},{2,1},{3,2},{4,3},{5,4},{6,5},{7,6},{8,7},{9,8},{10,9},{11,1... | collective-permute-start | bytes 147464 | tf_op jit(solution)/shard_map/ppermute | solution.py:352
  83.6 6.3 %collective-permute-start = (bf16[3,64,128]{2,1,0:T(8,128)(2,1)S(1)}, bf16[3,64,128]{2,1,0:T(8,128)(2,1)S(1)}, u32[]{:S(2)}, u32[]{:S(2)}) collective-permute-start(bf16[3,64,128]{2,1,0:T(8,128)(2,1)S(1)} %convert_element_type.39.refs_1_), channel_id=1, source_target_pairs={{0,1},{1,2},{2,3},{3,4},{4,5},{5,6},{6,7},{7,8},{8,9},{9,10},{10,1... | collective-permute-start | bytes 147464 | tf_op jit(solution)/shard_map/ppermute | solution.py:351
  90.0 18.6 %copy-start.2 = (bf16[2048,1024]{1,0:T(8,128)(2,1)S(1)}, bf16[2048,1024]{1,0:T(8,128)(2,1)}, u32[]{:S(2)}) copy-start(bf16[2048,1024]{1,0:T(8,128)(2,1)} %copy-done.1) | copy-start | bytes 12582916
  131.2 4.8 %collective-permute-start.7 = (bf16[3,64,128]{2,1,0:T(8,128)(2,1)S(1)}, bf16[3,64,128]{2,1,0:T(8,128)(2,1)S(1)}, u32[]{:S(2)}, u32[]{:S(2)}) collective-permute-start(bf16[3,64,128]{2,1,0:T(8,128)(2,1)S(1)} %convert_element_type.48.refs_1_), channel_id=1, source_target_pairs={{1,0},{2,1},{3,2},{4,3},{5,4},{6,5},{7,6},{8,7},{9,8},{10,9},{11,1... | collective-permute-start | bytes 147464 | tf_op jit(solution)/shard_map/ppermute | solution.py:352
  134.0 6.3 %collective-permute-start.6 = (bf16[3,64,128]{2,1,0:T(8,128)(2,1)S(1)}, bf16[3,64,128]{2,1,0:T(8,128)(2,1)S(1)}, u32[]{:S(2)}, u32[]{:S(2)}) collective-permute-start(bf16[3,64,128]{2,1,0:T(8,128)(2,1)S(1)} %convert_element_type.48.refs_1_), channel_id=1, source_target_pairs={{0,1},{1,2},{2,3},{3,4},{4,5},{5,6},{6,7},{7,8},{8,9},{9,10},{10,1... | collective-permute-start | bytes 147464 | tf_op jit(solution)/shard_map/ppermute | solution.py:351
where the time goes:
time: 152 us; the launch traced here: 151 us
  starting transfers between devices  40.7 us (27%)
  Pallas kernels  31.1 us (20%)
  blocking collectives  30.4 us (20%)
  waiting for transfers between devices  29 us (19%)
  local copies, waits for them, and re-layouts  15.6 us (10%)
  other arithmetic  3.57 us (2%)
    all_to_all x1, blocking collectives, per_device(): got = lax.all_to_all(partials, 'row', 0, 0, tiled=True)  21.3 us
    pallas_call x2, Pallas kernels, sweep(): call(body, out, flops=2 * E * S * S * 4 * 52, moved=6 * MB, in_specs=[vme...  19.3 us
    unnamed x28, local copies, waits for them, and re-layouts  11.1 us
    pallas_call x1, Pallas kernels, make_kernel(): call(kernel_body, (shape((NC * U, NR * U), BF), shape((NR, 3, E, U), BF))...  9.84 us
    all_to_all x1, blocking collectives, per_device(): partials = product(lax.all_to_all(out, 'col', 0, 0, tiled=True), kernel)  9.11 us
    all_to_all x1, waiting for transfers between devices, per_device(): got = lax.all_to_all(partials, 'row', 0, 0, tiled=True)  8.78 us
    ppermute x1, waiting for transfers between devices, per_device(): lax.ppermute(jnp.concatenate([flat[0:4].reshape(16 * S, S), own_meta]), '...  8.65 us
    all_to_all x1, starting transfers between devices, per_device(): got = lax.all_to_all(partials, 'row', 0, 0, tiled=True)  7.63 us
  transfers between devices with their start and end apart: 11, of which 6 were waited for; matrix products, arithmetic and copies ran while one was open for 6% of the time, Pallas kernels for 7%

commit v1 on v0

v1 whole, which is shorter than its diff:
```python
import math

import jax
import jax.numpy as jnp
from jax import lax
from jax.experimental import pallas as pl
from jax.experimental.pallas import tpu as pltpu
from jax.sharding import PartitionSpec as P


E, U, S = 64, 128, 128
NR, NC = 8, 16
TOTAL = U * NR * NC
MB = 1 << 20
ROWS = 4 * S
BF, F32 = jnp.bfloat16, jnp.float32
SIN = (3.14158202, -5.1671428, 2.54189903, -0.55463619)
NT = (((1,), (1,)), ((), ()))
TN = (((0,), (0,)), ((), ()))

SPACING = float(TOTAL) ** (-1.0 / 3.0)
TURNS = 2.0 / SPACING / (2.0 * math.pi)
SMOOTH = (0.5 * SPACING) ** 2 * TURNS * TURNS
FACTOR = TURNS / math.sqrt(2.0 * TOTAL)
WAVE = tuple(c * math.sqrt(2.0 * FACTOR) for c in SIN)


def dot(a, b, dims=(((1,), (0,)), ((), ()))):
    return lax.dot_general(a, b, dims, preferred_element_type=F32)


def call(body, out_shape, *, limit=24 * MB, flops=0, moved=0, **kwargs):
    return pl.pallas_call(
        body,
        out_shape=out_shape,
        compiler_params=pltpu.CompilerParams(vmem_limit_bytes=limit),
        cost_estimate=pl.CostEstimate(flops=flops, bytes_accessed=moved, transcendentals=0),
        **kwargs,
    )


def shape(dims, dtype):
    return jax.ShapeDtypeStruct(dims, dtype)


def hbm(dims, dtype):
    return pltpu.MemorySpace.HBM(dims, dtype)


def vmem(dims, dtype):
    return pltpu.MemorySpace.VMEM(dims, dtype)


def keep(*values):
    return tuple(pltpu.with_memory_space_constraint(v, pltpu.MemorySpace.HBM) for v in values)


IN_VMEM = pl.BlockSpec(memory_space=pltpu.VMEM)
IN_SMEM = pl.BlockSpec(memory_space=pltpu.SMEM)
IN_HBM = pl.BlockSpec(memory_space=pltpu.HBM)
IN_ANY = pl.BlockSpec(memory_space=pl.ANY)


def split3(x):
    a = x.astype(BF).astype(F32)
    b = (x - a).astype(BF).astype(F32)
    return a, b, (x - a - b).astype(BF).astype(F32)


def rows_at(line, pieces):
    out = jnp.zeros((16, U), F32)
    for at, value in pieces:
        out = jnp.where(line == at, value, out)
    return out


def pack_body(traces_h, points_h, coupling_h, columns_h, tiles, row_out, col_out, up, down, meta_out, *scratch):
    traces, points, coupling, columns, sems = scratch
    loads = [(points_h, points), (columns_h, columns), (coupling_h, coupling), (traces_h, traces)]
    loads += [(tiles.at[pl.ds(12 * ROWS, 4 * ROWS)], up.at[pl.ds(0, 4 * ROWS)])]
    loads += [(tiles.at[pl.ds(0, 4 * ROWS)], down.at[pl.ds(0, 4 * ROWS)])]
    loads = [pltpu.make_async_copy(a, b, sems.at[n]) for n, (a, b) in enumerate(loads)]
    for copy in loads:
        copy.start()
    lane = lax.broadcasted_iota(jnp.int32, (1, U), 1)
    loads[0].wait()
    p = (points[...] - 0.5) * TURNS
    parts = split3(p)
    norm = jnp.sum(p * p, axis=0, keepdims=True)
    line = lax.broadcasted_iota(jnp.int32, (16, U), 0)
    source = [(3 * i + d, parts[i][d : d + 1]) for i in range(3) for d in range(3)]
    source += [(9 + i, v) for i, v in enumerate(split3(norm))] + [(12, 1.0)]
    source = rows_at(line, source).astype(BF)
    shifted = split3(norm + SMOOTH)
    target = []
    for j in range(3):
        pieces = [(3 * i + d, -2.0 * parts[j][d : d + 1]) for i in range(3) for d in range(3)]
        if j == 0:
            pieces += [(9 + i, 1.0) for i in range(3)]
        target.append(rows_at(line, pieces + [(12, shifted[j])]).astype(BF))
    for r in range(NR):
        for j in range(3):
            row_out[r, 16 * j : 16 * j + 16] = target[j]
    loads[1].wait()
    offsets = jnp.zeros((1, U), jnp.int32)
    for n in range(64):
        offsets = jnp.where(lane == n, columns[n // 16, n // 4 % 4, n % 4], offsets)
    loads[2].wait()
    at = coupling[...]
    meta = [(0, (at >> 7).astype(F32)), (1, (at & 127).astype(F32)), (2, offsets.astype(F32))]
    meta = rows_at(line, meta).astype(BF)
    meta_out[...] = meta
    up[4 * ROWS :] = meta
    down[4 * ROWS :] = meta
    loads[3].wait()
    for c in range(NC):
        col_out[c, :E] = traces[...]
        col_out[c, E:] = source
    for copy in loads[4:]:
        copy.wait()


def pack(traces, points, coupling, columns, tiles):
    side = hbm((4 * ROWS + 16, S), BF)
    return call(
        pack_body,
        (hbm((NR, 48, U), BF), hbm((NC, E + 16, U), BF), side, side, vmem((16, U), BF)),
        in_specs=[IN_HBM] * 5,
        out_specs=(IN_VMEM,) * 5,
        scratch_shapes=[
            pltpu.VMEM((E, U), BF),
            pltpu.VMEM((3, U), F32),
            pltpu.VMEM((1, U), jnp.int32),
            pltpu.SMEM((4, 4, 4), jnp.int32),
            pltpu.SemaphoreType.DMA((6,)),
        ],
    )(*keep(traces, points, coupling, columns, tiles))


def edge_body(prev, nxt, meta, tiles, left_out, right_out, mid_out, sems):
    copies = []
    for out, j in ((left_out, 3), (right_out, 0)):
        pieces = [prev.at[pl.ds(j * ROWS, ROWS)]]
        pieces += [tiles.at[pl.ds((4 * i + j) * ROWS, ROWS)] for i in range(4)]
        pieces += [nxt.at[pl.ds(j * ROWS, ROWS)]]
        for n, piece in enumerate(pieces):
            copies.append(pltpu.make_async_copy(piece, out.at[pl.ds(n * ROWS, ROWS)], sems.at[len(copies)]))
    for copy in copies:
        copy.start()
    for j in range(3):
        value = (prev, None, nxt)[j]
        value = meta[...] if j == 1 else value[4 * ROWS :]
        for out, start in ((left_out, 6 * ROWS), (right_out, 6 * ROWS), (mid_out, 0)):
            out[start + 16 * j : start + 16 * j + 16] = value
    for copy in copies:
        copy.wait()


def edges(prev, nxt, meta, tiles):
    side = vmem((6 * ROWS + 48, S), BF)
    return call(
        edge_body,
        (side, side, vmem((48, U), BF)),
        moved=4 * MB,
        in_specs=[IN_VMEM, IN_VMEM, IN_VMEM, IN_ANY],
        out_specs=(IN_VMEM,) * 3,
        scratch_shapes=[pltpu.SemaphoreType.DMA((12,))],
    )(prev, nxt, meta, tiles)


def table_body(mid, lefts, rights, meta_out, moves_out, sides, sems):
    copies = [
        pltpu.make_async_copy(h.at[pl.ds(6 * ROWS, 48)], sides.at[n], sems.at[n]) for n, h in enumerate((lefts, rights))
    ]
    for copy in copies:
        copy.start()
    for copy in copies:
        copy.wait()
    moves_out[...] = jnp.zeros_like(moves_out)
    for br in range(3):
        for bc in range(3):
            b = 3 * br + bc
            m = (sides[0], mid[...], sides[1])[bc][16 * br : 16 * br + 16]
            meta_out[16 * b : 16 * b + 16] = m
            o = m.astype(F32)[2:3]
            o = o + 5.0 * (jnp.where(o >= 3.0, 1.0, 0.0) + jnp.where(o >= 6.0, 1.0, 0.0))
            moves_out[b : b + 1] = o.astype(jnp.int32)


def tables(mid, lefts, rights):
    return call(
        table_body,
        (vmem((144, U), BF), vmem((16, U), jnp.int32)),
        in_specs=[IN_VMEM, IN_ANY, IN_ANY],
        out_specs=(IN_VMEM,) * 2,
        scratch_shapes=[pltpu.VMEM((2, 48, U), BF), pltpu.SemaphoreType.DMA((2,))],
    )(mid, lefts, rights)


def write_partials(acc, out):
    for d in range(NR):
        for j in range(3):
            b = d - 1 + j
            if 0 <= b < NR:
                out[d, j] = acc[:, b * U : b * U + U].astype(BF)
            else:
                out[d, j] = jnp.zeros((E, U), BF)


def kernel_body(col_ref, row_ref, k_hbm, out_ref, acc, feats, dist_a, dist_b, k_ref, sem):
    gets = [pltpu.make_async_copy(row_ref.at[r], feats.at[:, pl.ds(r * U, U)], sem) for r in range(NR)]
    for copy in gets:
        copy.start()
    acc[...] = jnp.zeros_like(acc)

    def distances(n, out):
        own = col_ref[n, E:]
        out[...] = dot(jnp.concatenate([own, own, own], axis=0), feats[...], TN)

    def waves(n, dist):
        for i in range(0, U, 16):
            for j in range(0, NR * U, 512):
                d2 = dist[i : i + 16, j : j + 512]
                inv = lax.rsqrt(d2)
                turns = d2 * inv
                f = turns - jnp.round(turns)
                u = f * f
                s = f * (WAVE[0] + u * (WAVE[1] + u * (WAVE[2] + u * WAVE[3])))
                k_ref[n, i : i + 16, j : j + 512] = ((FACTOR - s * s) * inv).astype(BF)

    def accumulate(m):
        p = jnp.concatenate([col_ref[2 * m, :E], col_ref[2 * m + 1, :E]], axis=1)
        k = jnp.concatenate([k_ref[2 * m], k_ref[2 * m + 1]], axis=0)
        acc[...] += dot(p, k)

    def saved(n):
        return pltpu.make_async_copy(k_ref.at[pl.ds(2 * n, 2)], k_hbm.at[pl.ds(2 * n, 2)], sem)

    def pair(m):
        distances(2 * m + 1, dist_b)
        waves(2 * m, dist_a)
        distances(jnp.minimum(2 * m + 2, NC - 1), dist_a)
        waves(2 * m + 1, dist_b)
        saved(m).start()

    for copy in gets:
        copy.wait()
    distances(0, dist_a)
    pair(0)

    def step(m, carry):
        accumulate(m - 1)
        pair(m)
        return carry

    lax.fori_loop(1, NC // 2, step, 0)
    accumulate(NC // 2 - 1)
    write_partials(acc, out_ref)
    pltpu.make_async_copy(k_ref, k_hbm, sem).wait()


def make_kernel(cols, rows):
    return call(
        kernel_body,
        (hbm((NC, U, NR * U), BF), hbm((NR, 3, E, U), BF)),
        flops=40 * 2 * MB,
        moved=6 * MB,
        in_specs=[IN_VMEM, IN_HBM],
        out_specs=(IN_HBM, IN_VMEM),
        scratch_shapes=[
            pltpu.VMEM((E, NR * U), F32),
            pltpu.VMEM((48, NR * U), BF),
            pltpu.VMEM((U, NR * U), F32),
            pltpu.VMEM((U, NR * U), F32),
            pltpu.VMEM((NC, U, NR * U), BF),
            pltpu.SemaphoreType.DMA,
        ],
    )(cols, *keep(rows))


def product_body(p_ref, k_ref, out_ref, acc):
    acc[...] = jnp.zeros_like(acc)
    for n in range(0, NC, 4):
        p = jnp.concatenate([p_ref[n + i] for i in range(4)], axis=1)
        k = jnp.concatenate([k_ref[n + i] for i in range(4)], axis=0)
        acc[...] += dot(p, k)
    write_partials(acc, out_ref)


def product(present, kernel):
    return call(
        product_body,
        shape((NR, 3, E, U), BF),
        flops=2 * E * 2 * MB,
        moved=5 * MB,
        in_specs=[IN_VMEM, IN_VMEM],
        out_specs=IN_VMEM,
        scratch_shapes=[pltpu.VMEM((E, NR * U), F32)],
    )(present, kernel)


def span(b):
    return ((0, 2), (1, 3)) if b == 0 else ((6, 0), (7, 1)) if b == 2 else tuple((2 + i, i) for i in range(4))


def sweep_body(last, own_ref, mid, left, right, inc, metas, moves_v, tiles_h, prev_h, nxt_h, lefts_h, rights_h, *rest):
    if last:
        present_out, field_out = rest[:2]
    else:
        present_out, field_out = rest[0], None
    src, srcf, f1, fields, tiles, prev, nxt, lefts, rights, moves, sems = rest[2 if last else 1 :]
    loads = [(moves_v, moves), (tiles_h, tiles)]
    loads += [(h.at[pl.ds(0, 4 * ROWS)], v) for h, v in ((prev_h, prev), (nxt_h, nxt))]
    loads += [(h.at[pl.ds(0, 6 * ROWS)], v) for h, v in ((lefts_h, lefts), (rights_h, rights))]
    loads = [pltpu.make_async_copy(a, b, sems.at[n]) for n, (a, b) in enumerate(loads)]
    for copy in loads:
        copy.start()
    line = lax.broadcasted_iota(jnp.int32, (S, U), 0).astype(F32)

    def coupling(br, bc):
        at = 16 * (3 * br + bc)
        m = metas[at : at + 16].astype(F32)
        return m[0:1], jnp.where(m[1:2] == line, 1.0, 0.0).astype(BF)

    def masked(c, hi, ids):
        return jnp.concatenate([c * jnp.where(hi == float(t), 1.0, 0.0).astype(BF) for t in ids], axis=0)

    def place(br, bc):
        hi, lo = coupling(br, bc)
        c = (left, mid, right)[bc][br]
        places = [(R * 8 + C, i * 4 + j) for R, i in span(br) for C, j in span(bc)]
        out = dot(masked(c, hi, [t for _, t in places]), lo, NT).astype(BF)
        for n, (w, _) in enumerate(places):
            src[w] = out[n * E : n * E + E]

    hi, lo = coupling(1, 1)
    own = own_ref[...]
    top = own.astype(BF)
    low = (own - top.astype(F32)).astype(BF)
    both = jnp.concatenate([masked(top, hi, range(16)), masked(low, hi, range(16))], axis=1)
    twice = jnp.concatenate([lo, lo], axis=1)
    out = dot(both, twice, NT)
    for t in range(16):
        srcf[t] = out[t * E : t * E + E]
        src[(2 + t // 4) * 8 + 2 + t % 4] = out[t * E : t * E + E].astype(BF)
    for br in range(3):
        for bc in range(3):
            if br != 1 or bc != 1:
                place(br, bc)
    for copy in loads[:2]:
        copy.wait()

    def apply(values, base, block, tile, ref, start):
        total = None
        for h in range(2):
            ks = (2 * h, 2 * h + 1)
            x = jnp.concatenate([values[base + moves[block, tile * 4 + k]] for k in ks], axis=1)
            a = [ref[pl.ds(pl.multiple_of(start + k * S, S), S), :] for k in ks]
            y = dot(x, jnp.concatenate(a, axis=1), NT)
            total = y if total is None else total + y
        return total

    def own_tile(t, carry):
        i, j = t // 4, t % 4
        w = (2 + i) * 8 + 2 + j
        f1[w] = (srcf[t] + apply(src, w - 9, 4, t, tiles, t * ROWS)).astype(BF)
        return carry

    lax.fori_loop(0, 16, own_tile, 0, unroll=4)
    for copy in loads[2:]:
        copy.wait()

    def halo(w, block, tile, ref, start):
        y = apply(src, w - 9, block, tile, ref, start)
        f1[w] = (src[w].astype(F32) + y).astype(BF)

    def edge_row(j, carry):
        halo(8 + 2 + j, 1, 12 + j, prev, j * 4 * S)
        halo(48 + 2 + j, 7, j, nxt, j * 4 * S)
        return carry

    lax.fori_loop(0, 4, edge_row, 0)

    def edge_col(i, carry):
        w = (2 + i) * 8
        halo(w + 1, 3, i * 4 + 3, lefts, (1 + i) * 4 * S)
        halo(w + 6, 5, i * 4, rights, (1 + i) * 4 * S)
        return carry

    lax.fori_loop(0, 4, edge_col, 0)
    halo(9, 0, 15, lefts, 0)
    halo(14, 2, 12, rights, 0)
    halo(49, 6, 3, lefts, 5 * 4 * S)
    halo(54, 8, 0, rights, 5 * 4 * S)

    def final_tile(t, carry):
        i, j = t // 4, t % 4
        w = (2 + i) * 8 + 2 + j
        field = srcf[t] + apply(f1, w - 9, 4, t, tiles, t * ROWS)
        if last:
            field_out[pl.ds(t, E, stride=16), :] = field
        a = field.astype(BF)
        fields[t, :, :S] = a
        fields[t, :, S:] = (field - a.astype(F32)).astype(BF)
        return carry

    lax.fori_loop(0, 16, final_tile, 0, unroll=4)
    y = dot(fields[...].reshape(16 * E, 2 * S), jnp.concatenate([lo, lo], axis=0))
    read = jnp.zeros((E, U), F32)
    for t in range(16):
        read += jnp.where(hi == float(t), y[t * E : t * E + E], 0.0)
    present = (inc[...].astype(F32) + read).astype(BF)
    if last:
        present_out[...] = present
    else:
        for c in range(NC):
            present_out[c] = present


def sweep(last, *args):
    if last:
        out = (shape((E, U), BF), shape((E * 16, S), F32))
    else:
        out = shape((NC, E, U), BF)

    def body(*refs):
        sweep_body(last, *refs)

    return call(
        body,
        out,
        flops=2 * E * S * S * 4 * 52,
        moved=6 * MB,
        in_specs=[IN_VMEM] * 7 + [IN_HBM] * 5,
        out_specs=(IN_VMEM, IN_VMEM) if last else IN_VMEM,
        scratch_shapes=[
            pltpu.VMEM((64, E, S), BF),
            pltpu.VMEM((16, E, S), F32),
            pltpu.VMEM((64, E, S), BF),
            pltpu.VMEM((16, E, 2 * S), BF),
            pltpu.VMEM((16 * ROWS, S), BF),
            pltpu.VMEM((4 * ROWS, S), BF),
            pltpu.VMEM((4 * ROWS, S), BF),
            pltpu.VMEM((6 * ROWS, S), BF),
            pltpu.VMEM((6 * ROWS, S), BF),
            pltpu.SMEM((16, U), jnp.int32),
            pltpu.SemaphoreType.DMA((6,)),
        ],
    )(*args[:7], *keep(*args[7:]))


def shift(axis):
    size = lax.axis_size(axis)
    up = [(i, i + 1) for i in range(size - 1)]
    return up, [(j, i) for i, j in up]


def per_device(traces, incident, points, coupling, volume_tiles, tile_columns):
    row_up, row_down = shift("row")
    col_up, col_down = shift("col")
    tiles = volume_tiles.reshape(16 * ROWS, S)
    rows, cols, up, down, meta = pack(traces, points, coupling.reshape(1, U), tile_columns, tiles)
    rows = lax.all_to_all(rows, "row", 0, 0, tiled=True)
    cols = lax.all_to_all(cols, "col", 0, 0, tiled=True)
    prev = lax.ppermute(up, "row", row_up)
    nxt = lax.ppermute(down, "row", row_down)
    kernel, partials = make_kernel(cols, rows)
    lefts, rights, mid = edges(prev, nxt, meta, tiles)
    lefts = lax.ppermute(lefts, "col", col_up)
    rights = lax.ppermute(rights, "col", col_down)
    metas, moves = tables(mid, lefts, rights)
    for outer in range(2):
        last = outer == 1
        got = lax.all_to_all(partials, "row", 0, 0, tiled=True)
        sums = jnp.sum(got.astype(F32), axis=0)
        mid = sums.astype(BF)
        left = lax.ppermute(mid, "col", col_up)
        right = lax.ppermute(mid, "col", col_down)
        out = sweep(last, sums[1], mid, left, right, incident, metas, moves, tiles, prev, nxt, lefts, rights)
        if not last:
            out = lax.all_to_all(out, "col", 0, 0, tiled=True)
            partials = product(out, kernel)
    present, field = out
    return present, field.reshape(E, 4, 4, S)


def solution(mesh):
    in_specs = (
        P(None, ("row", "col")),
        P(None, ("row", "col")),
        P(None, ("row", "col")),
        P(("row", "col")),
        P("row", "col", None, None, None),
        P("row", "col", None),
    )
    out_specs = (P(None, ("row", "col")), P(None, "row", "col", None))
    return jax.shard_map(per_device, mesh=mesh, in_specs=in_specs, out_specs=out_specs, check_vma=False)
```

time: 152 us -> 125 us (0.82)
  blocking collectives: 30.4 us -> 60.7 us
  waiting for transfers between devices: 29 us -> 7.98 us
  local copies, waits for them, and re-layouts: 15.6 us -> 0.04 us
  starting transfers between devices: 40.7 us -> 25.5 us
  other arithmetic: 3.57 us -> 0.13 us
  Pallas kernels: 31.1 us -> 29.1 us
    all_to_all x1 -> x2, blocking collectives: 9.11 us -> 28.5 us  [the longest x1 18.5 us: per_device(): rows = lax.all_to_all(rows, 'row', 0, 0, tiled=True)]
    all_to_all x2 -> x0, starting transfers between devices: 14.9 us -> none  [the longest x1 7.63 us: per_device(): got = lax.all_to_all(partials, 'row', 0, 0, tiled=True)]
    unnamed x28 -> x14, local copies, waits for them, and re-layouts: 11.1 us -> 0.03 us
    all_to_all x1 -> x2, blocking collectives: 21.3 us -> 32.2 us  [per_device(): got = lax.all_to_all(partials, 'row', 0, 0, tiled=True)]
    ppermute x4, waiting for transfers between devices: 10.7 us -> 0.01 us  [the longest x1 0.01 us: per_device(): prev = lax.ppermute(up, 'row', row_up)]
    all_to_all x2 -> x0, waiting for transfers between devices: 8.78 us -> none  [the longest x1 8.78 us: per_device(): got = lax.all_to_all(partials, 'row', 0, 0, tiled=True)]
    another operation x15 -> x0, local copies, waits for them, and re-layouts: 2.81 us -> none  [per_device(): meta = jnp.stack(metas)]
    all_to_all x1, waiting for transfers between devices: 2.46 us -> 0.01 us  [per_device(): cols = lax.all_to_all(cols, 'col', 0, 0, tiled=True)]
  transfers between devices with their start and end apart: 11 -> 9, of which waited for: 6 -> 2; matrix products, arithmetic and copies ran while one was open for 6% -> 0% of each run, Pallas kernels for 7% -> 10%
where the time goes in v1:
time: 125 us; the launch traced here: 124 us
  blocking collectives  60.7 us (49%)
  Pallas kernels  29.1 us (23%)
  starting transfers between devices  25.5 us (20%)
  waiting for transfers between devices  7.98 us (6%)
    all_to_all x2, blocking collectives, per_device(): got = lax.all_to_all(partials, 'row', 0, 0, tiled=True)  32.2 us
    all_to_all x1, blocking collectives, per_device(): rows = lax.all_to_all(rows, 'row', 0, 0, tiled=True)  18.5 us
    pallas_call x2, Pallas kernels, sweep(): call(body, out, flops=2 * E * S * S * 4 * 52, moved=6 * MB, in_specs=[IN_...  13.6 us
    all_to_all x1, blocking collectives, per_device(): out = lax.all_to_all(out, 'col', 0, 0, tiled=True)  10.1 us
    pallas_call x1, Pallas kernels, make_kernel(): call(kernel_body, (hbm((NC, U, NR * U), BF), hbm((NR, 3, E, U), BF)), flo...  8.62 us
    ppermute x2, waiting for transfers between devices, per_device(): left = lax.ppermute(mid, 'col', col_up)  7.96 us
    all_to_all x1, starting transfers between devices, per_device(): cols = lax.all_to_all(cols, 'col', 0, 0, tiled=True)  5.39 us
    ppermute x2, starting transfers between devices, per_device(): left = lax.ppermute(mid, 'col', col_up)  4.47 us
  transfers between devices with their start and end apart: 9, of which 2 were waited for; matrix products, arithmetic and copies ran while one was open for 0% of the time, Pallas kernels for 10%

profile of v1, /device:TPU:8, one launch (start us, length us, event | category | flops | bytes accessed | tf_op | source)
XLA Modules:
  0.0 124.3 jit_solution(10238430436967803439)
XLA Ops:
  0.6 2.6 %shard_map.77 = (bf16[8,48,128]{2,1,0:T(8,128)(2,1)}, bf16[16,80,128]{2,1,0:T(8,128)(2,1)}, bf16[2064,128]{1,0:T(8,128)(2,1)}, bf16[2064,128]{1,0:T(8,128)(2,1)}, bf16[16,128]{1,0:T(8,128)(2,1)S(1)}) custom-call(bf16[64,128]{1,0:T(8,128)(2,1)} %traces_h.1, f32[3,128]{1,0:T(4,128)} %points_h.1, s32[1,128]{1,0:T(1,128)} %bitcast.11, s32[4,4,4]{2,1,0:T(4,128)} %columns_h.1, ...), custom_call_target="tpu_custom_call" | custom-call | tf_op jit(solution)/shard_map/pallas_call | solution.py:125
  3.2 3.4 %collective-permute-start.2 = (bf16[2064,128]{1,0:T(8,128)(2,1)}, bf16[2064,128]{1,0:T(8,128)(2,1)S(1)}, u32[]{:S(2)}, u32[]{:S(2)}) collective-permute-start(bf16[2064,128]{1,0:T(8,128)(2,1)} %get-tuple-element.19), channel_id=1, source_target_pairs={{0,16},{16,32},{32,48},{48,64},{64,80},{80,96},{96,112},{1,17},{17... | collective-permute-start | bytes 1585160 | tf_op jit(solution)/shard_map/ppermute | solution.py:465
  6.7 1.3 %collective-permute-start.3 = (bf16[2064,128]{1,0:T(8,128)(2,1)}, bf16[2064,128]{1,0:T(8,128)(2,1)S(1)}, u32[]{:S(2)}, u32[]{:S(2)}) collective-permute-start(bf16[2064,128]{1,0:T(8,128)(2,1)} %get-tuple-element.20), channel_id=1, source_target_pairs={{16,0},{32,16},{48,32},{64,48},{80,64},{96,80},{112,96},{17,1},{33... | collective-permute-start | bytes 1585160 | tf_op jit(solution)/shard_map/ppermute | solution.py:466
  8.0 18.5 %all_to_all.25.row_ref = bf16[8,48,128]{2,1,0:T(8,128)(2,1)} all-to-all(bf16[8,48,128]{2,1,0:T(8,128)(2,1)} %get-tuple-element.17), channel_id=1, replica_groups=mesh['row'=8,'col'=16] {'row'}, dimensions={0} | all-to-all | bytes 196608 | tf_op jit(solution)/shard_map/all_to_all | solution.py:463
  26.4 5.4 %all-to-all-start = ((bf16[16,80,128]{2,1,0:T(8,128)(2,1)}), bf16[16,80,128]{2,1,0:T(8,128)(2,1)S(1)}, u32[]{:S(2)}, u32[]{:S(2)}) async-start(bf16[16,80,128]{2,1,0:T(8,128)(2,1)} %get-tuple-element.16), calls=%async_computation | async-start | bytes 655360 | tf_op jit(solution)/shard_map/all_to_all | solution.py:464
  31.9 3.3 %shard_map.79 = (bf16[3120,128]{1,0:T(8,128)(2,1)}, bf16[3120,128]{1,0:T(8,128)(2,1)}, bf16[48,128]{1,0:T(8,128)(2,1)S(1)}) custom-call(bf16[2064,128]{1,0:T(8,128)(2,1)S(1)} %collective-permute-done.2.prev.refs_8_, bf16[2064,128]{1,0:T(8,128)(2,1)S(1)} %collective-permute-done.3.nxt.refs_9_, bf16[16,128]{1,0:T(8,128)(2,1)S(1)} %get-tuple-element.21.meta, ...), custom_call_target="tpu_custom_call" | custom-call | bytes 4194304 | tf_op jit(solution)/shard_map/pallas_call | solution.py:161
  35.2 2.0 %collective-permute-start.4 = (bf16[3120,128]{1,0:T(8,128)(2,1)}, bf16[3120,128]{1,0:T(8,128)(2,1)S(1)}, u32[]{:S(2)}, u32[]{:S(2)}) collective-permute-start(bf16[3120,128]{1,0:T(8,128)(2,1)} %get-tuple-element.23), channel_id=1, source_target_pairs={{0,1},{1,2},{2,3},{3,4},{4,5},{5,6},{6,7},{7,8},{8,9},{9,10},{10,1... | collective-permute-start | bytes 2396168 | tf_op jit(solution)/shard_map/ppermute | solution.py:469
  37.2 4.4 %collective-permute-start.5 = (bf16[3120,128]{1,0:T(8,128)(2,1)}, bf16[3120,128]{1,0:T(8,128)(2,1)S(1)}, u32[]{:S(2)}, u32[]{:S(2)}) collective-permute-start(bf16[3120,128]{1,0:T(8,128)(2,1)} %get-tuple-element.24), channel_id=1, source_target_pairs={{1,0},{2,1},{3,2},{4,3},{5,4},{6,5},{7,6},{8,7},{9,8},{10,9},{11,1... | collective-permute-start | bytes 2396168 | tf_op jit(solution)/shard_map/ppermute | solution.py:470
  41.7 8.6 %shard_map.78 = (bf16[16,128,1024]{2,1,0:T(8,128)(2,1)}, bf16[8,3,64,128]{3,2,1,0:T(8,128)(2,1)}) custom-call(bf16[16,80,128]{2,1,0:T(8,128)(2,1)S(1)} %all-to-all-done.col_ref, bf16[8,48,128]{2,1,0:T(8,128)(2,1)} %all_to_all.25.row_ref), custom_call_target="tpu_custom_call" | custom-call | flops 83886080 | bytes 6291456 | tf_op jit(solution)/shard_map/pallas_call | solution.py:263
  50.3 17.2 %all_to_all.26 = bf16[8,3,64,128]{3,2,1,0:T(8,128)(2,1)S(1)} all-to-all(bf16[8,3,64,128]{3,2,1,0:T(8,128)(2,1)} %get-tuple-element.18), channel_id=1, replica_groups=mesh['row'=8,'col'=16] {'row'}, dimensions={0} | all-to-all | bytes 786432 | tf_op jit(solution)/shard_map/all_to_all | solution.py:474
  67.5 0.1 convert_reduce_fusion.1
  67.6 2.2 %collective-permute-start.1 = (bf16[3,64,128]{2,1,0:T(8,128)(2,1)S(1)}, bf16[3,64,128]{2,1,0:T(8,128)(2,1)S(1)}, u32[]{:S(2)}, u32[]{:S(2)}) collective-permute-start(bf16[3,64,128]{2,1,0:T(8,128)(2,1)S(1)} %convert_element_type.13.refs_1_), channel_id=1, source_target_pairs={{1,0},{2,1},{3,2},{4,3},{5,4},{6,5},{7,6},{8,7},{9,8},{10,9},{11,1... | collective-permute-start | bytes 147464 | tf_op jit(solution)/shard_map/ppermute | solution.py:478
  69.8 2.4 %collective-permute-start = (bf16[3,64,128]{2,1,0:T(8,128)(2,1)S(1)}, bf16[3,64,128]{2,1,0:T(8,128)(2,1)S(1)}, u32[]{:S(2)}, u32[]{:S(2)}) collective-permute-start(bf16[3,64,128]{2,1,0:T(8,128)(2,1)S(1)} %convert_element_type.13.refs_1_), channel_id=1, source_target_pairs={{0,1},{1,2},{2,3},{3,4},{4,5},{5,6},{6,7},{7,8},{8,9},{9,10},{10,1... | collective-permute-start | bytes 147464 | tf_op jit(solution)/shard_map/ppermute | solution.py:477
  72.2 0.1 shard_map.80
  72.3 3.7 %collective-permute-done.refs_2_ = bf16[3,64,128]{2,1,0:T(8,128)(2,1)S(1)} collective-permute-done((bf16[3,64,128]{2,1,0:T(8,128)(2,1)S(1)}, bf16[3,64,128]{2,1,0:T(8,128)(2,1)S(1)}, u32[]{:S(2)}, u32[]{:S(2)}) %collective-permute-start) | collective-permute-done | bytes 49184 | tf_op jit(solution)/shard_map/ppermute | solution.py:477
  76.1 6.4 %shard_map.81 = bf16[16,64,128]{2,1,0:T(8,128)(2,1)S(1)} custom-call(f32[64,128]{1,0:T(8,128)S(1)} %slice_bitcast_fusion.1.refs_0_, bf16[3,64,128]{2,1,0:T(8,128)(2,1)S(1)} %convert_element_type.13.refs_1_, bf16[3,64,128]{2,1,0:T(8,128)(2,1)S(1)} %collective-permute-done.refs_2_, bf16[3,64,128]{2,1,0:T(8,128)(2,1)S(1)} %collective-permute-done.1.refs_3_, ...), custom_call_target="tpu_custom_call" | custom-call | flops 436207616 | bytes 6291456 | tf_op jit(solution)/shard_map/pallas_call | solution.py:429
  82.5 10.1 %all_to_all.27.p_ref = bf16[16,64,128]{2,1,0:T(8,128)(2,1)S(1)} all-to-all(bf16[16,64,128]{2,1,0:T(8,128)(2,1)S(1)} %shard_map.81), channel_id=1, replica_groups=mesh['row'=8,'col'=16] {'col'}, dimensions={0} | all-to-all | bytes 524288 | tf_op jit(solution)/shard_map/all_to_all | solution.py:481
  92.6 0.8 shard_map.82
  93.4 15.0 %all_to_all.28 = bf16[8,3,64,128]{3,2,1,0:T(8,128)(2,1)S(1)} all-to-all(bf16[8,3,64,128]{3,2,1,0:T(8,128)(2,1)S(1)} %shard_map.82), channel_id=1, replica_groups=mesh['row'=8,'col'=16] {'row'}, dimensions={0} | all-to-all | bytes 786432 | tf_op jit(solution)/shard_map/all_to_all | solution.py:474
  108.4 0.1 convert_reduce_fusion
  108.5 2.3 %collective-permute-start.7 = (bf16[3,64,128]{2,1,0:T(8,128)(2,1)S(1)}, bf16[3,64,128]{2,1,0:T(8,128)(2,1)S(1)}, u32[]{:S(2)}, u32[]{:S(2)}) collective-permute-start(bf16[3,64,128]{2,1,0:T(8,128)(2,1)S(1)} %convert_element_type.15.refs_1_), channel_id=1, source_target_pairs={{1,0},{2,1},{3,2},{4,3},{5,4},{6,5},{7,6},{8,7},{9,8},{10,9},{11,1... | collective-permute-start | bytes 147464 | tf_op jit(solution)/shard_map/ppermute | solution.py:478
  110.8 2.1 %collective-permute-start.6 = (bf16[3,64,128]{2,1,0:T(8,128)(2,1)S(1)}, bf16[3,64,128]{2,1,0:T(8,128)(2,1)S(1)}, u32[]{:S(2)}, u32[]{:S(2)}) collective-permute-start(bf16[3,64,128]{2,1,0:T(8,128)(2,1)S(1)} %convert_element_type.15.refs_1_), channel_id=1, source_target_pairs={{0,1},{1,2},{2,3},{3,4},{4,5},{5,6},{6,7},{7,8},{8,9},{9,10},{10,1... | collective-permute-start | bytes 147464 | tf_op jit(solution)/shard_map/ppermute | solution.py:477
  112.9 4.2 %collective-permute-done.6.refs_2_ = bf16[3,64,128]{2,1,0:T(8,128)(2,1)S(1)} collective-permute-done((bf16[3,64,128]{2,1,0:T(8,128)(2,1)S(1)}, bf16[3,64,128]{2,1,0:T(8,128)(2,1)S(1)}, u32[]{:S(2)}, u32[]{:S(2)}) %collective-permute-start.6) | collective-permute-done | bytes 49184 | tf_op jit(solution)/shard_map/ppermute | solution.py:477
  117.1 7.2 %shard_map.83 = (bf16[64,128]{1,0:T(8,128)(2,1)}, f32[1024,128]{1,0:T(8,128)}) custom-call(f32[64,128]{1,0:T(8,128)S(1)} %slice_bitcast_fusion.refs_0_, bf16[3,64,128]{2,1,0:T(8,128)(2,1)S(1)} %convert_element_type.15.refs_1_, bf16[3,64,128]{2,1,0:T(8,128)(2,1)S(1)} %collective-permute-done.6.refs_2_, ...), custom_call_target="tpu_custom_call" | custom-call | flops 436207616 | bytes 6291456 | tf_op jit(solution)/shard_map/pallas_call | solution.py:429
  (25 shorter events, 0.1 us)
Async XLA Ops:
  0.6 31.2 %copy-start = (bf16[4,4,4,128,128]{4,3,2,1,0:T(8,128)(2,1)S(1)}, bf16[4,4,4,128,128]{4,3,2,1,0:T(8,128)(2,1)}, u32[]{:S(2)}) copy-start(bf16[4,4,4,128,128]{4,3,2,1,0:T(8,128)(2,1)} %param.10) | copy-start | bytes 6291460
  3.2 72.9 %copy-start.6 = (bf16[64,128]{1,0:T(8,128)(2,1)S(1)}, bf16[64,128]{1,0:T(8,128)(2,1)}, u32[]{:S(2)}) copy-start(bf16[64,128]{1,0:T(8,128)(2,1)} %refs_4_.3) | copy-start | bytes 49156
  3.2 28.6 %collective-permute-start.2 = (bf16[2064,128]{1,0:T(8,128)(2,1)}, bf16[2064,128]{1,0:T(8,128)(2,1)S(1)}, u32[]{:S(2)}, u32[]{:S(2)}) collective-permute-start(bf16[2064,128]{1,0:T(8,128)(2,1)} %get-tuple-element.19), channel_id=1, source_target_pairs={{0,16},{16,32},{32,48},{48,64},{64,80},{80,96},{96,112},{1,17},{17... | collective-permute-start | bytes 1585160 | tf_op jit(solution)/shard_map/ppermute | solution.py:465
  6.7 25.2 %collective-permute-start.3 = (bf16[2064,128]{1,0:T(8,128)(2,1)}, bf16[2064,128]{1,0:T(8,128)(2,1)S(1)}, u32[]{:S(2)}, u32[]{:S(2)}) collective-permute-start(bf16[2064,128]{1,0:T(8,128)(2,1)} %get-tuple-element.20), channel_id=1, source_target_pairs={{16,0},{32,16},{48,32},{64,48},{80,64},{96,80},{112,96},{17,1},{33... | collective-permute-start | bytes 1585160 | tf_op jit(solution)/shard_map/ppermute | solution.py:466
  26.4 15.3 %all-to-all-start = ((bf16[16,80,128]{2,1,0:T(8,128)(2,1)}), bf16[16,80,128]{2,1,0:T(8,128)(2,1)S(1)}, u32[]{:S(2)}, u32[]{:S(2)}) async-start(bf16[16,80,128]{2,1,0:T(8,128)(2,1)} %get-tuple-element.16), calls=%async_computation | async-start | bytes 655360 | tf_op jit(solution)/shard_map/all_to_all | solution.py:464
  31.8 44.3 %copy-start.3 = (bf16[2064,128]{1,0:T(8,128)(2,1)}, bf16[2064,128]{1,0:T(8,128)(2,1)S(1)}, u32[]{:S(2)}) copy-start(bf16[2064,128]{1,0:T(8,128)(2,1)S(1)} %collective-permute-done.2.prev.refs_8_) | copy-start | bytes 1585156
  31.8 44.2 %copy-start.4 = (bf16[2064,128]{1,0:T(8,128)(2,1)}, bf16[2064,128]{1,0:T(8,128)(2,1)S(1)}, u32[]{:S(2)}) copy-start(bf16[2064,128]{1,0:T(8,128)(2,1)S(1)} %collective-permute-done.3.nxt.refs_9_) | copy-start | bytes 1585156
  35.2 37.0 %collective-permute-start.4 = (bf16[3120,128]{1,0:T(8,128)(2,1)}, bf16[3120,128]{1,0:T(8,128)(2,1)S(1)}, u32[]{:S(2)}, u32[]{:S(2)}) collective-permute-start(bf16[3120,128]{1,0:T(8,128)(2,1)} %get-tuple-element.23), channel_id=1, source_target_pairs={{0,1},{1,2},{2,3},{3,4},{4,5},{5,6},{6,7},{7,8},{8,9},{9,10},{10,1... | collective-permute-start | bytes 2396168 | tf_op jit(solution)/shard_map/ppermute | solution.py:469
  37.2 35.0 %collective-permute-start.5 = (bf16[3120,128]{1,0:T(8,128)(2,1)}, bf16[3120,128]{1,0:T(8,128)(2,1)S(1)}, u32[]{:S(2)}, u32[]{:S(2)}) collective-permute-start(bf16[3120,128]{1,0:T(8,128)(2,1)} %get-tuple-element.24), channel_id=1, source_target_pairs={{1,0},{2,1},{3,2},{4,3},{5,4},{6,5},{7,6},{8,7},{9,8},{10,9},{11,1... | collective-permute-start | bytes 2396168 | tf_op jit(solution)/shard_map/ppermute | solution.py:470
  67.5 25.1 %copy-start.5 = (bf16[16,128,1024]{2,1,0:T(8,128)(2,1)S(1)}, bf16[16,128,1024]{2,1,0:T(8,128)(2,1)}, u32[]{:S(2)}) copy-start(bf16[16,128,1024]{2,1,0:T(8,128)(2,1)} %get-tuple-element.27.k_ref) | copy-start | bytes 12582916
  67.6 4.7 %collective-permute-start.1 = (bf16[3,64,128]{2,1,0:T(8,128)(2,1)S(1)}, bf16[3,64,128]{2,1,0:T(8,128)(2,1)S(1)}, u32[]{:S(2)}, u32[]{:S(2)}) collective-permute-start(bf16[3,64,128]{2,1,0:T(8,128)(2,1)S(1)} %convert_element_type.13.refs_1_), channel_id=1, source_target_pairs={{1,0},{2,1},{3,2},{4,3},{5,4},{6,5},{7,6},{8,7},{9,8},{10,9},{11,1... | collective-permute-start | bytes 147464 | tf_op jit(solution)/shard_map/ppermute | solution.py:478
  69.8 6.3 %collective-permute-start = (bf16[3,64,128]{2,1,0:T(8,128)(2,1)S(1)}, bf16[3,64,128]{2,1,0:T(8,128)(2,1)S(1)}, u32[]{:S(2)}, u32[]{:S(2)}) collective-permute-start(bf16[3,64,128]{2,1,0:T(8,128)(2,1)S(1)} %convert_element_type.13.refs_1_), channel_id=1, source_target_pairs={{0,1},{1,2},{2,3},{3,4},{4,5},{5,6},{6,7},{7,8},{8,9},{9,10},{10,1... | collective-permute-start | bytes 147464 | tf_op jit(solution)/shard_map/ppermute | solution.py:477
  72.2 3.9 %copy-start.1 = (bf16[3120,128]{1,0:T(8,128)(2,1)}, bf16[3120,128]{1,0:T(8,128)(2,1)S(1)}, u32[]{:S(2)}) copy-start(bf16[3120,128]{1,0:T(8,128)(2,1)S(1)} %collective-permute-done.4.lefts.refs_10_) | copy-start | bytes 2396164
  72.2 3.9 %copy-start.2 = (bf16[3120,128]{1,0:T(8,128)(2,1)}, bf16[3120,128]{1,0:T(8,128)(2,1)S(1)}, u32[]{:S(2)}) copy-start(bf16[3120,128]{1,0:T(8,128)(2,1)S(1)} %collective-permute-done.5.rights.refs_11_) | copy-start | bytes 2396164
  108.5 4.4 %collective-permute-start.7 = (bf16[3,64,128]{2,1,0:T(8,128)(2,1)S(1)}, bf16[3,64,128]{2,1,0:T(8,128)(2,1)S(1)}, u32[]{:S(2)}, u32[]{:S(2)}) collective-permute-start(bf16[3,64,128]{2,1,0:T(8,128)(2,1)S(1)} %convert_element_type.15.refs_1_), channel_id=1, source_target_pairs={{1,0},{2,1},{3,2},{4,3},{5,4},{6,5},{7,6},{8,7},{9,8},{10,9},{11,1... | collective-permute-start | bytes 147464 | tf_op jit(solution)/shard_map/ppermute | solution.py:478
  110.8 6.3 %collective-permute-start.6 = (bf16[3,64,128]{2,1,0:T(8,128)(2,1)S(1)}, bf16[3,64,128]{2,1,0:T(8,128)(2,1)S(1)}, u32[]{:S(2)}, u32[]{:S(2)}) collective-permute-start(bf16[3,64,128]{2,1,0:T(8,128)(2,1)S(1)} %convert_element_type.15.refs_1_), channel_id=1, source_target_pairs={{0,1},{1,2},{2,3},{3,4},{4,5},{5,6},{6,7},{7,8},{8,9},{9,10},{10,1... | collective-permute-start | bytes 147464 | tf_op jit(solution)/shard_map/ppermute | solution.py:477

commit v2 on v1

--- a/solution.py
+++ b/solution.py
@@ -12,7 +12,9 @@
 NR, NC = 8, 16
 TOTAL = U * NR * NC
 MB = 1 << 20
+HEAD = 3 * E
 ROWS = 4 * S
+TAIL = HEAD + 2 * ROWS
 BF, F32 = jnp.bfloat16, jnp.float32
 SIN = (3.14158202, -5.1671428, 2.54189903, -0.55463619)
 NT = (((1,), (1,)), ((), ()))
@@ -137,64 +139,69 @@
     )(*keep(traces, points, coupling, columns, tiles))
 
 
-def edge_body(prev, nxt, meta, tiles, left_out, right_out, mid_out, sems):
+def fill_body(tiles, left_out, right_out, sems):
     copies = []
     for out, j in ((left_out, 3), (right_out, 0)):
-        pieces = [prev.at[pl.ds(j * ROWS, ROWS)]]
-        pieces += [tiles.at[pl.ds((4 * i + j) * ROWS, ROWS)] for i in range(4)]
-        pieces += [nxt.at[pl.ds(j * ROWS, ROWS)]]
-        for n, piece in enumerate(pieces):
-            copies.append(pltpu.make_async_copy(piece, out.at[pl.ds(n * ROWS, ROWS)], sems.at[len(copies)]))
-    for copy in copies:
-        copy.start()
-    for j in range(3):
-        value = (prev, None, nxt)[j]
-        value = meta[...] if j == 1 else value[4 * ROWS :]
-        for out, start in ((left_out, 6 * ROWS), (right_out, 6 * ROWS), (mid_out, 0)):
-            out[start + 16 * j : start + 16 * j + 16] = value
-    for copy in copies:
-        copy.wait()
-
-
-def edges(prev, nxt, meta, tiles):
-    side = vmem((6 * ROWS + 48, S), BF)
-    return call(
-        edge_body,
-        (side, side, vmem((48, U), BF)),
-        moved=4 * MB,
-        in_specs=[IN_VMEM, IN_VMEM, IN_VMEM, IN_ANY],
-        out_specs=(IN_VMEM,) * 3,
-        scratch_shapes=[pltpu.SemaphoreType.DMA((12,))],
-    )(prev, nxt, meta, tiles)
-
-
-def table_body(mid, lefts, rights, meta_out, moves_out, sides, sems):
-    copies = [
-        pltpu.make_async_copy(h.at[pl.ds(6 * ROWS, 48)], sides.at[n], sems.at[n]) for n, h in enumerate((lefts, rights))
-    ]
+        for i in range(4):
+            piece = tiles.at[pl.ds((4 * i + j) * ROWS, ROWS)]
+            copies.append(pltpu.make_async_copy(piece, out.at[pl.ds(i * ROWS, ROWS)], sems.at[len(copies)]))
     for copy in copies:
         copy.start()
     for copy in copies:
         copy.wait()
-    moves_out[...] = jnp.zeros_like(moves_out)
-    for br in range(3):
-        for bc in range(3):
-            b = 3 * br + bc
-            m = (sides[0], mid[...], sides[1])[bc][16 * br : 16 * br + 16]
-            meta_out[16 * b : 16 * b + 16] = m
-            o = m.astype(F32)[2:3]
-            o = o + 5.0 * (jnp.where(o >= 3.0, 1.0, 0.0) + jnp.where(o >= 6.0, 1.0, 0.0))
-            moves_out[b : b + 1] = o.astype(jnp.int32)
-
-
-def tables(mid, lefts, rights):
+
+
+def fill(tiles):
+    side = shape((4 * ROWS, S), BF)
     return call(
-        table_body,
-        (vmem((144, U), BF), vmem((16, U), jnp.int32)),
-        in_specs=[IN_VMEM, IN_ANY, IN_ANY],
+        fill_body,
+        (side, side),
+        moved=2 * MB,
+        in_specs=[IN_HBM],
         out_specs=(IN_VMEM,) * 2,
-        scratch_shapes=[pltpu.VMEM((2, 48, U), BF), pltpu.SemaphoreType.DMA((2,))],
-    )(mid, lefts, rights)
+        scratch_shapes=[pltpu.SemaphoreType.DMA((8,))],
+    )(*keep(tiles))
+
+
+def near_body(got, prev, nxt, meta, own_out, mid_out, left_out, right_out, meta_out, sems):
+    copies = []
+    for out, j in ((left_out, 3), (right_out, 0)):
+        for n, source in enumerate((prev, nxt)):
+            piece = source.at[pl.ds(j * ROWS, ROWS)]
+            copies.append(pltpu.make_async_copy(piece, out.at[pl.ds(HEAD + n * ROWS, ROWS)], sems.at[len(copies)]))
+    for n, source in enumerate((prev, nxt)):
+        piece = source.at[pl.ds(4 * ROWS, 16)]
+        copies.append(pltpu.make_async_copy(piece, meta_out.at[pl.ds(32 * n, 16)], sems.at[len(copies)]))
+    for copy in copies:
+        copy.start()
+    meta_out[16:32] = meta[...]
+    for j in range(3):
+        total = got[0, j].astype(F32)
+        for r in range(1, NR):
+            total += got[r, j].astype(F32)
+        if j == 1:
+            own_out[...] = total
+        value = total.astype(BF)
+        mid_out[j * E : j * E + E] = value
+        left_out[j * E : j * E + E] = value
+        right_out[j * E : j * E + E] = value
+    for copy in copies:
+        copy.wait()
+    metas = meta_out[...]
+    left_out[TAIL:] = metas
+    right_out[TAIL:] = metas
+
+
+def near(got, prev, nxt, meta):
+    side = shape((TAIL + 48, S), BF)
+    return call(
+        near_body,
+        (shape((E, U), F32), shape((HEAD, U), BF), side, side, shape((48, U), BF)),
+        moved=2 * MB,
+        in_specs=[IN_VMEM, IN_ANY, IN_ANY, IN_VMEM],
+        out_specs=(IN_VMEM,) * 5,
+        scratch_shapes=[pltpu.SemaphoreType.DMA((6,))],
+    )(got, prev, nxt, meta)
 
 
 def write_partials(acc, out):
@@ -303,23 +310,34 @@
     return ((0, 2), (1, 3)) if b == 0 else ((6, 0), (7, 1)) if b == 2 else tuple((2 + i, i) for i in range(4))
 
 
-def sweep_body(last, own_ref, mid, left, right, inc, metas, moves_v, tiles_h, prev_h, nxt_h, lefts_h, rights_h, *rest):
+def sweep_body(last, own_ref, mid, left, right, left_far, right_far, inc, mid_metas, tiles_h, prev_h, nxt_h, lefts_h, rights_h, *rest):
     if last:
         present_out, field_out = rest[:2]
     else:
         present_out, field_out = rest[0], None
-    src, srcf, f1, fields, tiles, prev, nxt, lefts, rights, moves, sems = rest[2 if last else 1 :]
+    src, srcf, f1, fields, tiles, prev, nxt, lefts, rights, moves_v, moves, sems = rest[2 if last else 1 :]
     loads = [(moves_v, moves), (tiles_h, tiles)]
     loads += [(h.at[pl.ds(0, 4 * ROWS)], v) for h, v in ((prev_h, prev), (nxt_h, nxt))]
-    loads += [(h.at[pl.ds(0, 6 * ROWS)], v) for h, v in ((lefts_h, lefts), (rights_h, rights))]
+    loads += [(lefts_h, lefts), (rights_h, rights)]
     loads = [pltpu.make_async_copy(a, b, sems.at[n]) for n, (a, b) in enumerate(loads)]
-    for copy in loads:
+    for copy in loads[1:]:
         copy.start()
+
+    def meta(br, bc):
+        m = mid_metas[16 * br : 16 * br + 16] if bc == 1 else (left_far, right_far)[bc // 2][TAIL + 16 * br : TAIL + 16 * br + 16]
+        return m.astype(F32)
+
+    moves_v[...] = jnp.zeros_like(moves_v)
+    for br in range(3):
+        for bc in range(3):
+            o = meta(br, bc)[2:3]
+            o = o + 5.0 * (jnp.where(o >= 3.0, 1.0, 0.0) + jnp.where(o >= 6.0, 1.0, 0.0))
+            moves_v[3 * br + bc : 3 * br + bc + 1] = o.astype(jnp.int32)
+    loads[0].start()
     line = lax.broadcasted_iota(jnp.int32, (S, U), 0).astype(F32)
 
     def coupling(br, bc):
-        at = 16 * (3 * br + bc)
-        m = metas[at : at + 16].astype(F32)
+        m = meta(br, bc)
         return m[0:1], jnp.where(m[1:2] == line, 1.0, 0.0).astype(BF)
 
     def masked(c, hi, ids):
@@ -327,7 +345,7 @@
 
     def place(br, bc):
         hi, lo = coupling(br, bc)
-        c = (left, mid, right)[bc][br]
+        c = (left, mid, right)[bc][br * E : br * E + E]
         places = [(R * 8 + C, i * 4 + j) for R, i in span(br) for C, j in span(bc)]
         out = dot(masked(c, hi, [t for _, t in places]), lo, NT).astype(BF)
         for n, (w, _) in enumerate(places):
@@ -355,7 +373,7 @@
         for h in range(2):
             ks = (2 * h, 2 * h + 1)
             x = jnp.concatenate([values[base + moves[block, tile * 4 + k]] for k in ks], axis=1)
-            a = [ref[pl.ds(pl.multiple_of(start + k * S, S), S), :] for k in ks]
+            a = [ref[pl.ds(pl.multiple_of(start + k * S, 64), S), :] for k in ks]
             y = dot(x, jnp.concatenate(a, axis=1), NT)
             total = y if total is None else total + y
         return total
@@ -383,15 +401,15 @@
 
     def edge_col(i, carry):
         w = (2 + i) * 8
-        halo(w + 1, 3, i * 4 + 3, lefts, (1 + i) * 4 * S)
-        halo(w + 6, 5, i * 4, rights, (1 + i) * 4 * S)
+        halo(w + 1, 3, i * 4 + 3, lefts, i * ROWS)
+        halo(w + 6, 5, i * 4, rights, i * ROWS)
         return carry
 
     lax.fori_loop(0, 4, edge_col, 0)
-    halo(9, 0, 15, lefts, 0)
-    halo(14, 2, 12, rights, 0)
-    halo(49, 6, 3, lefts, 5 * 4 * S)
-    halo(54, 8, 0, rights, 5 * 4 * S)
+    halo(9, 0, 15, left_far, HEAD)
+    halo(14, 2, 12, right_far, HEAD)
+    halo(49, 6, 3, left_far, HEAD + ROWS)
+    halo(54, 8, 0, right_far, HEAD + ROWS)
 
     def final_tile(t, carry):
         i, j = t // 4, t % 4
@@ -431,7 +449,7 @@
         out,
         flops=2 * E * S * S * 4 * 52,
         moved=6 * MB,
-        in_specs=[IN_VMEM] * 7 + [IN_HBM] * 5,
+        in_specs=[IN_VMEM] * 8 + [IN_HBM] * 5,
         out_specs=(IN_VMEM, IN_VMEM) if last else IN_VMEM,
         scratch_shapes=[
             pltpu.VMEM((64, E, S), BF),
@@ -441,12 +459,13 @@
             pltpu.VMEM((16 * ROWS, S), BF),
             pltpu.VMEM((4 * ROWS, S), BF),
             pltpu.VMEM((4 * ROWS, S), BF),
-            pltpu.VMEM((6 * ROWS, S), BF),
-            pltpu.VMEM((6 * ROWS, S), BF),
+            pltpu.VMEM((4 * ROWS, S), BF),
+            pltpu.VMEM((4 * ROWS, S), BF),
+            pltpu.VMEM((16, U), jnp.int32),
             pltpu.SMEM((16, U), jnp.int32),
             pltpu.SemaphoreType.DMA((6,)),
         ],
-    )(*args[:7], *keep(*args[7:]))
+    )(*args[:8], *keep(*args[8:]))
 
 
 def shift(axis):
@@ -462,24 +481,28 @@
     rows, cols, up, down, meta = pack(traces, points, coupling.reshape(1, U), tile_columns, tiles)
     rows = lax.all_to_all(rows, "row", 0, 0, tiled=True)
     cols = lax.all_to_all(cols, "col", 0, 0, tiled=True)
+    lefts, rights = fill(tiles)
+    lefts = lax.ppermute(lefts, "col", col_up)
+    rights = lax.ppermute(rights, "col", col_down)
     prev = lax.ppermute(up, "row", row_up)
     nxt = lax.ppermute(down, "row", row_down)
     kernel, partials = make_kernel(cols, rows)
-    lefts, rights, mid = edges(prev, nxt, meta, tiles)
-    lefts = lax.ppermute(lefts, "col", col_up)
-    rights = lax.ppermute(rights, "col", col_down)
-    metas, moves = tables(mid, lefts, rights)
+    got = lax.all_to_all(partials, "row", 0, 0, tiled=True)
+    own, mid, to_right, to_left, metas = near(got, prev, nxt, meta)
+    left = lax.ppermute(to_right, "col", col_up)
+    right = lax.ppermute(to_left, "col", col_down)
+    far = (left, right)
     for outer in range(2):
         last = outer == 1
-        got = lax.all_to_all(partials, "row", 0, 0, tiled=True)
-        sums = jnp.sum(got.astype(F32), axis=0)
-        mid = sums.astype(BF)
-        left = lax.ppermute(mid, "col", col_up)
-        right = lax.ppermute(mid, "col", col_down)
-        out = sweep(last, sums[1], mid, left, right, incident, metas, moves, tiles, prev, nxt, lefts, rights)
+        out = sweep(last, own, mid, left, right, *far, incident, metas, tiles, prev, nxt, lefts, rights)
         if not last:
             out = lax.all_to_all(out, "col", 0, 0, tiled=True)
             partials = product(out, kernel)
+            got = lax.all_to_all(partials, "row", 0, 0, tiled=True)
+            sums = jnp.sum(got.astype(F32), axis=0)
+            own, mid = sums[1], sums.astype(BF).reshape(HEAD, U)
+            left = lax.ppermute(mid, "col", col_up)
+            right = lax.ppermute(mid, "col", col_down)
     present, field = out
     return present, field.reshape(E, 4, 4, S)
 

time: 125 us -> 123 us (0.984)
  blocking collectives: 60.7 us -> 47.2 us
  starting transfers between devices: 25.5 us -> 32.6 us
  waiting for transfers between devices: 7.98 us -> 13 us
    all_to_all x2 -> x1, blocking collectives: 32.2 us -> 17.5 us  [per_device(): got = lax.all_to_all(partials, 'row', 0, 0, tiled=True)]
    ppermute x0 -> x2, starting transfers between devices: none -> 6.59 us  [the longest x1 4.54 us: per_device(): right = lax.ppermute(to_left, 'col', col_down)]
    all_to_all x0 -> x1, starting transfers between devices: none -> 5.78 us  [per_device(): got = lax.all_to_all(partials, 'row', 0, 0, tiled=True)]
    ppermute x0 -> x2, waiting for transfers between devices: none -> 4.54 us  [the longest x1 2.84 us: per_device(): left = lax.ppermute(to_right, 'col', col_up)]
    all_to_all x1, blocking collectives: 10.1 us -> 14 us  [per_device(): out = lax.all_to_all(out, 'col', 0, 0, tiled=True)]
    ppermute x2 -> x1, waiting for transfers between devices: 7.96 us -> 4.21 us  [per_device(): left = lax.ppermute(mid, 'col', col_up)]
    all_to_all x1, blocking collectives: 18.5 us -> 15.7 us  [per_device(): rows = lax.all_to_all(rows, 'row', 0, 0, tiled=True)]
    ppermute x2 -> x1, starting transfers between devices: 4.47 us -> 2.07 us  [per_device(): left = lax.ppermute(mid, 'col', col_up)]
  transfers between devices with their start and end apart: 9 -> 10, of which waited for: 2 -> 5; matrix products, arithmetic and copies ran while one was open for 0% -> 0% of each run, Pallas kernels for 10% -> 9%
where the time goes in v2:
time: 123 us; the launch traced here: 122 us
  blocking collectives  47.2 us (38%)
  starting transfers between devices  32.6 us (27%)
  Pallas kernels  28.2 us (23%)
  waiting for transfers between devices  13 us (11%)
    all_to_all x1, blocking collectives, per_device(): got = lax.all_to_all(partials, 'row', 0, 0, tiled=True)  17.5 us
    all_to_all x1, blocking collectives, per_device(): rows = lax.all_to_all(rows, 'row', 0, 0, tiled=True)  15.7 us
    pallas_call x2, Pallas kernels, sweep(): call(body, out, flops=2 * E * S * S * 4 * 52, moved=6 * MB, in_specs=[IN_...  14.2 us
    all_to_all x1, blocking collectives, per_device(): out = lax.all_to_all(out, 'col', 0, 0, tiled=True)  14 us
    pallas_call x1, Pallas kernels, make_kernel(): call(kernel_body, (hbm((NC, U, NR * U), BF), hbm((NR, 3, E, U), BF)), flo...  8.62 us
    all_to_all x1, starting transfers between devices, per_device(): got = lax.all_to_all(partials, 'row', 0, 0, tiled=True)  5.78 us
    all_to_all x1, starting transfers between devices, per_device(): cols = lax.all_to_all(cols, 'col', 0, 0, tiled=True)  5.39 us
    ppermute x1, starting transfers between devices, per_device(): rights = lax.ppermute(rights, 'col', col_down)  4.54 us
  transfers between devices with their start and end apart: 10, of which 5 were waited for; matrix products, arithmetic and copies ran while one was open for 0% of the time, Pallas kernels for 9%

profile of v2, /device:TPU:8, one launch (start us, length us, event | category | flops | bytes accessed | tf_op | source)
XLA Modules:
  0.0 122.0 jit_solution(14948689127650983189)
XLA Ops:
  0.6 2.4 %shard_map.77 = (bf16[8,48,128]{2,1,0:T(8,128)(2,1)}, bf16[16,80,128]{2,1,0:T(8,128)(2,1)}, bf16[2064,128]{1,0:T(8,128)(2,1)}, bf16[2064,128]{1,0:T(8,128)(2,1)}, bf16[16,128]{1,0:T(8,128)(2,1)S(1)}) custom-call(bf16[64,128]{1,0:T(8,128)(2,1)} %traces_h.1, f32[3,128]{1,0:T(4,128)} %points_h.1, s32[1,128]{1,0:T(1,128)} %bitcast.13, s32[4,4,4]{2,1,0:T(4,128)} %columns_h.1, ...), custom_call_target="tpu_custom_call" | custom-call | tf_op jit(solution)/shard_map/pallas_call | solution.py:127
  3.1 15.7 %all_to_all.25.row_ref = bf16[8,48,128]{2,1,0:T(8,128)(2,1)} all-to-all(bf16[8,48,128]{2,1,0:T(8,128)(2,1)} %get-tuple-element.19), channel_id=1, replica_groups=mesh['row'=8,'col'=16] {'row'}, dimensions={0} | all-to-all | bytes 196608 | tf_op jit(solution)/shard_map/all_to_all | solution.py:482
  18.7 5.4 %all-to-all-start = ((bf16[16,80,128]{2,1,0:T(8,128)(2,1)}), bf16[16,80,128]{2,1,0:T(8,128)(2,1)S(1)}, u32[]{:S(2)}, u32[]{:S(2)}) async-start(bf16[16,80,128]{2,1,0:T(8,128)(2,1)} %get-tuple-element.18), calls=%async_computation | async-start | bytes 655360 | tf_op jit(solution)/shard_map/all_to_all | solution.py:483
  24.1 2.8 %collective-permute-start = (bf16[2064,128]{1,0:T(8,128)(2,1)}, bf16[2064,128]{1,0:T(8,128)(2,1)S(1)}, u32[]{:S(2)}, u32[]{:S(2)}) collective-permute-start(bf16[2064,128]{1,0:T(8,128)(2,1)} %get-tuple-element.21), channel_id=1, source_target_pairs={{0,16},{16,32},{32,48},{48,64},{64,80},{80,96},{96,112},{1,17},{17... | collective-permute-start | bytes 1585160 | tf_op jit(solution)/shard_map/ppermute | solution.py:487
  26.9 1.3 %collective-permute-start.1 = (bf16[2064,128]{1,0:T(8,128)(2,1)}, bf16[2064,128]{1,0:T(8,128)(2,1)S(1)}, u32[]{:S(2)}, u32[]{:S(2)}) collective-permute-start(bf16[2064,128]{1,0:T(8,128)(2,1)} %get-tuple-element.22), channel_id=1, source_target_pairs={{16,0},{32,16},{48,32},{64,48},{80,64},{96,80},{112,96},{17,1},{33... | collective-permute-start | bytes 1585160 | tf_op jit(solution)/shard_map/ppermute | solution.py:488
  28.2 2.1 %all-to-all-done.col_ref = bf16[16,80,128]{2,1,0:T(8,128)(2,1)S(1)} async-done(((bf16[16,80,128]{2,1,0:T(8,128)(2,1)}), bf16[16,80,128]{2,1,0:T(8,128)(2,1)S(1)}, u32[]{:S(2)}, u32[]{:S(2)}) %all-to-all-start) | async-done | bytes 327712 | tf_op jit(solution)/shard_map/all_to_all | solution.py:483
  30.3 8.6 %shard_map.78 = (bf16[16,128,1024]{2,1,0:T(8,128)(2,1)}, bf16[8,3,64,128]{3,2,1,0:T(8,128)(2,1)}) custom-call(bf16[16,80,128]{2,1,0:T(8,128)(2,1)S(1)} %all-to-all-done.col_ref, bf16[8,48,128]{2,1,0:T(8,128)(2,1)} %all_to_all.25.row_ref), custom_call_target="tpu_custom_call" | custom-call | flops 83886080 | bytes 6291456 | tf_op jit(solution)/shard_map/pallas_call | solution.py:270
  38.9 5.8 %all-to-all-start.2 = ((bf16[8,3,64,128]{3,2,1,0:T(8,128)(2,1)}), bf16[8,3,64,128]{3,2,1,0:T(8,128)(2,1)S(1)}, u32[]{:S(2)}, u32[]{:S(2)}) async-start(bf16[8,3,64,128]{3,2,1,0:T(8,128)(2,1)} %get-tuple-element.20), calls=%async_computation.2 | async-start | bytes 786432 | tf_op jit(solution)/shard_map/all_to_all | solution.py:490
  44.7 1.3 %shard_map.80 = (bf16[2048,128]{1,0:T(8,128)(2,1)S(1)}, bf16[2048,128]{1,0:T(8,128)(2,1)S(1)}) custom-call(bf16[8192,128]{1,0:T(8,128)(2,1)} %bitcast.10), custom_call_target="tpu_custom_call" | custom-call | bytes 2097152 | tf_op jit(solution)/shard_map/pallas_call | solution.py:156
  46.0 1.9 %collective-permute-start.4 = (bf16[2048,128]{1,0:T(8,128)(2,1)S(1)}, bf16[2048,128]{1,0:T(8,128)(2,1)S(1)}, u32[]{:S(2)}, u32[]{:S(2)}) collective-permute-start(bf16[2048,128]{1,0:T(8,128)(2,1)S(1)} %get-tuple-element.29), channel_id=1, source_target_pairs={{0,1},{1,2},{2,3},{3,4},{4,5},{5,6},{6,7},{7,8},{8,9},{9,10},{10,1... | collective-permute-start | bytes 1572872 | tf_op jit(solution)/shard_map/ppermute | solution.py:485
  48.0 4.5 %collective-permute-start.5 = (bf16[2048,128]{1,0:T(8,128)(2,1)S(1)}, bf16[2048,128]{1,0:T(8,128)(2,1)}, u32[]{:S(2)}, u32[]{:S(2)}) collective-permute-start(bf16[2048,128]{1,0:T(8,128)(2,1)S(1)} %get-tuple-element.30), channel_id=1, source_target_pairs={{1,0},{2,1},{3,2},{4,3},{5,4},{6,5},{7,6},{8,7},{9,8},{10,9},{11,1... | collective-permute-start | bytes 1572872 | tf_op jit(solution)/shard_map/ppermute | solution.py:486
  52.6 2.1 %all-to-all-done.2.got = bf16[8,3,64,128]{3,2,1,0:T(8,128)(2,1)S(1)} async-done(((bf16[8,3,64,128]{3,2,1,0:T(8,128)(2,1)}), bf16[8,3,64,128]{3,2,1,0:T(8,128)(2,1)S(1)}, u32[]{:S(2)}, u32[]{:S(2)}) %all-to-all-start.2) | async-done | bytes 393248 | tf_op jit(solution)/shard_map/all_to_all | solution.py:490
  55.5 2.1 %collective-permute-start.2 = (bf16[1264,128]{1,0:T(8,128)(2,1)S(1)}, bf16[1264,128]{1,0:T(8,128)(2,1)S(1)}, u32[]{:S(2)}, u32[]{:S(2)}) collective-permute-start(bf16[1264,128]{1,0:T(8,128)(2,1)S(1)} %get-tuple-element.26), channel_id=1, source_target_pairs={{0,1},{1,2},{2,3},{3,4},{4,5},{5,6},{6,7},{7,8},{8,9},{9,10},{10,1... | collective-permute-start | bytes 970760 | tf_op jit(solution)/shard_map/ppermute | solution.py:492
  57.5 4.5 %collective-permute-start.3 = (bf16[1264,128]{1,0:T(8,128)(2,1)S(1)}, bf16[1264,128]{1,0:T(8,128)(2,1)S(1)}, u32[]{:S(2)}, u32[]{:S(2)}) collective-permute-start(bf16[1264,128]{1,0:T(8,128)(2,1)S(1)} %get-tuple-element.27), channel_id=1, source_target_pairs={{1,0},{2,1},{3,2},{4,3},{5,4},{6,5},{7,6},{8,7},{9,8},{10,9},{11,1... | collective-permute-start | bytes 970760 | tf_op jit(solution)/shard_map/ppermute | solution.py:493
  62.1 2.8 %collective-permute-done.2.refs_2_.refs_4_ = bf16[1264,128]{1,0:T(8,128)(2,1)S(1)} collective-permute-done((bf16[1264,128]{1,0:T(8,128)(2,1)S(1)}, bf16[1264,128]{1,0:T(8,128)(2,1)S(1)}, u32[]{:S(2)}, u32[]{:S(2)}) %collective-permute-start.2) | collective-permute-done | bytes 323616 | tf_op jit(solution)/shard_map/ppermute | solution.py:492
  65.0 1.7 %collective-permute-done.3.refs_3_.refs_5_ = bf16[1264,128]{1,0:T(8,128)(2,1)S(1)} collective-permute-done((bf16[1264,128]{1,0:T(8,128)(2,1)S(1)}, bf16[1264,128]{1,0:T(8,128)(2,1)S(1)}, u32[]{:S(2)}, u32[]{:S(2)}) %collective-permute-start.3) | collective-permute-done | bytes 323616 | tf_op jit(solution)/shard_map/ppermute | solution.py:493
  66.7 6.8 %shard_map.81 = bf16[16,64,128]{2,1,0:T(8,128)(2,1)S(1)} custom-call(f32[64,128]{1,0:T(8,128)S(1)} %get-tuple-element.24.refs_0_, bf16[192,128]{1,0:T(8,128)(2,1)S(1)} %get-tuple-element.25.refs_1_, bf16[1264,128]{1,0:T(8,128)(2,1)S(1)} %collective-permute-done.2.refs_2_.refs_4_, bf16[1264,128]{1,0:T(8,128)(2,1)S(1)} %collective-permute-done.3.refs_3_.refs_5_, ...), custom_call_target="tpu_custom_call" | custom-call | flops 436207616 | bytes 6291456 | tf_op jit(solution)/shard_map/pallas_call | solution.py:447
  73.5 14.0 %all_to_all.26.p_ref = bf16[16,64,128]{2,1,0:T(8,128)(2,1)S(1)} all-to-all(bf16[16,64,128]{2,1,0:T(8,128)(2,1)S(1)} %shard_map.81), channel_id=1, replica_groups=mesh['row'=8,'col'=16] {'col'}, dimensions={0} | all-to-all | bytes 524288 | tf_op jit(solution)/shard_map/all_to_all | solution.py:499
  87.5 0.8 shard_map.82
  88.4 17.5 %all_to_all.27 = bf16[8,3,64,128]{3,2,1,0:T(8,128)(2,1)S(1)} all-to-all(bf16[8,3,64,128]{3,2,1,0:T(8,128)(2,1)S(1)} %shard_map.82), channel_id=1, replica_groups=mesh['row'=8,'col'=16] {'row'}, dimensions={0} | all-to-all | bytes 786432 | tf_op jit(solution)/shard_map/all_to_all | solution.py:501
  106.0 2.3 %collective-permute-start.7 = (bf16[192,128]{1,0:T(8,128)(2,1)S(1)}, bf16[192,128]{1,0:T(8,128)(2,1)S(1)}, u32[]{:S(2)}, u32[]{:S(2)}) collective-permute-start(bf16[192,128]{1,0:T(8,128)(2,1)S(1)} %bitcast.6), channel_id=1, source_target_pairs={{1,0},{2,1},{3,2},{4,3},{5,4},{6,5},{7,6},{8,7},{9,8},{10,9},{11,1... | collective-permute-start | bytes 147464 | tf_op jit(solution)/shard_map/ppermute | solution.py:505
  108.2 2.1 %collective-permute-start.6 = (bf16[192,128]{1,0:T(8,128)(2,1)S(1)}, bf16[192,128]{1,0:T(8,128)(2,1)S(1)}, u32[]{:S(2)}, u32[]{:S(2)}) collective-permute-start(bf16[192,128]{1,0:T(8,128)(2,1)S(1)} %bitcast.7), channel_id=1, source_target_pairs={{0,1},{1,2},{2,3},{3,4},{4,5},{5,6},{6,7},{7,8},{8,9},{9,10},{10,1... | collective-permute-start | bytes 147464 | tf_op jit(solution)/shard_map/ppermute | solution.py:504
  110.3 4.2 %collective-permute-done.6.refs_2_ = bf16[192,128]{1,0:T(8,128)(2,1)S(1)} collective-permute-done((bf16[192,128]{1,0:T(8,128)(2,1)S(1)}, bf16[192,128]{1,0:T(8,128)(2,1)S(1)}, u32[]{:S(2)}, u32[]{:S(2)}) %collective-permute-start.6) | collective-permute-done | bytes 49184 | tf_op jit(solution)/shard_map/ppermute | solution.py:504
  114.6 7.4 %shard_map.83 = (bf16[64,128]{1,0:T(8,128)(2,1)}, f32[1024,128]{1,0:T(8,128)}) custom-call(f32[64,128]{1,0:T(8,128)S(1)} %slice_bitcast_fusion.refs_0_, bf16[192,128]{1,0:T(8,128)(2,1)S(1)} %bitcast.8, bf16[192,128]{1,0:T(8,128)(2,1)S(1)} %collective-permute-done.6.refs_2_, bf16[192,128]{1,0:T(8,128)(2,1)S(1)} %collective-permute-done.7.refs_3_, ...), custom_call_target="tpu_custom_call" | custom-call | flops 436207616 | bytes 6291456 | tf_op jit(solution)/shard_map/pallas_call | solution.py:447
  (19 shorter events, 0.9 us)
Async XLA Ops:
  0.6 66.0 %copy-start.3 = (bf16[64,128]{1,0:T(8,128)(2,1)S(1)}, bf16[64,128]{1,0:T(8,128)(2,1)}, u32[]{:S(2)}) copy-start(bf16[64,128]{1,0:T(8,128)(2,1)} %refs_6_.3) | copy-start | bytes 49156
  18.7 11.5 %all-to-all-start = ((bf16[16,80,128]{2,1,0:T(8,128)(2,1)}), bf16[16,80,128]{2,1,0:T(8,128)(2,1)S(1)}, u32[]{:S(2)}, u32[]{:S(2)}) async-start(bf16[16,80,128]{2,1,0:T(8,128)(2,1)} %get-tuple-element.18), calls=%async_computation | async-start | bytes 655360 | tf_op jit(solution)/shard_map/all_to_all | solution.py:483
  24.1 28.4 %collective-permute-start = (bf16[2064,128]{1,0:T(8,128)(2,1)}, bf16[2064,128]{1,0:T(8,128)(2,1)S(1)}, u32[]{:S(2)}, u32[]{:S(2)}) collective-permute-start(bf16[2064,128]{1,0:T(8,128)(2,1)} %get-tuple-element.21), channel_id=1, source_target_pairs={{0,16},{16,32},{32,48},{48,64},{64,80},{80,96},{96,112},{1,17},{17... | collective-permute-start | bytes 1585160 | tf_op jit(solution)/shard_map/ppermute | solution.py:487
  26.9 25.7 %collective-permute-start.1 = (bf16[2064,128]{1,0:T(8,128)(2,1)}, bf16[2064,128]{1,0:T(8,128)(2,1)S(1)}, u32[]{:S(2)}, u32[]{:S(2)}) collective-permute-start(bf16[2064,128]{1,0:T(8,128)(2,1)} %get-tuple-element.22), channel_id=1, source_target_pairs={{16,0},{32,16},{48,32},{64,48},{80,64},{96,80},{112,96},{17,1},{33... | collective-permute-start | bytes 1585160 | tf_op jit(solution)/shard_map/ppermute | solution.py:488
  38.9 15.8 %all-to-all-start.2 = ((bf16[8,3,64,128]{3,2,1,0:T(8,128)(2,1)}), bf16[8,3,64,128]{3,2,1,0:T(8,128)(2,1)S(1)}, u32[]{:S(2)}, u32[]{:S(2)}) async-start(bf16[8,3,64,128]{3,2,1,0:T(8,128)(2,1)} %get-tuple-element.20), calls=%async_computation.2 | async-start | bytes 786432 | tf_op jit(solution)/shard_map/all_to_all | solution.py:490
  46.0 16.1 %collective-permute-start.4 = (bf16[2048,128]{1,0:T(8,128)(2,1)S(1)}, bf16[2048,128]{1,0:T(8,128)(2,1)S(1)}, u32[]{:S(2)}, u32[]{:S(2)}) collective-permute-start(bf16[2048,128]{1,0:T(8,128)(2,1)S(1)} %get-tuple-element.29), channel_id=1, source_target_pairs={{0,1},{1,2},{2,3},{3,4},{4,5},{5,6},{6,7},{7,8},{8,9},{9,10},{10,1... | collective-permute-start | bytes 1572872 | tf_op jit(solution)/shard_map/ppermute | solution.py:485
  48.0 14.1 %collective-permute-start.5 = (bf16[2048,128]{1,0:T(8,128)(2,1)S(1)}, bf16[2048,128]{1,0:T(8,128)(2,1)}, u32[]{:S(2)}, u32[]{:S(2)}) collective-permute-start(bf16[2048,128]{1,0:T(8,128)(2,1)S(1)} %get-tuple-element.30), channel_id=1, source_target_pairs={{1,0},{2,1},{3,2},{4,3},{5,4},{6,5},{7,6},{8,7},{9,8},{10,9},{11,1... | collective-permute-start | bytes 1572872 | tf_op jit(solution)/shard_map/ppermute | solution.py:486
  52.5 14.1 %copy-start = (bf16[2064,128]{1,0:T(8,128)(2,1)}, bf16[2064,128]{1,0:T(8,128)(2,1)S(1)}, u32[]{:S(2)}) copy-start(bf16[2064,128]{1,0:T(8,128)(2,1)S(1)} %collective-permute-done.prev.refs_9_) | copy-start | bytes 1585156
  52.5 14.1 %copy-start.1 = (bf16[2064,128]{1,0:T(8,128)(2,1)}, bf16[2064,128]{1,0:T(8,128)(2,1)S(1)}, u32[]{:S(2)}) copy-start(bf16[2064,128]{1,0:T(8,128)(2,1)S(1)} %collective-permute-done.1.nxt.refs_10_) | copy-start | bytes 1585156
  54.7 32.8 %copy-start.2 = (bf16[16,128,1024]{2,1,0:T(8,128)(2,1)S(1)}, bf16[16,128,1024]{2,1,0:T(8,128)(2,1)}, u32[]{:S(2)}) copy-start(bf16[16,128,1024]{2,1,0:T(8,128)(2,1)} %get-tuple-element.31.k_ref) | copy-start | bytes 12582916
  55.5 9.5 %collective-permute-start.2 = (bf16[1264,128]{1,0:T(8,128)(2,1)S(1)}, bf16[1264,128]{1,0:T(8,128)(2,1)S(1)}, u32[]{:S(2)}, u32[]{:S(2)}) collective-permute-start(bf16[1264,128]{1,0:T(8,128)(2,1)S(1)} %get-tuple-element.26), channel_id=1, source_target_pairs={{0,1},{1,2},{2,3},{3,4},{4,5},{5,6},{6,7},{7,8},{8,9},{9,10},{10,1... | collective-permute-start | bytes 970760 | tf_op jit(solution)/shard_map/ppermute | solution.py:492
  57.5 9.1 %collective-permute-start.3 = (bf16[1264,128]{1,0:T(8,128)(2,1)S(1)}, bf16[1264,128]{1,0:T(8,128)(2,1)S(1)}, u32[]{:S(2)}, u32[]{:S(2)}) collective-permute-start(bf16[1264,128]{1,0:T(8,128)(2,1)S(1)} %get-tuple-element.27), channel_id=1, source_target_pairs={{1,0},{2,1},{3,2},{4,3},{5,4},{6,5},{7,6},{8,7},{9,8},{10,9},{11,1... | collective-permute-start | bytes 970760 | tf_op jit(solution)/shard_map/ppermute | solution.py:493
  62.1 4.6 %copy-start.4 = (bf16[2048,128]{1,0:T(8,128)(2,1)}, bf16[2048,128]{1,0:T(8,128)(2,1)S(1)}, u32[]{:S(2)}) copy-start(bf16[2048,128]{1,0:T(8,128)(2,1)S(1)} %collective-permute-done.4.refs_11_) | copy-start | bytes 1572868
  106.0 4.4 %collective-permute-start.7 = (bf16[192,128]{1,0:T(8,128)(2,1)S(1)}, bf16[192,128]{1,0:T(8,128)(2,1)S(1)}, u32[]{:S(2)}, u32[]{:S(2)}) collective-permute-start(bf16[192,128]{1,0:T(8,128)(2,1)S(1)} %bitcast.6), channel_id=1, source_target_pairs={{1,0},{2,1},{3,2},{4,3},{5,4},{6,5},{7,6},{8,7},{9,8},{10,9},{11,1... | collective-permute-start | bytes 147464 | tf_op jit(solution)/shard_map/ppermute | solution.py:505
  108.2 6.3 %collective-permute-start.6 = (bf16[192,128]{1,0:T(8,128)(2,1)S(1)}, bf16[192,128]{1,0:T(8,128)(2,1)S(1)}, u32[]{:S(2)}, u32[]{:S(2)}) collective-permute-start(bf16[192,128]{1,0:T(8,128)(2,1)S(1)} %bitcast.7), channel_id=1, source_target_pairs={{0,1},{1,2},{2,3},{3,4},{4,5},{5,6},{6,7},{7,8},{8,9},{9,10},{10,1... | collective-permute-start | bytes 147464 | tf_op jit(solution)/shard_map/ppermute | solution.py:504

commit v3 on v2

--- a/solution.py
+++ b/solution.py
@@ -139,6 +139,10 @@
     )(*keep(traces, points, coupling, columns, tiles))
 
 
+def column_of(odd, side):
+    return 3 * odd if side else 3 - 3 * odd
+
+
 def fill_body(tiles, left_out, right_out, sems):
     copies = []
     for out, j in ((left_out, 3), (right_out, 0)):
@@ -163,11 +167,12 @@
     )(*keep(tiles))
 
 
-def near_body(got, prev, nxt, meta, own_out, mid_out, left_out, right_out, meta_out, sems):
+def near_body(parity, got, prev, nxt, meta, own_out, mid_out, out_a, out_b, meta_out, sems):
     copies = []
-    for out, j in ((left_out, 3), (right_out, 0)):
+    for side, out in enumerate((out_a, out_b)):
+        j = column_of(parity[0], side)
         for n, source in enumerate((prev, nxt)):
-            piece = source.at[pl.ds(j * ROWS, ROWS)]
+            piece = source.at[pl.ds(pl.multiple_of(j * ROWS, ROWS), ROWS)]
             copies.append(pltpu.make_async_copy(piece, out.at[pl.ds(HEAD + n * ROWS, ROWS)], sems.at[len(copies)]))
     for n, source in enumerate((prev, nxt)):
         piece = source.at[pl.ds(4 * ROWS, 16)]
@@ -183,25 +188,25 @@
             own_out[...] = total
         value = total.astype(BF)
         mid_out[j * E : j * E + E] = value
-        left_out[j * E : j * E + E] = value
-        right_out[j * E : j * E + E] = value
+        out_a[j * E : j * E + E] = value
+        out_b[j * E : j * E + E] = value
     for copy in copies:
         copy.wait()
     metas = meta_out[...]
-    left_out[TAIL:] = metas
-    right_out[TAIL:] = metas
-
-
-def near(got, prev, nxt, meta):
+    out_a[TAIL:] = metas
+    out_b[TAIL:] = metas
+
+
+def near(parity, got, prev, nxt, meta):
     side = shape((TAIL + 48, S), BF)
     return call(
         near_body,
         (shape((E, U), F32), shape((HEAD, U), BF), side, side, shape((48, U), BF)),
         moved=2 * MB,
-        in_specs=[IN_VMEM, IN_ANY, IN_ANY, IN_VMEM],
+        in_specs=[IN_SMEM, IN_VMEM, IN_ANY, IN_ANY, IN_VMEM],
         out_specs=(IN_VMEM,) * 5,
         scratch_shapes=[pltpu.SemaphoreType.DMA((6,))],
-    )(got, prev, nxt, meta)
+    )(parity, got, prev, nxt, meta)
 
 
 def write_partials(acc, out):
@@ -310,7 +315,7 @@
     return ((0, 2), (1, 3)) if b == 0 else ((6, 0), (7, 1)) if b == 2 else tuple((2 + i, i) for i in range(4))
 
 
-def sweep_body(last, own_ref, mid, left, right, left_far, right_far, inc, mid_metas, tiles_h, prev_h, nxt_h, lefts_h, rights_h, *rest):
+def sweep_body(last, parity, own_ref, mid, near_a, near_b, far_a, far_b, inc, mid_metas, tiles_h, prev_h, nxt_h, lefts_h, rights_h, *rest):
     if last:
         present_out, field_out = rest[:2]
     else:
@@ -319,13 +324,16 @@
     loads = [(moves_v, moves), (tiles_h, tiles)]
     loads += [(h.at[pl.ds(0, 4 * ROWS)], v) for h, v in ((prev_h, prev), (nxt_h, nxt))]
     loads += [(lefts_h, lefts), (rights_h, rights)]
+    odd = parity[0]
+    partners = ((6 - 6 * odd, 2 * odd, 6 - 5 * odd, 3 * odd), (6 * odd, 2 - 2 * odd, 1 + 5 * odd, 3 - 3 * odd))
     loads = [pltpu.make_async_copy(a, b, sems.at[n]) for n, (a, b) in enumerate(loads)]
     for copy in loads[1:]:
         copy.start()
 
     def meta(br, bc):
-        m = mid_metas[16 * br : 16 * br + 16] if bc == 1 else (left_far, right_far)[bc // 2][TAIL + 16 * br : TAIL + 16 * br + 16]
-        return m.astype(F32)
+        if bc == 1:
+            return mid_metas[16 * br : 16 * br + 16].astype(F32)
+        return (far_a, far_b)[bc // 2][TAIL + 16 * br : TAIL + 16 * br + 16].astype(F32)
 
     moves_v[...] = jnp.zeros_like(moves_v)
     for br in range(3):
@@ -341,12 +349,14 @@
         return m[0:1], jnp.where(m[1:2] == line, 1.0, 0.0).astype(BF)
 
     def masked(c, hi, ids):
-        return jnp.concatenate([c * jnp.where(hi == float(t), 1.0, 0.0).astype(BF) for t in ids], axis=0)
+        ids = [t.astype(F32) if isinstance(t, jax.Array) else float(t) for t in ids]
+        return jnp.concatenate([c * jnp.where(hi == t, 1.0, 0.0).astype(BF) for t in ids], axis=0)
 
     def place(br, bc):
         hi, lo = coupling(br, bc)
-        c = (left, mid, right)[bc][br * E : br * E + E]
-        places = [(R * 8 + C, i * 4 + j) for R, i in span(br) for C, j in span(bc)]
+        c = (near_a, mid, near_b)[bc][br * E : br * E + E]
+        C, j = (2, 0) if bc == 1 else partners[bc // 2][:2]
+        places = [(R * 8 + C + n, i * 4 + j + n) for R, i in span(br) for n in range(4 if bc == 1 else 2)]
         out = dot(masked(c, hi, [t for _, t in places]), lo, NT).astype(BF)
         for n, (w, _) in enumerate(places):
             src[w] = out[n * E : n * E + E]
@@ -373,7 +383,7 @@
         for h in range(2):
             ks = (2 * h, 2 * h + 1)
             x = jnp.concatenate([values[base + moves[block, tile * 4 + k]] for k in ks], axis=1)
-            a = [ref[pl.ds(pl.multiple_of(start + k * S, 64), S), :] for k in ks]
+            a = [ref[start + k * S : start + k * S + S, :] for k in ks]
             y = dot(x, jnp.concatenate(a, axis=1), NT)
             total = y if total is None else total + y
         return total
@@ -384,7 +394,8 @@
         f1[w] = (srcf[t] + apply(src, w - 9, 4, t, tiles, t * ROWS)).astype(BF)
         return carry
 
-    lax.fori_loop(0, 16, own_tile, 0, unroll=4)
+    for t in range(16):
+        own_tile(t, 0)
     for copy in loads[2:]:
         copy.wait()
 
@@ -397,19 +408,20 @@
         halo(48 + 2 + j, 7, j, nxt, j * 4 * S)
         return carry
 
-    lax.fori_loop(0, 4, edge_row, 0)
+    for j in range(4):
+        edge_row(j, 0)
 
     def edge_col(i, carry):
         w = (2 + i) * 8
-        halo(w + 1, 3, i * 4 + 3, lefts, i * ROWS)
-        halo(w + 6, 5, i * 4, rights, i * ROWS)
+        halo(w + 1, 5 - 2 * odd, i * 4 + 3, lefts, i * ROWS)
+        halo(w + 6, 3 + 2 * odd, i * 4, rights, i * ROWS)
         return carry
 
-    lax.fori_loop(0, 4, edge_col, 0)
-    halo(9, 0, 15, left_far, HEAD)
-    halo(14, 2, 12, right_far, HEAD)
-    halo(49, 6, 3, left_far, HEAD + ROWS)
-    halo(54, 8, 0, right_far, HEAD + ROWS)
+    for i in range(4):
+        edge_col(i, 0)
+    for n, ref in enumerate((far_a, far_b)):
+        halo(8 + partners[n][2], 2 * n, 12 + partners[n][3], ref, HEAD)
+        halo(48 + partners[n][2], 6 + 2 * n, partners[n][3], ref, HEAD + ROWS)
 
     def final_tile(t, carry):
         i, j = t // 4, t % 4
@@ -422,7 +434,8 @@
         fields[t, :, S:] = (field - a.astype(F32)).astype(BF)
         return carry
 
-    lax.fori_loop(0, 16, final_tile, 0, unroll=4)
+    for t in range(16):
+        final_tile(t, 0)
     y = dot(fields[...].reshape(16 * E, 2 * S), jnp.concatenate([lo, lo], axis=0))
     read = jnp.zeros((E, U), F32)
     for t in range(16):
@@ -449,7 +462,7 @@
         out,
         flops=2 * E * S * S * 4 * 52,
         moved=6 * MB,
-        in_specs=[IN_VMEM] * 8 + [IN_HBM] * 5,
+        in_specs=[IN_SMEM] + [IN_VMEM] * 8 + [IN_HBM] * 5,
         out_specs=(IN_VMEM, IN_VMEM) if last else IN_VMEM,
         scratch_shapes=[
             pltpu.VMEM((64, E, S), BF),
@@ -465,7 +478,7 @@
             pltpu.SMEM((16, U), jnp.int32),
             pltpu.SemaphoreType.DMA((6,)),
         ],
-    )(*args[:8], *keep(*args[8:]))
+    )(*args[:9], *keep(*args[9:]))
 
 
 def shift(axis):
@@ -477,6 +490,9 @@
 def per_device(traces, incident, points, coupling, volume_tiles, tile_columns):
     row_up, row_down = shift("row")
     col_up, col_down = shift("col")
+    parity = (lax.axis_index("col") % 2).reshape(1)
+    swap_a = [(c, c ^ 1) for c in range(NC)]
+    swap_b = [(c, ((c - 1) ^ 1) + 1) for c in range(1, NC - 1)]
     tiles = volume_tiles.reshape(16 * ROWS, S)
     rows, cols, up, down, meta = pack(traces, points, coupling.reshape(1, U), tile_columns, tiles)
     rows = lax.all_to_all(rows, "row", 0, 0, tiled=True)
@@ -488,21 +504,21 @@
     nxt = lax.ppermute(down, "row", row_down)
     kernel, partials = make_kernel(cols, rows)
     got = lax.all_to_all(partials, "row", 0, 0, tiled=True)
-    own, mid, to_right, to_left, metas = near(got, prev, nxt, meta)
-    left = lax.ppermute(to_right, "col", col_up)
-    right = lax.ppermute(to_left, "col", col_down)
-    far = (left, right)
+    own, mid, near_a, near_b, metas = near(parity, got, prev, nxt, meta)
+    near_a = lax.ppermute(near_a, "col", swap_a)
+    near_b = lax.ppermute(near_b, "col", swap_b)
+    far = (near_a, near_b)
     for outer in range(2):
         last = outer == 1
-        out = sweep(last, own, mid, left, right, *far, incident, metas, tiles, prev, nxt, lefts, rights)
+        out = sweep(last, parity, own, mid, near_a, near_b, *far, incident, metas, tiles, prev, nxt, lefts, rights)
         if not last:
             out = lax.all_to_all(out, "col", 0, 0, tiled=True)
             partials = product(out, kernel)
             got = lax.all_to_all(partials, "row", 0, 0, tiled=True)
             sums = jnp.sum(got.astype(F32), axis=0)
             own, mid = sums[1], sums.astype(BF).reshape(HEAD, U)
-            left = lax.ppermute(mid, "col", col_up)
-            right = lax.ppermute(mid, "col", col_down)
+            near_a = lax.ppermute(mid, "col", swap_a)
+            near_b = lax.ppermute(mid, "col", swap_b)
     present, field = out
     return present, field.reshape(E, 4, 4, S)
 

time: 123 us -> 118 us (0.959)
  starting transfers between devices: 32.6 us -> 27.7 us
  Pallas kernels: 28.2 us -> 24.9 us
  blocking collectives: 47.2 us -> 48.8 us
    ppermute x4, starting transfers between devices: 10.9 us -> 6.06 us  [the longest x1 3.63 us: per_device(): near_b = lax.ppermute(near_b, 'col', swap_b)]
    pallas_call x2, Pallas kernels: 14.2 us -> 10.9 us  [sweep(): call(body, out, flops=2 * E * S * S * 4 * 52, moved=6 * MB, in_specs=[IN_...]
    all_to_all x1, blocking collectives: 14 us -> 15.6 us  [per_device(): out = lax.all_to_all(out, 'col', 0, 0, tiled=True)]
  transfers between devices with their start and end apart: 10 -> 10, of which waited for: 5 -> 4; matrix products, arithmetic and copies ran while one was open for 0% -> 0% of each run, Pallas kernels for 9% -> 9%
where the time goes in v3:
time: 118 us; the launch traced here: 116 us
  blocking collectives  48.8 us (41%)
  starting transfers between devices  27.7 us (23%)
  Pallas kernels  24.9 us (21%)
  waiting for transfers between devices  14 us (12%)
    all_to_all x1, blocking collectives, per_device(): got = lax.all_to_all(partials, 'row', 0, 0, tiled=True)  17.5 us
    all_to_all x1, blocking collectives, per_device(): rows = lax.all_to_all(rows, 'row', 0, 0, tiled=True)  15.7 us
    all_to_all x1, blocking collectives, per_device(): out = lax.all_to_all(out, 'col', 0, 0, tiled=True)  15.6 us
    pallas_call x2, Pallas kernels, sweep(): call(body, out, flops=2 * E * S * S * 4 * 52, moved=6 * MB, in_specs=[IN_...  10.9 us
    pallas_call x1, Pallas kernels, make_kernel(): call(kernel_body, (hbm((NC, U, NR * U), BF), hbm((NR, 3, E, U), BF)), flo...  8.6 us
    ppermute x1, waiting for transfers between devices, per_device(): near_b = lax.ppermute(near_b, 'col', swap_b)  5.81 us
    all_to_all x1, starting transfers between devices, per_device(): got = lax.all_to_all(partials, 'row', 0, 0, tiled=True)  5.77 us
    all_to_all x1, starting transfers between devices, per_device(): cols = lax.all_to_all(cols, 'col', 0, 0, tiled=True)  5.39 us
  transfers between devices with their start and end apart: 10, of which 4 were waited for; matrix products, arithmetic and copies ran while one was open for 0% of the time, Pallas kernels for 9%

profile of v3, /device:TPU:8, one launch (start us, length us, event | category | flops | bytes accessed | tf_op | source)
XLA Modules:
  0.0 116.3 jit_solution(181515518197233095)
XLA Ops:
  0.6 2.4 %shard_map.77 = (bf16[8,48,128]{2,1,0:T(8,128)(2,1)}, bf16[16,80,128]{2,1,0:T(8,128)(2,1)}, bf16[2064,128]{1,0:T(8,128)(2,1)}, bf16[2064,128]{1,0:T(8,128)(2,1)}, bf16[16,128]{1,0:T(8,128)(2,1)S(1)}) custom-call(bf16[64,128]{1,0:T(8,128)(2,1)} %traces_h.1, f32[3,128]{1,0:T(4,128)} %points_h.1, s32[1,128]{1,0:T(1,128)} %bitcast.14, s32[4,4,4]{2,1,0:T(4,128)} %columns_h.1, ...), custom_call_target="tpu_custom_call" | custom-call | tf_op jit(solution)/shard_map/pallas_call | solution.py:127
  3.1 15.7 %all_to_all.25.row_ref = bf16[8,48,128]{2,1,0:T(8,128)(2,1)} all-to-all(bf16[8,48,128]{2,1,0:T(8,128)(2,1)} %get-tuple-element.19), channel_id=1, replica_groups=mesh['row'=8,'col'=16] {'row'}, dimensions={0} | all-to-all | bytes 196608 | tf_op jit(solution)/shard_map/all_to_all | solution.py:498
  18.7 5.4 %all-to-all-start = ((bf16[16,80,128]{2,1,0:T(8,128)(2,1)}), bf16[16,80,128]{2,1,0:T(8,128)(2,1)S(1)}, u32[]{:S(2)}, u32[]{:S(2)}) async-start(bf16[16,80,128]{2,1,0:T(8,128)(2,1)} %get-tuple-element.18), calls=%async_computation | async-start | bytes 655360 | tf_op jit(solution)/shard_map/all_to_all | solution.py:499
  24.1 2.8 %collective-permute-start = (bf16[2064,128]{1,0:T(8,128)(2,1)}, bf16[2064,128]{1,0:T(8,128)(2,1)S(1)}, u32[]{:S(2)}, u32[]{:S(2)}) collective-permute-start(bf16[2064,128]{1,0:T(8,128)(2,1)} %get-tuple-element.21), channel_id=1, source_target_pairs={{0,16},{16,32},{32,48},{48,64},{64,80},{80,96},{96,112},{1,17},{17... | collective-permute-start | bytes 1585160 | tf_op jit(solution)/shard_map/ppermute | solution.py:503
  26.9 1.3 %collective-permute-start.1 = (bf16[2064,128]{1,0:T(8,128)(2,1)}, bf16[2064,128]{1,0:T(8,128)(2,1)S(1)}, u32[]{:S(2)}, u32[]{:S(2)}) collective-permute-start(bf16[2064,128]{1,0:T(8,128)(2,1)} %get-tuple-element.22), channel_id=1, source_target_pairs={{16,0},{32,16},{48,32},{64,48},{80,64},{96,80},{112,96},{17,1},{33... | collective-permute-start | bytes 1585160 | tf_op jit(solution)/shard_map/ppermute | solution.py:504
  28.2 2.1 %all-to-all-done.col_ref = bf16[16,80,128]{2,1,0:T(8,128)(2,1)S(1)} async-done(((bf16[16,80,128]{2,1,0:T(8,128)(2,1)}), bf16[16,80,128]{2,1,0:T(8,128)(2,1)S(1)}, u32[]{:S(2)}, u32[]{:S(2)}) %all-to-all-start) | async-done | bytes 327712 | tf_op jit(solution)/shard_map/all_to_all | solution.py:499
  30.3 8.6 %shard_map.78 = (bf16[16,128,1024]{2,1,0:T(8,128)(2,1)}, bf16[8,3,64,128]{3,2,1,0:T(8,128)(2,1)}) custom-call(bf16[16,80,128]{2,1,0:T(8,128)(2,1)S(1)} %all-to-all-done.col_ref, bf16[8,48,128]{2,1,0:T(8,128)(2,1)} %all_to_all.25.row_ref), custom_call_target="tpu_custom_call" | custom-call | flops 83886080 | bytes 6291456 | tf_op jit(solution)/shard_map/pallas_call | solution.py:275
  38.9 5.8 %all-to-all-start.2 = ((bf16[8,3,64,128]{3,2,1,0:T(8,128)(2,1)}), bf16[8,3,64,128]{3,2,1,0:T(8,128)(2,1)S(1)}, u32[]{:S(2)}, u32[]{:S(2)}) async-start(bf16[8,3,64,128]{3,2,1,0:T(8,128)(2,1)} %get-tuple-element.20), calls=%async_computation.2 | async-start | bytes 786432 | tf_op jit(solution)/shard_map/all_to_all | solution.py:506
  44.7 1.3 %shard_map.80 = (bf16[2048,128]{1,0:T(8,128)(2,1)S(1)}, bf16[2048,128]{1,0:T(8,128)(2,1)S(1)}) custom-call(bf16[8192,128]{1,0:T(8,128)(2,1)} %bitcast.11), custom_call_target="tpu_custom_call" | custom-call | bytes 2097152 | tf_op jit(solution)/shard_map/pallas_call | solution.py:160
  46.0 1.9 %collective-permute-start.4 = (bf16[2048,128]{1,0:T(8,128)(2,1)S(1)}, bf16[2048,128]{1,0:T(8,128)(2,1)S(1)}, u32[]{:S(2)}, u32[]{:S(2)}) collective-permute-start(bf16[2048,128]{1,0:T(8,128)(2,1)S(1)} %get-tuple-element.29), channel_id=1, source_target_pairs={{0,1},{1,2},{2,3},{3,4},{4,5},{5,6},{6,7},{7,8},{8,9},{9,10},{10,1... | collective-permute-start | bytes 1572872 | tf_op jit(solution)/shard_map/ppermute | solution.py:501
  47.9 4.5 %collective-permute-start.5 = (bf16[2048,128]{1,0:T(8,128)(2,1)S(1)}, bf16[2048,128]{1,0:T(8,128)(2,1)}, u32[]{:S(2)}, u32[]{:S(2)}) collective-permute-start(bf16[2048,128]{1,0:T(8,128)(2,1)S(1)} %get-tuple-element.30), channel_id=1, source_target_pairs={{1,0},{2,1},{3,2},{4,3},{5,4},{6,5},{7,6},{8,7},{9,8},{10,9},{11,1... | collective-permute-start | bytes 1572872 | tf_op jit(solution)/shard_map/ppermute | solution.py:502
  52.5 2.1 %all-to-all-done.2.got = bf16[8,3,64,128]{3,2,1,0:T(8,128)(2,1)S(1)} async-done(((bf16[8,3,64,128]{3,2,1,0:T(8,128)(2,1)}), bf16[8,3,64,128]{3,2,1,0:T(8,128)(2,1)S(1)}, u32[]{:S(2)}, u32[]{:S(2)}) %all-to-all-start.2) | async-done | bytes 393248 | tf_op jit(solution)/shard_map/all_to_all | solution.py:506
  54.7 0.8 shard_map.79
  55.5 0.1 collective-permute-start.2
  55.6 3.6 %collective-permute-start.3 = (bf16[1264,128]{1,0:T(8,128)(2,1)S(1)}, bf16[1264,128]{1,0:T(8,128)(2,1)S(1)}, u32[]{:S(2)}, u32[]{:S(2)}) collective-permute-start(bf16[1264,128]{1,0:T(8,128)(2,1)S(1)} %get-tuple-element.27), channel_id=1, source_target_pairs={{1,2},{2,1},{3,4},{4,3},{5,6},{6,5},{7,8},{8,7},{9,10},{10,9},{11,... | collective-permute-start | bytes 970760 | tf_op jit(solution)/shard_map/ppermute | solution.py:509
  59.2 5.8 %collective-permute-done.3.refs_4_.refs_6_ = bf16[1264,128]{1,0:T(8,128)(2,1)S(1)} collective-permute-done((bf16[1264,128]{1,0:T(8,128)(2,1)S(1)}, bf16[1264,128]{1,0:T(8,128)(2,1)S(1)}, u32[]{:S(2)}, u32[]{:S(2)}) %collective-permute-start.3) | collective-permute-done | bytes 323616 | tf_op jit(solution)/shard_map/ppermute | solution.py:509
  65.1 5.1 %shard_map.81 = bf16[16,64,128]{2,1,0:T(8,128)(2,1)S(1)} custom-call(s32[1]{0:T(128)} %bitcast.parity.refs_0_, f32[64,128]{1,0:T(8,128)S(1)} %get-tuple-element.24.refs_1_, bf16[192,128]{1,0:T(8,128)(2,1)S(1)} %get-tuple-element.25.refs_2_, bf16[1264,128]{1,0:T(8,128)(2,1)S(1)} %collective-permute-done.2.refs_3_.refs_5_, ...), custom_call_target="tpu_custom_call" | custom-call | flops 436207616 | bytes 6291456 | tf_op jit(solution)/shard_map/pallas_call | solution.py:460
  70.2 15.6 %all_to_all.26.p_ref = bf16[16,64,128]{2,1,0:T(8,128)(2,1)S(1)} all-to-all(bf16[16,64,128]{2,1,0:T(8,128)(2,1)S(1)} %shard_map.81), channel_id=1, replica_groups=mesh['row'=8,'col'=16] {'col'}, dimensions={0} | all-to-all | bytes 524288 | tf_op jit(solution)/shard_map/all_to_all | solution.py:515
  85.8 0.8 shard_map.82
  86.7 17.5 %all_to_all.27 = bf16[8,3,64,128]{3,2,1,0:T(8,128)(2,1)S(1)} all-to-all(bf16[8,3,64,128]{3,2,1,0:T(8,128)(2,1)S(1)} %shard_map.82), channel_id=1, replica_groups=mesh['row'=8,'col'=16] {'row'}, dimensions={0} | all-to-all | bytes 786432 | tf_op jit(solution)/shard_map/all_to_all | solution.py:517
  104.2 2.3 %collective-permute-start.7 = (bf16[192,128]{1,0:T(8,128)(2,1)S(1)}, bf16[192,128]{1,0:T(8,128)(2,1)S(1)}, u32[]{:S(2)}, u32[]{:S(2)}) collective-permute-start(bf16[192,128]{1,0:T(8,128)(2,1)S(1)} %bitcast.7), channel_id=1, source_target_pairs={{1,2},{2,1},{3,4},{4,3},{5,6},{6,5},{7,8},{8,7},{9,10},{10,9},{11,... | collective-permute-start | bytes 147464 | tf_op jit(solution)/shard_map/ppermute | solution.py:521
  106.5 0.1 collective-permute-start.6
  106.6 3.9 %collective-permute-done.7.refs_4_ = bf16[192,128]{1,0:T(8,128)(2,1)S(1)} collective-permute-done((bf16[192,128]{1,0:T(8,128)(2,1)S(1)}, bf16[192,128]{1,0:T(8,128)(2,1)S(1)}, u32[]{:S(2)}, u32[]{:S(2)}) %collective-permute-start.7) | collective-permute-done | bytes 49184 | tf_op jit(solution)/shard_map/ppermute | solution.py:521
  110.6 5.8 %shard_map.83 = (bf16[64,128]{1,0:T(8,128)(2,1)}, f32[1024,128]{1,0:T(8,128)}) custom-call(s32[1]{0:T(128)} %bitcast.parity.refs_0_, f32[64,128]{1,0:T(8,128)S(1)} %slice_bitcast_fusion.refs_1_, bf16[192,128]{1,0:T(8,128)(2,1)S(1)} %bitcast.9, bf16[192,128]{1,0:T(8,128)(2,1)S(1)} %collective-permute-done.6.refs_3_, ...), custom_call_target="tpu_custom_call" | custom-call | flops 436207616 | bytes 6291456 | tf_op jit(solution)/shard_map/pallas_call | solution.py:460
  (19 shorter events, 0.1 us)
Async XLA Ops:
  0.6 64.4 %copy-start.3 = (bf16[64,128]{1,0:T(8,128)(2,1)S(1)}, bf16[64,128]{1,0:T(8,128)(2,1)}, u32[]{:S(2)}) copy-start(bf16[64,128]{1,0:T(8,128)(2,1)} %refs_7_.3) | copy-start | bytes 49156
  18.7 11.5 %all-to-all-start = ((bf16[16,80,128]{2,1,0:T(8,128)(2,1)}), bf16[16,80,128]{2,1,0:T(8,128)(2,1)S(1)}, u32[]{:S(2)}, u32[]{:S(2)}) async-start(bf16[16,80,128]{2,1,0:T(8,128)(2,1)} %get-tuple-element.18), calls=%async_computation | async-start | bytes 655360 | tf_op jit(solution)/shard_map/all_to_all | solution.py:499
  24.1 28.4 %collective-permute-start = (bf16[2064,128]{1,0:T(8,128)(2,1)}, bf16[2064,128]{1,0:T(8,128)(2,1)S(1)}, u32[]{:S(2)}, u32[]{:S(2)}) collective-permute-start(bf16[2064,128]{1,0:T(8,128)(2,1)} %get-tuple-element.21), channel_id=1, source_target_pairs={{0,16},{16,32},{32,48},{48,64},{64,80},{80,96},{96,112},{1,17},{17... | collective-permute-start | bytes 1585160 | tf_op jit(solution)/shard_map/ppermute | solution.py:503
  26.9 25.6 %collective-permute-start.1 = (bf16[2064,128]{1,0:T(8,128)(2,1)}, bf16[2064,128]{1,0:T(8,128)(2,1)S(1)}, u32[]{:S(2)}, u32[]{:S(2)}) collective-permute-start(bf16[2064,128]{1,0:T(8,128)(2,1)} %get-tuple-element.22), channel_id=1, source_target_pairs={{16,0},{32,16},{48,32},{64,48},{80,64},{96,80},{112,96},{17,1},{33... | collective-permute-start | bytes 1585160 | tf_op jit(solution)/shard_map/ppermute | solution.py:504
  38.9 15.8 %all-to-all-start.2 = ((bf16[8,3,64,128]{3,2,1,0:T(8,128)(2,1)}), bf16[8,3,64,128]{3,2,1,0:T(8,128)(2,1)S(1)}, u32[]{:S(2)}, u32[]{:S(2)}) async-start(bf16[8,3,64,128]{3,2,1,0:T(8,128)(2,1)} %get-tuple-element.20), calls=%async_computation.2 | async-start | bytes 786432 | tf_op jit(solution)/shard_map/all_to_all | solution.py:506
  46.0 13.2 %collective-permute-start.4 = (bf16[2048,128]{1,0:T(8,128)(2,1)S(1)}, bf16[2048,128]{1,0:T(8,128)(2,1)S(1)}, u32[]{:S(2)}, u32[]{:S(2)}) collective-permute-start(bf16[2048,128]{1,0:T(8,128)(2,1)S(1)} %get-tuple-element.29), channel_id=1, source_target_pairs={{0,1},{1,2},{2,3},{3,4},{4,5},{5,6},{6,7},{7,8},{8,9},{9,10},{10,1... | collective-permute-start | bytes 1572872 | tf_op jit(solution)/shard_map/ppermute | solution.py:501
  47.9 11.3 %collective-permute-start.5 = (bf16[2048,128]{1,0:T(8,128)(2,1)S(1)}, bf16[2048,128]{1,0:T(8,128)(2,1)}, u32[]{:S(2)}, u32[]{:S(2)}) collective-permute-start(bf16[2048,128]{1,0:T(8,128)(2,1)S(1)} %get-tuple-element.30), channel_id=1, source_target_pairs={{1,0},{2,1},{3,2},{4,3},{5,4},{6,5},{7,6},{8,7},{9,8},{10,9},{11,1... | collective-permute-start | bytes 1572872 | tf_op jit(solution)/shard_map/ppermute | solution.py:502
  52.5 12.5 %copy-start = (bf16[2064,128]{1,0:T(8,128)(2,1)}, bf16[2064,128]{1,0:T(8,128)(2,1)S(1)}, u32[]{:S(2)}) copy-start(bf16[2064,128]{1,0:T(8,128)(2,1)S(1)} %collective-permute-done.prev.refs_10_) | copy-start | bytes 1585156
  52.5 12.5 %copy-start.1 = (bf16[2064,128]{1,0:T(8,128)(2,1)}, bf16[2064,128]{1,0:T(8,128)(2,1)S(1)}, u32[]{:S(2)}) copy-start(bf16[2064,128]{1,0:T(8,128)(2,1)S(1)} %collective-permute-done.1.nxt.refs_11_) | copy-start | bytes 1585156
  54.7 31.1 %copy-start.2 = (bf16[16,128,1024]{2,1,0:T(8,128)(2,1)S(1)}, bf16[16,128,1024]{2,1,0:T(8,128)(2,1)}, u32[]{:S(2)}) copy-start(bf16[16,128,1024]{2,1,0:T(8,128)(2,1)} %get-tuple-element.31.k_ref) | copy-start | bytes 12582916
  55.5 3.8 %collective-permute-start.2 = (bf16[1264,128]{1,0:T(8,128)(2,1)S(1)}, bf16[1264,128]{1,0:T(8,128)(2,1)S(1)}, u32[]{:S(2)}, u32[]{:S(2)}) collective-permute-start(bf16[1264,128]{1,0:T(8,128)(2,1)S(1)} %get-tuple-element.26), channel_id=1, source_target_pairs={{0,1},{1,0},{2,3},{3,2},{4,5},{5,4},{6,7},{7,6},{8,9},{9,8},{10,11... | collective-permute-start | bytes 970760 | tf_op jit(solution)/shard_map/ppermute | solution.py:508
  55.6 9.5 %collective-permute-start.3 = (bf16[1264,128]{1,0:T(8,128)(2,1)S(1)}, bf16[1264,128]{1,0:T(8,128)(2,1)S(1)}, u32[]{:S(2)}, u32[]{:S(2)}) collective-permute-start(bf16[1264,128]{1,0:T(8,128)(2,1)S(1)} %get-tuple-element.27), channel_id=1, source_target_pairs={{1,2},{2,1},{3,4},{4,3},{5,6},{6,5},{7,8},{8,7},{9,10},{10,9},{11,... | collective-permute-start | bytes 970760 | tf_op jit(solution)/shard_map/ppermute | solution.py:509
  59.2 5.8 %copy-start.4 = (bf16[2048,128]{1,0:T(8,128)(2,1)}, bf16[2048,128]{1,0:T(8,128)(2,1)S(1)}, u32[]{:S(2)}) copy-start(bf16[2048,128]{1,0:T(8,128)(2,1)S(1)} %collective-permute-done.4.refs_12_) | copy-start | bytes 1572868
  104.2 6.3 %collective-permute-start.7 = (bf16[192,128]{1,0:T(8,128)(2,1)S(1)}, bf16[192,128]{1,0:T(8,128)(2,1)S(1)}, u32[]{:S(2)}, u32[]{:S(2)}) collective-permute-start(bf16[192,128]{1,0:T(8,128)(2,1)S(1)} %bitcast.7), channel_id=1, source_target_pairs={{1,2},{2,1},{3,4},{4,3},{5,6},{6,5},{7,8},{8,7},{9,10},{10,9},{11,... | collective-permute-start | bytes 147464 | tf_op jit(solution)/shard_map/ppermute | solution.py:521
  106.5 4.0 %collective-permute-start.6 = (bf16[192,128]{1,0:T(8,128)(2,1)S(1)}, bf16[192,128]{1,0:T(8,128)(2,1)S(1)}, u32[]{:S(2)}, u32[]{:S(2)}) collective-permute-start(bf16[192,128]{1,0:T(8,128)(2,1)S(1)} %bitcast.8), channel_id=1, source_target_pairs={{0,1},{1,0},{2,3},{3,2},{4,5},{5,4},{6,7},{7,6},{8,9},{9,8},{10,11... | collective-permute-start | bytes 147464 | tf_op jit(solution)/shard_map/ppermute | solution.py:520

commit v4 on v3

--- a/solution.py
+++ b/solution.py
@@ -14,7 +14,7 @@
 MB = 1 << 20
 HEAD = 3 * E
 ROWS = 4 * S
-TAIL = HEAD + 2 * ROWS
+TAIL = 2 * ROWS
 BF, F32 = jnp.bfloat16, jnp.float32
 SIN = (3.14158202, -5.1671428, 2.54189903, -0.55463619)
 NT = (((1,), (1,)), ((), ()))
@@ -167,46 +167,57 @@
     )(*keep(tiles))
 
 
-def near_body(parity, got, prev, nxt, meta, own_out, mid_out, out_a, out_b, meta_out, sems):
+def corner_body(parity, prev, nxt, meta, out_a, out_b, meta_out, sems):
     copies = []
     for side, out in enumerate((out_a, out_b)):
         j = column_of(parity[0], side)
         for n, source in enumerate((prev, nxt)):
             piece = source.at[pl.ds(pl.multiple_of(j * ROWS, ROWS), ROWS)]
-            copies.append(pltpu.make_async_copy(piece, out.at[pl.ds(HEAD + n * ROWS, ROWS)], sems.at[len(copies)]))
+            copies.append(pltpu.make_async_copy(piece, out.at[pl.ds(n * ROWS, ROWS)], sems.at[len(copies)]))
     for n, source in enumerate((prev, nxt)):
         piece = source.at[pl.ds(4 * ROWS, 16)]
         copies.append(pltpu.make_async_copy(piece, meta_out.at[pl.ds(32 * n, 16)], sems.at[len(copies)]))
     for copy in copies:
         copy.start()
     meta_out[16:32] = meta[...]
+    for copy in copies[4:]:
+        copy.wait()
+    metas = meta_out[...]
+    out_a[TAIL:] = metas
+    out_b[TAIL:] = metas
+    for copy in copies[:4]:
+        copy.wait()
+
+
+def corners(parity, prev, nxt, meta):
+    side = shape((TAIL + 48, S), BF)
+    return call(
+        corner_body,
+        (side, side, shape((48, U), BF)),
+        moved=2 * MB,
+        in_specs=[IN_SMEM, IN_ANY, IN_ANY, IN_VMEM],
+        out_specs=(IN_VMEM,) * 3,
+        scratch_shapes=[pltpu.SemaphoreType.DMA((6,))],
+    )(parity, prev, nxt, meta)
+
+
+def near_body(got, own_out, mid_out):
     for j in range(3):
         total = got[0, j].astype(F32)
         for r in range(1, NR):
             total += got[r, j].astype(F32)
         if j == 1:
             own_out[...] = total
-        value = total.astype(BF)
-        mid_out[j * E : j * E + E] = value
-        out_a[j * E : j * E + E] = value
-        out_b[j * E : j * E + E] = value
-    for copy in copies:
-        copy.wait()
-    metas = meta_out[...]
-    out_a[TAIL:] = metas
-    out_b[TAIL:] = metas
-
-
-def near(parity, got, prev, nxt, meta):
-    side = shape((TAIL + 48, S), BF)
+        mid_out[j * E : j * E + E] = total.astype(BF)
+
+
+def near(got):
     return call(
         near_body,
-        (shape((E, U), F32), shape((HEAD, U), BF), side, side, shape((48, U), BF)),
-        moved=2 * MB,
-        in_specs=[IN_SMEM, IN_VMEM, IN_ANY, IN_ANY, IN_VMEM],
-        out_specs=(IN_VMEM,) * 5,
-        scratch_shapes=[pltpu.SemaphoreType.DMA((6,))],
-    )(parity, got, prev, nxt, meta)
+        (shape((E, U), F32), shape((HEAD, U), BF)),
+        in_specs=[IN_VMEM],
+        out_specs=(IN_VMEM,) * 2,
+    )(got)
 
 
 def write_partials(acc, out):
@@ -420,8 +431,8 @@
     for i in range(4):
         edge_col(i, 0)
     for n, ref in enumerate((far_a, far_b)):
-        halo(8 + partners[n][2], 2 * n, 12 + partners[n][3], ref, HEAD)
-        halo(48 + partners[n][2], 6 + 2 * n, partners[n][3], ref, HEAD + ROWS)
+        halo(8 + partners[n][2], 2 * n, 12 + partners[n][3], ref, 0)
+        halo(48 + partners[n][2], 6 + 2 * n, partners[n][3], ref, ROWS)
 
     def final_tile(t, carry):
         i, j = t // 4, t % 4
@@ -504,21 +515,21 @@
     nxt = lax.ppermute(down, "row", row_down)
     kernel, partials = make_kernel(cols, rows)
     got = lax.all_to_all(partials, "row", 0, 0, tiled=True)
-    own, mid, near_a, near_b, metas = near(parity, got, prev, nxt, meta)
-    near_a = lax.ppermute(near_a, "col", swap_a)
-    near_b = lax.ppermute(near_b, "col", swap_b)
-    far = (near_a, near_b)
+    far_a, far_b, metas = corners(parity, prev, nxt, meta)
+    far_a = lax.ppermute(far_a, "col", swap_a)
+    far_b = lax.ppermute(far_b, "col", swap_b)
     for outer in range(2):
         last = outer == 1
-        out = sweep(last, parity, own, mid, near_a, near_b, *far, incident, metas, tiles, prev, nxt, lefts, rights)
+        own, mid = near(got)
+        near_a = lax.ppermute(mid, "col", swap_a)
+        near_b = lax.ppermute(mid, "col", swap_b)
+        out = sweep(
+            last, parity, own, mid, near_a, near_b, far_a, far_b, incident, metas, tiles, prev, nxt, lefts, rights
+        )
         if not last:
             out = lax.all_to_all(out, "col", 0, 0, tiled=True)
             partials = product(out, kernel)
             got = lax.all_to_all(partials, "row", 0, 0, tiled=True)
-            sums = jnp.sum(got.astype(F32), axis=0)
-            own, mid = sums[1], sums.astype(BF).reshape(HEAD, U)
-            near_a = lax.ppermute(mid, "col", swap_a)
-            near_b = lax.ppermute(mid, "col", swap_b)
     present, field = out
     return present, field.reshape(E, 4, 4, S)
 

time: 118 us -> 118 us (level)
  the two profiles are of different devices: /device:TPU:8 before, /device:TPU:1 now
where the time goes in v4:
time: 118 us
  blocking collectives  42.3 us (36%)
  starting transfers between devices  34.4 us (29%)
  Pallas kernels  25.7 us (22%)
  waiting for transfers between devices  14.2 us (12%)
    all_to_all x1, blocking collectives, per_device(): rows = lax.all_to_all(rows, 'row', 0, 0, tiled=True)  17 us
    all_to_all x1, blocking collectives, per_device(): got = lax.all_to_all(partials, 'row', 0, 0, tiled=True)  14 us
    all_to_all x1, blocking collectives, per_device(): out = lax.all_to_all(out, 'col', 0, 0, tiled=True)  11.4 us
    pallas_call x2, Pallas kernels, sweep(): call(body, out, flops=2 * E * S * S * 4 * 52, moved=6 * MB, in_specs=[IN_...  10.9 us
    pallas_call x1, Pallas kernels, make_kernel(): call(kernel_body, (hbm((NC, U, NR * U), BF), hbm((NR, 3, E, U), BF)), flo...  8.59 us
    all_to_all x1, starting transfers between devices, per_device(): got = lax.all_to_all(partials, 'row', 0, 0, tiled=True)  7.43 us
    all_to_all x1, starting transfers between devices, per_device(): cols = lax.all_to_all(cols, 'col', 0, 0, tiled=True)  7.31 us
    ppermute x2, waiting for transfers between devices, per_device(): near_b = lax.ppermute(mid, 'col', swap_b)  6.88 us
  transfers between devices with their start and end apart: 12, of which 4 were waited for; matrix products, arithmetic and copies ran while one was open for 0% of the time, Pallas kernels for 10%

profile of v4, /device:TPU:1, one launch (start us, length us, event | category | flops | bytes accessed | tf_op | source)
XLA Modules:
  0.0 117.5 jit_solution(9704278794788931608)
XLA Ops:
  0.6 2.4 %shard_map.77 = (bf16[8,48,128]{2,1,0:T(8,128)(2,1)}, bf16[16,80,128]{2,1,0:T(8,128)(2,1)}, bf16[2064,128]{1,0:T(8,128)(2,1)}, bf16[2064,128]{1,0:T(8,128)(2,1)}, bf16[16,128]{1,0:T(8,128)(2,1)S(1)}) custom-call(bf16[64,128]{1,0:T(8,128)(2,1)} %traces_h.1, f32[3,128]{1,0:T(4,128)} %points_h.1, s32[1,128]{1,0:T(1,128)} %bitcast.8, s32[4,4,4]{2,1,0:T(4,128)} %columns_h.1, ...), custom_call_target="tpu_custom_call" | custom-call | tf_op jit(solution)/shard_map/pallas_call | solution.py:127
  3.1 4.0 %collective-permute-start.2 = (bf16[2064,128]{1,0:T(8,128)(2,1)}, bf16[2064,128]{1,0:T(8,128)(2,1)S(1)}, u32[]{:S(2)}, u32[]{:S(2)}) collective-permute-start(bf16[2064,128]{1,0:T(8,128)(2,1)} %get-tuple-element.25), channel_id=1, source_target_pairs={{0,16},{16,32},{32,48},{48,64},{64,80},{80,96},{96,112},{1,17},{17... | collective-permute-start | bytes 1585160 | tf_op jit(solution)/shard_map/ppermute | solution.py:514
  7.0 1.3 %collective-permute-start.3 = (bf16[2064,128]{1,0:T(8,128)(2,1)}, bf16[2064,128]{1,0:T(8,128)(2,1)S(1)}, u32[]{:S(2)}, u32[]{:S(2)}) collective-permute-start(bf16[2064,128]{1,0:T(8,128)(2,1)} %get-tuple-element.26), channel_id=1, source_target_pairs={{16,0},{32,16},{48,32},{64,48},{80,64},{96,80},{112,96},{17,1},{33... | collective-permute-start | bytes 1585160 | tf_op jit(solution)/shard_map/ppermute | solution.py:515
  8.3 17.0 %all_to_all.25.row_ref = bf16[8,48,128]{2,1,0:T(8,128)(2,1)} all-to-all(bf16[8,48,128]{2,1,0:T(8,128)(2,1)} %get-tuple-element.21), channel_id=1, replica_groups=mesh['row'=8,'col'=16] {'row'}, dimensions={0} | all-to-all | bytes 196608 | tf_op jit(solution)/shard_map/all_to_all | solution.py:509
  25.4 7.3 %all-to-all-start = ((bf16[16,80,128]{2,1,0:T(8,128)(2,1)}), bf16[16,80,128]{2,1,0:T(8,128)(2,1)S(1)}, u32[]{:S(2)}, u32[]{:S(2)}) async-start(bf16[16,80,128]{2,1,0:T(8,128)(2,1)} %get-tuple-element.20), calls=%async_computation | async-start | bytes 655360 | tf_op jit(solution)/shard_map/all_to_all | solution.py:510
  32.7 1.3 %shard_map.81 = (bf16[2048,128]{1,0:T(8,128)(2,1)S(1)}, bf16[2048,128]{1,0:T(8,128)(2,1)S(1)}) custom-call(bf16[8192,128]{1,0:T(8,128)(2,1)} %bitcast.5), custom_call_target="tpu_custom_call" | custom-call | bytes 2097152 | tf_op jit(solution)/shard_map/pallas_call | solution.py:160
  34.0 3.5 %collective-permute-start.6 = (bf16[2048,128]{1,0:T(8,128)(2,1)S(1)}, bf16[2048,128]{1,0:T(8,128)(2,1)}, u32[]{:S(2)}, u32[]{:S(2)}) collective-permute-start(bf16[2048,128]{1,0:T(8,128)(2,1)S(1)} %get-tuple-element.31), channel_id=1, source_target_pairs={{0,1},{1,2},{2,3},{3,4},{4,5},{5,6},{6,7},{7,8},{8,9},{9,10},{10,1... | collective-permute-start | bytes 1572872 | tf_op jit(solution)/shard_map/ppermute | solution.py:512
  37.6 1.9 %collective-permute-start.7 = (bf16[2048,128]{1,0:T(8,128)(2,1)S(1)}, bf16[2048,128]{1,0:T(8,128)(2,1)}, u32[]{:S(2)}, u32[]{:S(2)}) collective-permute-start(bf16[2048,128]{1,0:T(8,128)(2,1)S(1)} %get-tuple-element.32), channel_id=1, source_target_pairs={{1,0},{2,1},{3,2},{4,3},{5,4},{6,5},{7,6},{8,7},{9,8},{10,9},{11,1... | collective-permute-start | bytes 1572872 | tf_op jit(solution)/shard_map/ppermute | solution.py:513
  39.5 1.1 all-to-all-done.col_ref
  40.7 8.6 %shard_map.78 = (bf16[16,128,1024]{2,1,0:T(8,128)(2,1)}, bf16[8,3,64,128]{3,2,1,0:T(8,128)(2,1)}) custom-call(bf16[16,80,128]{2,1,0:T(8,128)(2,1)S(1)} %all-to-all-done.col_ref, bf16[8,48,128]{2,1,0:T(8,128)(2,1)} %all_to_all.25.row_ref), custom_call_target="tpu_custom_call" | custom-call | flops 83886080 | bytes 6291456 | tf_op jit(solution)/shard_map/pallas_call | solution.py:286
  49.3 7.4 %all-to-all-start.2 = ((bf16[8,3,64,128]{3,2,1,0:T(8,128)(2,1)}), bf16[8,3,64,128]{3,2,1,0:T(8,128)(2,1)S(1)}, u32[]{:S(2)}, u32[]{:S(2)}) async-start(bf16[8,3,64,128]{3,2,1,0:T(8,128)(2,1)} %get-tuple-element.22), calls=%async_computation.2 | async-start | bytes 786432 | tf_op jit(solution)/shard_map/all_to_all | solution.py:517
  56.7 1.5 %shard_map.80 = (bf16[1072,128]{1,0:T(8,128)(2,1)}, bf16[1072,128]{1,0:T(8,128)(2,1)S(1)}, bf16[48,128]{1,0:T(8,128)(2,1)S(1)}) custom-call(s32[1]{0:T(128)} %bitcast.parity.refs_0_, bf16[2064,128]{1,0:T(8,128)(2,1)S(1)} %collective-permute-done.2.prev.refs_10_, bf16[2064,128]{1,0:T(8,128)(2,1)S(1)} %collective-permute-done.3.nxt.refs_11_, ...), custom_call_target="tpu_custom_call" | custom-call | bytes 2097152 | tf_op jit(solution)/shard_map/pallas_call | solution.py:194
  59.0 1.9 %collective-permute-start.5 = (bf16[1072,128]{1,0:T(8,128)(2,1)S(1)}, bf16[1072,128]{1,0:T(8,128)(2,1)S(1)}, u32[]{:S(2)}, u32[]{:S(2)}) collective-permute-start(bf16[1072,128]{1,0:T(8,128)(2,1)S(1)} %get-tuple-element.29), channel_id=1, source_target_pairs={{1,2},{2,1},{3,4},{4,3},{5,6},{6,5},{7,8},{8,7},{9,10},{10,9},{11,... | collective-permute-start | bytes 823304 | tf_op jit(solution)/shard_map/ppermute | solution.py:520
  60.9 6.2 %all-to-all-done.2.got = bf16[8,3,64,128]{3,2,1,0:T(8,128)(2,1)S(1)} async-done(((bf16[8,3,64,128]{3,2,1,0:T(8,128)(2,1)}), bf16[8,3,64,128]{3,2,1,0:T(8,128)(2,1)S(1)}, u32[]{:S(2)}, u32[]{:S(2)}) %all-to-all-start.2) | async-done | bytes 393248 | tf_op jit(solution)/shard_map/all_to_all | solution.py:517
  67.1 1.1 collective-permute-start
  68.2 2.1 %collective-permute-start.1 = (bf16[192,128]{1,0:T(8,128)(2,1)S(1)}, bf16[192,128]{1,0:T(8,128)(2,1)S(1)}, u32[]{:S(2)}, u32[]{:S(2)}) collective-permute-start(bf16[192,128]{1,0:T(8,128)(2,1)S(1)} %get-tuple-element.24.refs_2_), channel_id=1, source_target_pairs={{1,2},{2,1},{3,4},{4,3},{5,6},{6,5},{7,8},{8,7},{9,10},{10,9},{11,... | collective-permute-start | bytes 147464 | tf_op jit(solution)/shard_map/ppermute | solution.py:525
  70.3 3.4 %collective-permute-done.1.refs_4_ = bf16[192,128]{1,0:T(8,128)(2,1)S(1)} collective-permute-done((bf16[192,128]{1,0:T(8,128)(2,1)S(1)}, bf16[192,128]{1,0:T(8,128)(2,1)S(1)}, u32[]{:S(2)}, u32[]{:S(2)}) %collective-permute-start.1) | collective-permute-done | bytes 49184 | tf_op jit(solution)/shard_map/ppermute | solution.py:525
  73.7 5.1 %shard_map.82 = bf16[16,64,128]{2,1,0:T(8,128)(2,1)S(1)} custom-call(s32[1]{0:T(128)} %bitcast.parity.refs_0_, f32[64,128]{1,0:T(8,128)S(1)} %get-tuple-element.23.refs_1_, bf16[192,128]{1,0:T(8,128)(2,1)S(1)} %get-tuple-element.24.refs_2_, bf16[192,128]{1,0:T(8,128)(2,1)S(1)} %collective-permute-done.refs_3_, ...), custom_call_target="tpu_custom_call" | custom-call | flops 436207616 | bytes 6291456 | tf_op jit(solution)/shard_map/pallas_call | solution.py:471
  78.9 11.4 %all_to_all.26.p_ref = bf16[16,64,128]{2,1,0:T(8,128)(2,1)S(1)} all-to-all(bf16[16,64,128]{2,1,0:T(8,128)(2,1)S(1)} %shard_map.82), channel_id=1, replica_groups=mesh['row'=8,'col'=16] {'col'}, dimensions={0} | all-to-all | bytes 524288 | tf_op jit(solution)/shard_map/all_to_all | solution.py:530
  91.1 14.0 %all_to_all.27.got = bf16[8,3,64,128]{3,2,1,0:T(8,128)(2,1)S(1)} all-to-all(bf16[8,3,64,128]{3,2,1,0:T(8,128)(2,1)S(1)} %shard_map.83), channel_id=1, replica_groups=mesh['row'=8,'col'=16] {'row'}, dimensions={0} | all-to-all | bytes 786432 | tf_op jit(solution)/shard_map/all_to_all | solution.py:532
  105.1 1.3 %collective-permute-start.8 = (bf16[192,128]{1,0:T(8,128)(2,1)S(1)}, bf16[192,128]{1,0:T(8,128)(2,1)S(1)}, u32[]{:S(2)}, u32[]{:S(2)}) collective-permute-start(bf16[192,128]{1,0:T(8,128)(2,1)S(1)} %get-tuple-element.35.refs_2_), channel_id=1, source_target_pairs={{0,1},{1,0},{2,3},{3,2},{4,5},{5,4},{6,7},{7,6},{8,9},{9,8},{10,11... | collective-permute-start | bytes 147464 | tf_op jit(solution)/shard_map/ppermute | solution.py:524
  106.3 1.9 %collective-permute-start.9 = (bf16[192,128]{1,0:T(8,128)(2,1)S(1)}, bf16[192,128]{1,0:T(8,128)(2,1)S(1)}, u32[]{:S(2)}, u32[]{:S(2)}) collective-permute-start(bf16[192,128]{1,0:T(8,128)(2,1)S(1)} %get-tuple-element.35.refs_2_), channel_id=1, source_target_pairs={{1,2},{2,1},{3,4},{4,3},{5,6},{6,5},{7,8},{8,7},{9,10},{10,9},{11,... | collective-permute-start | bytes 147464 | tf_op jit(solution)/shard_map/ppermute | solution.py:525
  108.3 3.5 %collective-permute-done.9.refs_4_ = bf16[192,128]{1,0:T(8,128)(2,1)S(1)} collective-permute-done((bf16[192,128]{1,0:T(8,128)(2,1)S(1)}, bf16[192,128]{1,0:T(8,128)(2,1)S(1)}, u32[]{:S(2)}, u32[]{:S(2)}) %collective-permute-start.9) | collective-permute-done | bytes 49184 | tf_op jit(solution)/shard_map/ppermute | solution.py:525
  111.7 5.8 %shard_map.85 = (bf16[64,128]{1,0:T(8,128)(2,1)}, f32[1024,128]{1,0:T(8,128)}) custom-call(s32[1]{0:T(128)} %bitcast.parity.refs_0_, f32[64,128]{1,0:T(8,128)S(1)} %get-tuple-element.34.refs_1_, bf16[192,128]{1,0:T(8,128)(2,1)S(1)} %get-tuple-element.35.refs_2_, bf16[192,128]{1,0:T(8,128)(2,1)S(1)} %collective-permute-done.8.refs_3_, ...), custom_call_target="tpu_custom_call" | custom-call | flops 436207616 | bytes 6291456 | tf_op jit(solution)/shard_map/pallas_call | solution.py:471
  (20 shorter events, 1.8 us)
Async XLA Ops:
  0.6 73.1 %copy-start.3 = (bf16[64,128]{1,0:T(8,128)(2,1)S(1)}, bf16[64,128]{1,0:T(8,128)(2,1)}, u32[]{:S(2)}) copy-start(bf16[64,128]{1,0:T(8,128)(2,1)} %refs_7_.3) | copy-start | bytes 49156
  3.1 53.6 %collective-permute-start.2 = (bf16[2064,128]{1,0:T(8,128)(2,1)}, bf16[2064,128]{1,0:T(8,128)(2,1)S(1)}, u32[]{:S(2)}, u32[]{:S(2)}) collective-permute-start(bf16[2064,128]{1,0:T(8,128)(2,1)} %get-tuple-element.25), channel_id=1, source_target_pairs={{0,16},{16,32},{32,48},{48,64},{64,80},{80,96},{96,112},{1,17},{17... | collective-permute-start | bytes 1585160 | tf_op jit(solution)/shard_map/ppermute | solution.py:514
  7.0 49.7 %collective-permute-start.3 = (bf16[2064,128]{1,0:T(8,128)(2,1)}, bf16[2064,128]{1,0:T(8,128)(2,1)S(1)}, u32[]{:S(2)}, u32[]{:S(2)}) collective-permute-start(bf16[2064,128]{1,0:T(8,128)(2,1)} %get-tuple-element.26), channel_id=1, source_target_pairs={{16,0},{32,16},{48,32},{64,48},{80,64},{96,80},{112,96},{17,1},{33... | collective-permute-start | bytes 1585160 | tf_op jit(solution)/shard_map/ppermute | solution.py:515
  25.4 15.3 %all-to-all-start = ((bf16[16,80,128]{2,1,0:T(8,128)(2,1)}), bf16[16,80,128]{2,1,0:T(8,128)(2,1)S(1)}, u32[]{:S(2)}, u32[]{:S(2)}) async-start(bf16[16,80,128]{2,1,0:T(8,128)(2,1)} %get-tuple-element.20), calls=%async_computation | async-start | bytes 655360 | tf_op jit(solution)/shard_map/all_to_all | solution.py:510
  34.0 34.1 %collective-permute-start.6 = (bf16[2048,128]{1,0:T(8,128)(2,1)S(1)}, bf16[2048,128]{1,0:T(8,128)(2,1)}, u32[]{:S(2)}, u32[]{:S(2)}) collective-permute-start(bf16[2048,128]{1,0:T(8,128)(2,1)S(1)} %get-tuple-element.31), channel_id=1, source_target_pairs={{0,1},{1,2},{2,3},{3,4},{4,5},{5,6},{6,7},{7,8},{8,9},{9,10},{10,1... | collective-permute-start | bytes 1572872 | tf_op jit(solution)/shard_map/ppermute | solution.py:512
  37.6 32.7 %collective-permute-start.7 = (bf16[2048,128]{1,0:T(8,128)(2,1)S(1)}, bf16[2048,128]{1,0:T(8,128)(2,1)}, u32[]{:S(2)}, u32[]{:S(2)}) collective-permute-start(bf16[2048,128]{1,0:T(8,128)(2,1)S(1)} %get-tuple-element.32), channel_id=1, source_target_pairs={{1,0},{2,1},{3,2},{4,3},{5,4},{6,5},{7,6},{8,7},{9,8},{10,9},{11,1... | collective-permute-start | bytes 1572872 | tf_op jit(solution)/shard_map/ppermute | solution.py:513
  49.3 17.8 %all-to-all-start.2 = ((bf16[8,3,64,128]{3,2,1,0:T(8,128)(2,1)}), bf16[8,3,64,128]{3,2,1,0:T(8,128)(2,1)S(1)}, u32[]{:S(2)}, u32[]{:S(2)}) async-start(bf16[8,3,64,128]{3,2,1,0:T(8,128)(2,1)} %get-tuple-element.22), calls=%async_computation.2 | async-start | bytes 786432 | tf_op jit(solution)/shard_map/all_to_all | solution.py:517
  56.7 17.0 %copy-start = (bf16[2064,128]{1,0:T(8,128)(2,1)}, bf16[2064,128]{1,0:T(8,128)(2,1)S(1)}, u32[]{:S(2)}) copy-start(bf16[2064,128]{1,0:T(8,128)(2,1)S(1)} %collective-permute-done.2.prev.refs_10_) | copy-start | bytes 1585156
  56.7 17.0 %copy-start.1 = (bf16[2064,128]{1,0:T(8,128)(2,1)}, bf16[2064,128]{1,0:T(8,128)(2,1)S(1)}, u32[]{:S(2)}) copy-start(bf16[2064,128]{1,0:T(8,128)(2,1)S(1)} %collective-permute-done.3.nxt.refs_11_) | copy-start | bytes 1585156
  58.2 15.5 %collective-permute-start.4 = (bf16[1072,128]{1,0:T(8,128)(2,1)}, bf16[1072,128]{1,0:T(8,128)(2,1)S(1)}, u32[]{:S(2)}, u32[]{:S(2)}) collective-permute-start(bf16[1072,128]{1,0:T(8,128)(2,1)} %get-tuple-element.28), channel_id=1, source_target_pairs={{0,1},{1,0},{2,3},{3,2},{4,5},{5,4},{6,7},{7,6},{8,9},{9,8},{10,11... | collective-permute-start | bytes 823304 | tf_op jit(solution)/shard_map/ppermute | solution.py:519
  59.0 14.7 %collective-permute-start.5 = (bf16[1072,128]{1,0:T(8,128)(2,1)S(1)}, bf16[1072,128]{1,0:T(8,128)(2,1)S(1)}, u32[]{:S(2)}, u32[]{:S(2)}) collective-permute-start(bf16[1072,128]{1,0:T(8,128)(2,1)S(1)} %get-tuple-element.29), channel_id=1, source_target_pairs={{1,2},{2,1},{3,4},{4,3},{5,6},{6,5},{7,8},{8,7},{9,10},{10,9},{11,... | collective-permute-start | bytes 823304 | tf_op jit(solution)/shard_map/ppermute | solution.py:520
  67.0 23.2 %copy-start.2 = (bf16[16,128,1024]{2,1,0:T(8,128)(2,1)S(1)}, bf16[16,128,1024]{2,1,0:T(8,128)(2,1)}, u32[]{:S(2)}) copy-start(bf16[16,128,1024]{2,1,0:T(8,128)(2,1)} %get-tuple-element.33.k_ref) | copy-start | bytes 12582916
  67.1 3.2 %collective-permute-start = (bf16[192,128]{1,0:T(8,128)(2,1)S(1)}, bf16[192,128]{1,0:T(8,128)(2,1)S(1)}, u32[]{:S(2)}, u32[]{:S(2)}) collective-permute-start(bf16[192,128]{1,0:T(8,128)(2,1)S(1)} %get-tuple-element.24.refs_2_), channel_id=1, source_target_pairs={{0,1},{1,0},{2,3},{3,2},{4,5},{5,4},{6,7},{7,6},{8,9},{9,8},{10,11... | collective-permute-start | bytes 147464 | tf_op jit(solution)/shard_map/ppermute | solution.py:524
  68.2 5.5 %collective-permute-start.1 = (bf16[192,128]{1,0:T(8,128)(2,1)S(1)}, bf16[192,128]{1,0:T(8,128)(2,1)S(1)}, u32[]{:S(2)}, u32[]{:S(2)}) collective-permute-start(bf16[192,128]{1,0:T(8,128)(2,1)S(1)} %get-tuple-element.24.refs_2_), channel_id=1, source_target_pairs={{1,2},{2,1},{3,4},{4,3},{5,6},{6,5},{7,8},{8,7},{9,10},{10,9},{11,... | collective-permute-start | bytes 147464 | tf_op jit(solution)/shard_map/ppermute | solution.py:525
  105.1 3.2 %collective-permute-start.8 = (bf16[192,128]{1,0:T(8,128)(2,1)S(1)}, bf16[192,128]{1,0:T(8,128)(2,1)S(1)}, u32[]{:S(2)}, u32[]{:S(2)}) collective-permute-start(bf16[192,128]{1,0:T(8,128)(2,1)S(1)} %get-tuple-element.35.refs_2_), channel_id=1, source_target_pairs={{0,1},{1,0},{2,3},{3,2},{4,5},{5,4},{6,7},{7,6},{8,9},{9,8},{10,11... | collective-permute-start | bytes 147464 | tf_op jit(solution)/shard_map/ppermute | solution.py:524
  106.3 5.4 %collective-permute-start.9 = (bf16[192,128]{1,0:T(8,128)(2,1)S(1)}, bf16[192,128]{1,0:T(8,128)(2,1)S(1)}, u32[]{:S(2)}, u32[]{:S(2)}) collective-permute-start(bf16[192,128]{1,0:T(8,128)(2,1)S(1)} %get-tuple-element.35.refs_2_), channel_id=1, source_target_pairs={{1,2},{2,1},{3,4},{4,3},{5,6},{6,5},{7,8},{8,7},{9,10},{10,9},{11,... | collective-permute-start | bytes 147464 | tf_op jit(solution)/shard_map/ppermute | solution.py:525

commit v5 on v4

--- a/solution.py
+++ b/solution.py
@@ -49,10 +49,6 @@
     return pltpu.MemorySpace.HBM(dims, dtype)
 
 
-def vmem(dims, dtype):
-    return pltpu.MemorySpace.VMEM(dims, dtype)
-
-
 def keep(*values):
     return tuple(pltpu.with_memory_space_constraint(v, pltpu.MemorySpace.HBM) for v in values)
 
@@ -76,15 +72,11 @@
     return out
 
 
-def pack_body(traces_h, points_h, coupling_h, columns_h, tiles, row_out, col_out, up, down, meta_out, *scratch):
-    traces, points, coupling, columns, sems = scratch
-    loads = [(points_h, points), (columns_h, columns), (coupling_h, coupling), (traces_h, traces)]
-    loads += [(tiles.at[pl.ds(12 * ROWS, 4 * ROWS)], up.at[pl.ds(0, 4 * ROWS)])]
-    loads += [(tiles.at[pl.ds(0, 4 * ROWS)], down.at[pl.ds(0, 4 * ROWS)])]
+def pack_body(traces_h, points_h, row_out, col_out, traces, points, sems):
+    loads = [(points_h, points), (traces_h, traces)]
     loads = [pltpu.make_async_copy(a, b, sems.at[n]) for n, (a, b) in enumerate(loads)]
     for copy in loads:
         copy.start()
-    lane = lax.broadcasted_iota(jnp.int32, (1, U), 1)
     loads[0].wait()
     p = (points[...] - 0.5) * TURNS
     parts = split3(p)
@@ -104,50 +96,71 @@
         for j in range(3):
             row_out[r, 16 * j : 16 * j + 16] = target[j]
     loads[1].wait()
+    for c in range(NC):
+        col_out[c, :E] = traces[...]
+        col_out[c, E:] = source
+
+
+def pack(traces, points):
+    return call(
+        pack_body,
+        (hbm((NR, 48, U), BF), hbm((NC, E + 16, U), BF)),
+        in_specs=[IN_HBM] * 2,
+        out_specs=(IN_VMEM,) * 2,
+        scratch_shapes=[pltpu.VMEM((E, U), BF), pltpu.VMEM((3, U), F32), pltpu.SemaphoreType.DMA((2,))],
+    )(*keep(traces, points))
+
+
+def slices_body(coupling_h, columns_h, tiles, up, down, meta_out, coupling, columns, sems):
+    loads = [(columns_h, columns), (coupling_h, coupling)]
+    loads += [(tiles.at[pl.ds(12 * ROWS, 4 * ROWS)], up.at[pl.ds(0, 4 * ROWS)])]
+    loads += [(tiles.at[pl.ds(0, 4 * ROWS)], down.at[pl.ds(0, 4 * ROWS)])]
+    loads = [pltpu.make_async_copy(a, b, sems.at[n]) for n, (a, b) in enumerate(loads)]
+    for copy in loads:
+        copy.start()
+    lane = lax.broadcasted_iota(jnp.int32, (1, U), 1)
+    line = lax.broadcasted_iota(jnp.int32, (16, U), 0)
+    loads[0].wait()
     offsets = jnp.zeros((1, U), jnp.int32)
     for n in range(64):
         offsets = jnp.where(lane == n, columns[n // 16, n // 4 % 4, n % 4], offsets)
-    loads[2].wait()
+    loads[1].wait()
     at = coupling[...]
     meta = [(0, (at >> 7).astype(F32)), (1, (at & 127).astype(F32)), (2, offsets.astype(F32))]
     meta = rows_at(line, meta).astype(BF)
     meta_out[...] = meta
     up[4 * ROWS :] = meta
     down[4 * ROWS :] = meta
-    loads[3].wait()
-    for c in range(NC):
-        col_out[c, :E] = traces[...]
-        col_out[c, E:] = source
-    for copy in loads[4:]:
-        copy.wait()
-
-
-def pack(traces, points, coupling, columns, tiles):
+    for copy in loads[2:]:
+        copy.wait()
+
+
+def slices(coupling, columns, tiles):
     side = hbm((4 * ROWS + 16, S), BF)
     return call(
-        pack_body,
-        (hbm((NR, 48, U), BF), hbm((NC, E + 16, U), BF), side, side, vmem((16, U), BF)),
-        in_specs=[IN_HBM] * 5,
-        out_specs=(IN_VMEM,) * 5,
+        slices_body,
+        (side, side, shape((16, U), BF)),
+        moved=2 * MB,
+        in_specs=[IN_HBM] * 3,
+        out_specs=(IN_VMEM,) * 3,
         scratch_shapes=[
-            pltpu.VMEM((E, U), BF),
-            pltpu.VMEM((3, U), F32),
             pltpu.VMEM((1, U), jnp.int32),
             pltpu.SMEM((4, 4, 4), jnp.int32),
-            pltpu.SemaphoreType.DMA((6,)),
+            pltpu.SemaphoreType.DMA((4,)),
         ],
-    )(*keep(traces, points, coupling, columns, tiles))
+    )(*keep(coupling, columns, tiles))
 
 
 def column_of(odd, side):
     return 3 * odd if side else 3 - 3 * odd
 
 
-def fill_body(tiles, left_out, right_out, sems):
+def fill_body(parity, tiles, out_a, out_b, sems):
     copies = []
-    for out, j in ((left_out, 3), (right_out, 0)):
+    for side, out in enumerate((out_a, out_b)):
+        j = column_of(parity[0], side)
         for i in range(4):
-            piece = tiles.at[pl.ds((4 * i + j) * ROWS, ROWS)]
+            piece = tiles.at[pl.ds(pl.multiple_of((4 * i + j) * ROWS, ROWS), ROWS)]
             copies.append(pltpu.make_async_copy(piece, out.at[pl.ds(i * ROWS, ROWS)], sems.at[len(copies)]))
     for copy in copies:
         copy.start()
@@ -155,16 +168,16 @@
         copy.wait()
 
 
-def fill(tiles):
+def fill(parity, tiles):
     side = shape((4 * ROWS, S), BF)
     return call(
         fill_body,
         (side, side),
         moved=2 * MB,
-        in_specs=[IN_HBM],
+        in_specs=[IN_SMEM, IN_HBM],
         out_specs=(IN_VMEM,) * 2,
         scratch_shapes=[pltpu.SemaphoreType.DMA((8,))],
-    )(*keep(tiles))
+    )(parity, *keep(tiles))
 
 
 def corner_body(parity, prev, nxt, meta, out_a, out_b, meta_out, sems):
@@ -326,15 +339,15 @@
     return ((0, 2), (1, 3)) if b == 0 else ((6, 0), (7, 1)) if b == 2 else tuple((2 + i, i) for i in range(4))
 
 
-def sweep_body(last, parity, own_ref, mid, near_a, near_b, far_a, far_b, inc, mid_metas, tiles_h, prev_h, nxt_h, lefts_h, rights_h, *rest):
+def sweep_body(last, parity, own_ref, mid, near_a, near_b, far_a, far_b, inc, mid_metas, tiles_h, prev_h, nxt_h, edge_a_h, edge_b_h, *rest):
     if last:
         present_out, field_out = rest[:2]
     else:
         present_out, field_out = rest[0], None
-    src, srcf, f1, fields, tiles, prev, nxt, lefts, rights, moves_v, moves, sems = rest[2 if last else 1 :]
+    src, srcf, f1, fields, tiles, prev, nxt, edge_a, edge_b, moves_v, moves, sems = rest[2 if last else 1 :]
     loads = [(moves_v, moves), (tiles_h, tiles)]
     loads += [(h.at[pl.ds(0, 4 * ROWS)], v) for h, v in ((prev_h, prev), (nxt_h, nxt))]
-    loads += [(lefts_h, lefts), (rights_h, rights)]
+    loads += [(edge_a_h, edge_a), (edge_b_h, edge_b)]
     odd = parity[0]
     partners = ((6 - 6 * odd, 2 * odd, 6 - 5 * odd, 3 * odd), (6 * odd, 2 - 2 * odd, 1 + 5 * odd, 3 - 3 * odd))
     loads = [pltpu.make_async_copy(a, b, sems.at[n]) for n, (a, b) in enumerate(loads)]
@@ -424,8 +437,8 @@
 
     def edge_col(i, carry):
         w = (2 + i) * 8
-        halo(w + 1, 5 - 2 * odd, i * 4 + 3, lefts, i * ROWS)
-        halo(w + 6, 3 + 2 * odd, i * 4, rights, i * ROWS)
+        for n, ref in enumerate((edge_a, edge_b)):
+            halo(w + partners[n][2], 3 + 2 * n, i * 4 + partners[n][3], ref, i * ROWS)
         return carry
 
     for i in range(4):
@@ -500,17 +513,17 @@
 
 def per_device(traces, incident, points, coupling, volume_tiles, tile_columns):
     row_up, row_down = shift("row")
-    col_up, col_down = shift("col")
     parity = (lax.axis_index("col") % 2).reshape(1)
     swap_a = [(c, c ^ 1) for c in range(NC)]
     swap_b = [(c, ((c - 1) ^ 1) + 1) for c in range(1, NC - 1)]
     tiles = volume_tiles.reshape(16 * ROWS, S)
-    rows, cols, up, down, meta = pack(traces, points, coupling.reshape(1, U), tile_columns, tiles)
+    rows, cols = pack(traces, points)
     rows = lax.all_to_all(rows, "row", 0, 0, tiled=True)
     cols = lax.all_to_all(cols, "col", 0, 0, tiled=True)
-    lefts, rights = fill(tiles)
-    lefts = lax.ppermute(lefts, "col", col_up)
-    rights = lax.ppermute(rights, "col", col_down)
+    edge_a, edge_b = fill(parity, tiles)
+    edge_a = lax.ppermute(edge_a, "col", swap_a)
+    edge_b = lax.ppermute(edge_b, "col", swap_b)
+    up, down, meta = slices(coupling.reshape(1, U), tile_columns, tiles)
     prev = lax.ppermute(up, "row", row_up)
     nxt = lax.ppermute(down, "row", row_down)
     kernel, partials = make_kernel(cols, rows)
@@ -524,7 +537,7 @@
         near_a = lax.ppermute(mid, "col", swap_a)
         near_b = lax.ppermute(mid, "col", swap_b)
         out = sweep(
-            last, parity, own, mid, near_a, near_b, far_a, far_b, incident, metas, tiles, prev, nxt, lefts, rights
+            last, parity, own, mid, near_a, near_b, far_a, far_b, incident, metas, tiles, prev, nxt, edge_a, edge_b
         )
         if not last:
             out = lax.all_to_all(out, "col", 0, 0, tiled=True)

time: 118 us -> 117 us (level)
  blocking collectives: 42.3 us -> 39.9 us
  starting transfers between devices: 34.4 us -> 32.2 us
  Pallas kernels: 25.7 us -> 27.3 us
  waiting for transfers between devices: 14.2 us -> 15.7 us
    all_to_all x1, waiting for transfers between devices: 1.15 us -> 2.9 us  [per_device(): cols = lax.all_to_all(cols, 'col', 0, 0, tiled=True)]
    ppermute x2, starting transfers between devices: 5.46 us -> 3.72 us  [the longest x1 3.52 us: per_device(): edge_b = lax.ppermute(edge_b, 'col', swap_b)]
    all_to_all x1, blocking collectives: 14 us -> 12.6 us  [per_device(): got = lax.all_to_all(partials, 'row', 0, 0, tiled=True)]
    pallas_call x2 -> x3, Pallas kernels: 3.77 us -> 5.12 us  [the longest x1 2.25 us: slices(): call(slices_body, (side, side, shape((16, U), BF)), moved=2 * MB, in_spec...]
  transfers between devices with their start and end apart: 12 -> 12, of which waited for: 4 -> 4; matrix products, arithmetic and copies ran while one was open for 0% -> 0% of each run, Pallas kernels for 10% -> 11%
where the time goes in v5:
time: 117 us; the launch traced here: 116 us
  blocking collectives  39.9 us (34%)
  starting transfers between devices  32.2 us (28%)
  Pallas kernels  27.3 us (23%)
  waiting for transfers between devices  15.7 us (13%)
    all_to_all x1, blocking collectives, per_device(): rows = lax.all_to_all(rows, 'row', 0, 0, tiled=True)  16.2 us
    all_to_all x1, blocking collectives, per_device(): got = lax.all_to_all(partials, 'row', 0, 0, tiled=True)  12.6 us
    pallas_call x2, Pallas kernels, sweep(): call(body, out, flops=2 * E * S * S * 4 * 52, moved=6 * MB, in_specs=[IN_...  11.2 us
    all_to_all x1, blocking collectives, per_device(): out = lax.all_to_all(out, 'col', 0, 0, tiled=True)  11.1 us
    pallas_call x1, Pallas kernels, make_kernel(): call(kernel_body, (hbm((NC, U, NR * U), BF), hbm((NR, 3, E, U), BF)), flo...  8.59 us
    all_to_all x1, starting transfers between devices, per_device(): cols = lax.all_to_all(cols, 'col', 0, 0, tiled=True)  7.6 us
    ppermute x2, waiting for transfers between devices, per_device(): near_b = lax.ppermute(mid, 'col', swap_b)  6.58 us
    all_to_all x1, starting transfers between devices, per_device(): got = lax.all_to_all(partials, 'row', 0, 0, tiled=True)  6.27 us
  transfers between devices with their start and end apart: 12, of which 4 were waited for; matrix products, arithmetic and copies ran while one was open for 0% of the time, Pallas kernels for 11%

profile of v5, /device:TPU:1, one launch (start us, length us, event | category | flops | bytes accessed | tf_op | source)
XLA Modules:
  0.0 115.8 jit_solution(11762641119563409276)
XLA Ops:
  0.6 2.3 %shard_map.80 = (bf16[2064,128]{1,0:T(8,128)(2,1)}, bf16[2064,128]{1,0:T(8,128)(2,1)}, bf16[16,128]{1,0:T(8,128)(2,1)S(1)}) custom-call(s32[1,128]{1,0:T(1,128)} %bitcast.8, s32[4,4,4]{2,1,0:T(4,128)} %columns_h.1, bf16[8192,128]{1,0:T(8,128)(2,1)} %bitcast.4), custom_call_target="tpu_custom_call" | custom-call | bytes 2097152 | tf_op jit(solution)/shard_map/pallas_call | solution.py:140
  2.9 4.0 %collective-permute-start.2 = (bf16[2064,128]{1,0:T(8,128)(2,1)}, bf16[2064,128]{1,0:T(8,128)(2,1)S(1)}, u32[]{:S(2)}, u32[]{:S(2)}) collective-permute-start(bf16[2064,128]{1,0:T(8,128)(2,1)} %get-tuple-element.25), channel_id=1, source_target_pairs={{0,16},{16,32},{32,48},{48,64},{64,80},{80,96},{96,112},{1,17},{17... | collective-permute-start | bytes 1585160 | tf_op jit(solution)/shard_map/ppermute | solution.py:527
  6.9 1.3 %collective-permute-start.3 = (bf16[2064,128]{1,0:T(8,128)(2,1)}, bf16[2064,128]{1,0:T(8,128)(2,1)S(1)}, u32[]{:S(2)}, u32[]{:S(2)}) collective-permute-start(bf16[2064,128]{1,0:T(8,128)(2,1)} %get-tuple-element.26), channel_id=1, source_target_pairs={{16,0},{32,16},{48,32},{64,48},{80,64},{96,80},{112,96},{17,1},{33... | collective-permute-start | bytes 1585160 | tf_op jit(solution)/shard_map/ppermute | solution.py:528
  8.2 1.5 %shard_map.77 = (bf16[8,48,128]{2,1,0:T(8,128)(2,1)}, bf16[16,80,128]{2,1,0:T(8,128)(2,1)}) custom-call(bf16[64,128]{1,0:T(8,128)(2,1)} %traces_h.1, f32[3,128]{1,0:T(4,128)} %points_h.1), custom_call_target="tpu_custom_call" | custom-call | tf_op jit(solution)/shard_map/pallas_call | solution.py:105
  9.7 16.2 %all_to_all.25.row_ref = bf16[8,48,128]{2,1,0:T(8,128)(2,1)} all-to-all(bf16[8,48,128]{2,1,0:T(8,128)(2,1)} %get-tuple-element.21), channel_id=1, replica_groups=mesh['row'=8,'col'=16] {'row'}, dimensions={0} | all-to-all | bytes 196608 | tf_op jit(solution)/shard_map/all_to_all | solution.py:521
  25.9 7.6 %all-to-all-start = ((bf16[16,80,128]{2,1,0:T(8,128)(2,1)}), bf16[16,80,128]{2,1,0:T(8,128)(2,1)S(1)}, u32[]{:S(2)}, u32[]{:S(2)}) async-start(bf16[16,80,128]{2,1,0:T(8,128)(2,1)} %get-tuple-element.20), calls=%async_computation | async-start | bytes 655360 | tf_op jit(solution)/shard_map/all_to_all | solution.py:522
  33.5 1.3 %shard_map.82 = (bf16[2048,128]{1,0:T(8,128)(2,1)S(1)}, bf16[2048,128]{1,0:T(8,128)(2,1)S(1)}) custom-call(s32[1]{0:T(128)} %bitcast.parity.refs_0_, bf16[8192,128]{1,0:T(8,128)(2,1)} %bitcast.5), custom_call_target="tpu_custom_call" | custom-call | bytes 2097152 | tf_op jit(solution)/shard_map/pallas_call | solution.py:173
  35.1 3.5 %collective-permute-start.7 = (bf16[2048,128]{1,0:T(8,128)(2,1)S(1)}, bf16[2048,128]{1,0:T(8,128)(2,1)}, u32[]{:S(2)}, u32[]{:S(2)}) collective-permute-start(bf16[2048,128]{1,0:T(8,128)(2,1)S(1)} %get-tuple-element.32), channel_id=1, source_target_pairs={{1,2},{2,1},{3,4},{4,3},{5,6},{6,5},{7,8},{8,7},{9,10},{10,9},{11,... | collective-permute-start | bytes 1572872 | tf_op jit(solution)/shard_map/ppermute | solution.py:525
  38.6 2.9 %all-to-all-done.col_ref = bf16[16,80,128]{2,1,0:T(8,128)(2,1)S(1)} async-done(((bf16[16,80,128]{2,1,0:T(8,128)(2,1)}), bf16[16,80,128]{2,1,0:T(8,128)(2,1)S(1)}, u32[]{:S(2)}, u32[]{:S(2)}) %all-to-all-start) | async-done | bytes 327712 | tf_op jit(solution)/shard_map/all_to_all | solution.py:522
  41.5 8.6 %shard_map.78 = (bf16[16,128,1024]{2,1,0:T(8,128)(2,1)}, bf16[8,3,64,128]{3,2,1,0:T(8,128)(2,1)}) custom-call(bf16[16,80,128]{2,1,0:T(8,128)(2,1)S(1)} %all-to-all-done.col_ref, bf16[8,48,128]{2,1,0:T(8,128)(2,1)} %all_to_all.25.row_ref), custom_call_target="tpu_custom_call" | custom-call | flops 83886080 | bytes 6291456 | tf_op jit(solution)/shard_map/pallas_call | solution.py:299
  50.1 6.3 %all-to-all-start.2 = ((bf16[8,3,64,128]{3,2,1,0:T(8,128)(2,1)}), bf16[8,3,64,128]{3,2,1,0:T(8,128)(2,1)S(1)}, u32[]{:S(2)}, u32[]{:S(2)}) async-start(bf16[8,3,64,128]{3,2,1,0:T(8,128)(2,1)} %get-tuple-element.22), calls=%async_computation.2 | async-start | bytes 786432 | tf_op jit(solution)/shard_map/all_to_all | solution.py:530
  56.4 1.5 %shard_map.81 = (bf16[1072,128]{1,0:T(8,128)(2,1)}, bf16[1072,128]{1,0:T(8,128)(2,1)S(1)}, bf16[48,128]{1,0:T(8,128)(2,1)S(1)}) custom-call(s32[1]{0:T(128)} %bitcast.parity.refs_0_, bf16[2064,128]{1,0:T(8,128)(2,1)S(1)} %collective-permute-done.2.prev.refs_10_, bf16[2064,128]{1,0:T(8,128)(2,1)S(1)} %collective-permute-done.3.nxt.refs_11_, ...), custom_call_target="tpu_custom_call" | custom-call | bytes 2097152 | tf_op jit(solution)/shard_map/pallas_call | solution.py:207
  58.6 1.9 %collective-permute-start.5 = (bf16[1072,128]{1,0:T(8,128)(2,1)S(1)}, bf16[1072,128]{1,0:T(8,128)(2,1)S(1)}, u32[]{:S(2)}, u32[]{:S(2)}) collective-permute-start(bf16[1072,128]{1,0:T(8,128)(2,1)S(1)} %get-tuple-element.29), channel_id=1, source_target_pairs={{1,2},{2,1},{3,4},{4,3},{5,6},{6,5},{7,8},{8,7},{9,10},{10,9},{11,... | collective-permute-start | bytes 823304 | tf_op jit(solution)/shard_map/ppermute | solution.py:533
  60.6 6.2 %all-to-all-done.2.got = bf16[8,3,64,128]{3,2,1,0:T(8,128)(2,1)S(1)} async-done(((bf16[8,3,64,128]{3,2,1,0:T(8,128)(2,1)}), bf16[8,3,64,128]{3,2,1,0:T(8,128)(2,1)S(1)}, u32[]{:S(2)}, u32[]{:S(2)}) %all-to-all-start.2) | async-done | bytes 393248 | tf_op jit(solution)/shard_map/all_to_all | solution.py:530
  66.8 1.1 collective-permute-start
  67.9 2.1 %collective-permute-start.1 = (bf16[192,128]{1,0:T(8,128)(2,1)S(1)}, bf16[192,128]{1,0:T(8,128)(2,1)S(1)}, u32[]{:S(2)}, u32[]{:S(2)}) collective-permute-start(bf16[192,128]{1,0:T(8,128)(2,1)S(1)} %get-tuple-element.24.refs_2_), channel_id=1, source_target_pairs={{1,2},{2,1},{3,4},{4,3},{5,6},{6,5},{7,8},{8,7},{9,10},{10,9},{11,... | collective-permute-start | bytes 147464 | tf_op jit(solution)/shard_map/ppermute | solution.py:538
  70.0 3.4 %collective-permute-done.1.refs_4_ = bf16[192,128]{1,0:T(8,128)(2,1)S(1)} collective-permute-done((bf16[192,128]{1,0:T(8,128)(2,1)S(1)}, bf16[192,128]{1,0:T(8,128)(2,1)S(1)}, u32[]{:S(2)}, u32[]{:S(2)}) %collective-permute-start.1) | collective-permute-done | bytes 49184 | tf_op jit(solution)/shard_map/ppermute | solution.py:538
  73.4 5.3 %shard_map.83 = bf16[16,64,128]{2,1,0:T(8,128)(2,1)S(1)} custom-call(s32[1]{0:T(128)} %bitcast.parity.refs_0_, f32[64,128]{1,0:T(8,128)S(1)} %get-tuple-element.23.refs_1_, bf16[192,128]{1,0:T(8,128)(2,1)S(1)} %get-tuple-element.24.refs_2_, bf16[192,128]{1,0:T(8,128)(2,1)S(1)} %collective-permute-done.refs_3_, ...), custom_call_target="tpu_custom_call" | custom-call | flops 436207616 | bytes 6291456 | tf_op jit(solution)/shard_map/pallas_call | solution.py:484
  78.7 11.1 %all_to_all.26.p_ref = bf16[16,64,128]{2,1,0:T(8,128)(2,1)S(1)} all-to-all(bf16[16,64,128]{2,1,0:T(8,128)(2,1)S(1)} %shard_map.83), channel_id=1, replica_groups=mesh['row'=8,'col'=16] {'col'}, dimensions={0} | all-to-all | bytes 524288 | tf_op jit(solution)/shard_map/all_to_all | solution.py:543
  90.6 12.6 %all_to_all.27.got = bf16[8,3,64,128]{3,2,1,0:T(8,128)(2,1)S(1)} all-to-all(bf16[8,3,64,128]{3,2,1,0:T(8,128)(2,1)S(1)} %shard_map.84), channel_id=1, replica_groups=mesh['row'=8,'col'=16] {'row'}, dimensions={0} | all-to-all | bytes 786432 | tf_op jit(solution)/shard_map/all_to_all | solution.py:545
  103.3 1.3 %collective-permute-start.8 = (bf16[192,128]{1,0:T(8,128)(2,1)S(1)}, bf16[192,128]{1,0:T(8,128)(2,1)S(1)}, u32[]{:S(2)}, u32[]{:S(2)}) collective-permute-start(bf16[192,128]{1,0:T(8,128)(2,1)S(1)} %get-tuple-element.35.refs_2_), channel_id=1, source_target_pairs={{0,1},{1,0},{2,3},{3,2},{4,5},{5,4},{6,7},{7,6},{8,9},{9,8},{10,11... | collective-permute-start | bytes 147464 | tf_op jit(solution)/shard_map/ppermute | solution.py:537
  104.5 2.2 %collective-permute-start.9 = (bf16[192,128]{1,0:T(8,128)(2,1)S(1)}, bf16[192,128]{1,0:T(8,128)(2,1)S(1)}, u32[]{:S(2)}, u32[]{:S(2)}) collective-permute-start(bf16[192,128]{1,0:T(8,128)(2,1)S(1)} %get-tuple-element.35.refs_2_), channel_id=1, source_target_pairs={{1,2},{2,1},{3,4},{4,3},{5,6},{6,5},{7,8},{8,7},{9,10},{10,9},{11,... | collective-permute-start | bytes 147464 | tf_op jit(solution)/shard_map/ppermute | solution.py:538
  106.8 3.2 %collective-permute-done.9.refs_4_ = bf16[192,128]{1,0:T(8,128)(2,1)S(1)} collective-permute-done((bf16[192,128]{1,0:T(8,128)(2,1)S(1)}, bf16[192,128]{1,0:T(8,128)(2,1)S(1)}, u32[]{:S(2)}, u32[]{:S(2)}) %collective-permute-start.9) | collective-permute-done | bytes 49184 | tf_op jit(solution)/shard_map/ppermute | solution.py:538
  109.9 5.9 %shard_map.86 = (bf16[64,128]{1,0:T(8,128)(2,1)}, f32[1024,128]{1,0:T(8,128)}) custom-call(s32[1]{0:T(128)} %bitcast.parity.refs_0_, f32[64,128]{1,0:T(8,128)S(1)} %get-tuple-element.34.refs_1_, bf16[192,128]{1,0:T(8,128)(2,1)S(1)} %get-tuple-element.35.refs_2_, bf16[192,128]{1,0:T(8,128)(2,1)S(1)} %collective-permute-done.8.refs_3_, ...), custom_call_target="tpu_custom_call" | custom-call | flops 436207616 | bytes 6291456 | tf_op jit(solution)/shard_map/pallas_call | solution.py:484
  (21 shorter events, 1.9 us)
Async XLA Ops:
  0.6 72.8 %copy-start.3 = (bf16[64,128]{1,0:T(8,128)(2,1)S(1)}, bf16[64,128]{1,0:T(8,128)(2,1)}, u32[]{:S(2)}) copy-start(bf16[64,128]{1,0:T(8,128)(2,1)} %refs_7_.3) | copy-start | bytes 49156
  2.9 53.5 %collective-permute-start.2 = (bf16[2064,128]{1,0:T(8,128)(2,1)}, bf16[2064,128]{1,0:T(8,128)(2,1)S(1)}, u32[]{:S(2)}, u32[]{:S(2)}) collective-permute-start(bf16[2064,128]{1,0:T(8,128)(2,1)} %get-tuple-element.25), channel_id=1, source_target_pairs={{0,16},{16,32},{32,48},{48,64},{64,80},{80,96},{96,112},{1,17},{17... | collective-permute-start | bytes 1585160 | tf_op jit(solution)/shard_map/ppermute | solution.py:527
  6.9 49.5 %collective-permute-start.3 = (bf16[2064,128]{1,0:T(8,128)(2,1)}, bf16[2064,128]{1,0:T(8,128)(2,1)S(1)}, u32[]{:S(2)}, u32[]{:S(2)}) collective-permute-start(bf16[2064,128]{1,0:T(8,128)(2,1)} %get-tuple-element.26), channel_id=1, source_target_pairs={{16,0},{32,16},{48,32},{64,48},{80,64},{96,80},{112,96},{17,1},{33... | collective-permute-start | bytes 1585160 | tf_op jit(solution)/shard_map/ppermute | solution.py:528
  25.9 15.6 %all-to-all-start = ((bf16[16,80,128]{2,1,0:T(8,128)(2,1)}), bf16[16,80,128]{2,1,0:T(8,128)(2,1)S(1)}, u32[]{:S(2)}, u32[]{:S(2)}) async-start(bf16[16,80,128]{2,1,0:T(8,128)(2,1)} %get-tuple-element.20), calls=%async_computation | async-start | bytes 655360 | tf_op jit(solution)/shard_map/all_to_all | solution.py:522
  34.9 33.0 %collective-permute-start.6 = (bf16[2048,128]{1,0:T(8,128)(2,1)S(1)}, bf16[2048,128]{1,0:T(8,128)(2,1)}, u32[]{:S(2)}, u32[]{:S(2)}) collective-permute-start(bf16[2048,128]{1,0:T(8,128)(2,1)S(1)} %get-tuple-element.31), channel_id=1, source_target_pairs={{0,1},{1,0},{2,3},{3,2},{4,5},{5,4},{6,7},{7,6},{8,9},{9,8},{10,11... | collective-permute-start | bytes 1572872 | tf_op jit(solution)/shard_map/ppermute | solution.py:524
  35.1 34.9 %collective-permute-start.7 = (bf16[2048,128]{1,0:T(8,128)(2,1)S(1)}, bf16[2048,128]{1,0:T(8,128)(2,1)}, u32[]{:S(2)}, u32[]{:S(2)}) collective-permute-start(bf16[2048,128]{1,0:T(8,128)(2,1)S(1)} %get-tuple-element.32), channel_id=1, source_target_pairs={{1,2},{2,1},{3,4},{4,3},{5,6},{6,5},{7,8},{8,7},{9,10},{10,9},{11,... | collective-permute-start | bytes 1572872 | tf_op jit(solution)/shard_map/ppermute | solution.py:525
  50.1 16.6 %all-to-all-start.2 = ((bf16[8,3,64,128]{3,2,1,0:T(8,128)(2,1)}), bf16[8,3,64,128]{3,2,1,0:T(8,128)(2,1)S(1)}, u32[]{:S(2)}, u32[]{:S(2)}) async-start(bf16[8,3,64,128]{3,2,1,0:T(8,128)(2,1)} %get-tuple-element.22), calls=%async_computation.2 | async-start | bytes 786432 | tf_op jit(solution)/shard_map/all_to_all | solution.py:530
  56.4 17.0 %copy-start = (bf16[2064,128]{1,0:T(8,128)(2,1)}, bf16[2064,128]{1,0:T(8,128)(2,1)S(1)}, u32[]{:S(2)}) copy-start(bf16[2064,128]{1,0:T(8,128)(2,1)S(1)} %collective-permute-done.2.prev.refs_10_) | copy-start | bytes 1585156
  56.4 17.0 %copy-start.1 = (bf16[2064,128]{1,0:T(8,128)(2,1)}, bf16[2064,128]{1,0:T(8,128)(2,1)S(1)}, u32[]{:S(2)}) copy-start(bf16[2064,128]{1,0:T(8,128)(2,1)S(1)} %collective-permute-done.3.nxt.refs_11_) | copy-start | bytes 1585156
  57.9 15.5 %collective-permute-start.4 = (bf16[1072,128]{1,0:T(8,128)(2,1)}, bf16[1072,128]{1,0:T(8,128)(2,1)S(1)}, u32[]{:S(2)}, u32[]{:S(2)}) collective-permute-start(bf16[1072,128]{1,0:T(8,128)(2,1)} %get-tuple-element.28), channel_id=1, source_target_pairs={{0,1},{1,0},{2,3},{3,2},{4,5},{5,4},{6,7},{7,6},{8,9},{9,8},{10,11... | collective-permute-start | bytes 823304 | tf_op jit(solution)/shard_map/ppermute | solution.py:532
  58.6 14.8 %collective-permute-start.5 = (bf16[1072,128]{1,0:T(8,128)(2,1)S(1)}, bf16[1072,128]{1,0:T(8,128)(2,1)S(1)}, u32[]{:S(2)}, u32[]{:S(2)}) collective-permute-start(bf16[1072,128]{1,0:T(8,128)(2,1)S(1)} %get-tuple-element.29), channel_id=1, source_target_pairs={{1,2},{2,1},{3,4},{4,3},{5,6},{6,5},{7,8},{8,7},{9,10},{10,9},{11,... | collective-permute-start | bytes 823304 | tf_op jit(solution)/shard_map/ppermute | solution.py:533
  66.7 23.0 %copy-start.2 = (bf16[16,128,1024]{2,1,0:T(8,128)(2,1)S(1)}, bf16[16,128,1024]{2,1,0:T(8,128)(2,1)}, u32[]{:S(2)}) copy-start(bf16[16,128,1024]{2,1,0:T(8,128)(2,1)} %get-tuple-element.33.k_ref) | copy-start | bytes 12582916
  66.8 3.2 %collective-permute-start = (bf16[192,128]{1,0:T(8,128)(2,1)S(1)}, bf16[192,128]{1,0:T(8,128)(2,1)S(1)}, u32[]{:S(2)}, u32[]{:S(2)}) collective-permute-start(bf16[192,128]{1,0:T(8,128)(2,1)S(1)} %get-tuple-element.24.refs_2_), channel_id=1, source_target_pairs={{0,1},{1,0},{2,3},{3,2},{4,5},{5,4},{6,7},{7,6},{8,9},{9,8},{10,11... | collective-permute-start | bytes 147464 | tf_op jit(solution)/shard_map/ppermute | solution.py:537
  67.9 5.5 %collective-permute-start.1 = (bf16[192,128]{1,0:T(8,128)(2,1)S(1)}, bf16[192,128]{1,0:T(8,128)(2,1)S(1)}, u32[]{:S(2)}, u32[]{:S(2)}) collective-permute-start(bf16[192,128]{1,0:T(8,128)(2,1)S(1)} %get-tuple-element.24.refs_2_), channel_id=1, source_target_pairs={{1,2},{2,1},{3,4},{4,3},{5,6},{6,5},{7,8},{8,7},{9,10},{10,9},{11,... | collective-permute-start | bytes 147464 | tf_op jit(solution)/shard_map/ppermute | solution.py:538
  103.3 3.5 %collective-permute-start.8 = (bf16[192,128]{1,0:T(8,128)(2,1)S(1)}, bf16[192,128]{1,0:T(8,128)(2,1)S(1)}, u32[]{:S(2)}, u32[]{:S(2)}) collective-permute-start(bf16[192,128]{1,0:T(8,128)(2,1)S(1)} %get-tuple-element.35.refs_2_), channel_id=1, source_target_pairs={{0,1},{1,0},{2,3},{3,2},{4,5},{5,4},{6,7},{7,6},{8,9},{9,8},{10,11... | collective-permute-start | bytes 147464 | tf_op jit(solution)/shard_map/ppermute | solution.py:537
  104.5 5.4 %collective-permute-start.9 = (bf16[192,128]{1,0:T(8,128)(2,1)S(1)}, bf16[192,128]{1,0:T(8,128)(2,1)S(1)}, u32[]{:S(2)}, u32[]{:S(2)}) collective-permute-start(bf16[192,128]{1,0:T(8,128)(2,1)S(1)} %get-tuple-element.35.refs_2_), channel_id=1, source_target_pairs={{1,2},{2,1},{3,4},{4,3},{5,6},{6,5},{7,8},{8,7},{9,10},{10,9},{11,... | collective-permute-start | bytes 147464 | tf_op jit(solution)/shard_map/ppermute | solution.py:538

commit v6 on v5

--- a/solution.py
+++ b/solution.py
@@ -31,11 +31,11 @@
     return lax.dot_general(a, b, dims, preferred_element_type=F32)
 
 
-def call(body, out_shape, *, limit=24 * MB, flops=0, moved=0, **kwargs):
+def call(body, out_shape, *, limit=24 * MB, flops=0, moved=0, flags=None, **kwargs):
     return pl.pallas_call(
         body,
         out_shape=out_shape,
-        compiler_params=pltpu.CompilerParams(vmem_limit_bytes=limit),
+        compiler_params=pltpu.CompilerParams(vmem_limit_bytes=limit, **({"flags": flags} if flags else {})),
         cost_estimate=pl.CostEstimate(flops=flops, bytes_accessed=moved, transcendentals=0),
         **kwargs,
     )
@@ -359,12 +359,14 @@
             return mid_metas[16 * br : 16 * br + 16].astype(F32)
         return (far_a, far_b)[bc // 2][TAIL + 16 * br : TAIL + 16 * br + 16].astype(F32)
 
-    moves_v[...] = jnp.zeros_like(moves_v)
-    for br in range(3):
-        for bc in range(3):
-            o = meta(br, bc)[2:3]
-            o = o + 5.0 * (jnp.where(o >= 3.0, 1.0, 0.0) + jnp.where(o >= 6.0, 1.0, 0.0))
-            moves_v[3 * br + bc : 3 * br + bc + 1] = o.astype(jnp.int32)
+    rows = []
+    for b in range(9):
+        o = meta(b // 3, b % 3)[2:3]
+        rows.append(o + 5.0 * (jnp.where(o >= 3.0, 1.0, 0.0) + jnp.where(o >= 6.0, 1.0, 0.0)))
+    lane = lax.broadcasted_iota(jnp.int32, (1, U), 1)
+    for n in range(5):
+        value = rows[2 * n] if n == 4 else jnp.where(lane < 64, rows[2 * n], pltpu.roll(rows[2 * n + 1], 64, 1))
+        moves_v[n : n + 1] = value.astype(jnp.int32)
     loads[0].start()
     line = lax.broadcasted_iota(jnp.int32, (S, U), 0).astype(F32)
 
@@ -406,7 +408,7 @@
         total = None
         for h in range(2):
             ks = (2 * h, 2 * h + 1)
-            x = jnp.concatenate([values[base + moves[block, tile * 4 + k]] for k in ks], axis=1)
+            x = jnp.concatenate([values[base + moves[block // 2, block % 2 * 64 + tile * 4 + k]] for k in ks], axis=1)
             a = [ref[start + k * S : start + k * S + S, :] for k in ks]
             y = dot(x, jnp.concatenate(a, axis=1), NT)
             total = y if total is None else total + y
@@ -498,8 +500,8 @@
             pltpu.VMEM((4 * ROWS, S), BF),
             pltpu.VMEM((4 * ROWS, S), BF),
             pltpu.VMEM((4 * ROWS, S), BF),
-            pltpu.VMEM((16, U), jnp.int32),
-            pltpu.SMEM((16, U), jnp.int32),
+            pltpu.VMEM((5, U), jnp.int32),
+            pltpu.SMEM((5, U), jnp.int32),
             pltpu.SemaphoreType.DMA((6,)),
         ],
     )(*args[:9], *keep(*args[9:]))
@@ -534,8 +536,8 @@
     for outer in range(2):
         last = outer == 1
         own, mid = near(got)
+        near_b = lax.ppermute(mid, "col", swap_b)
         near_a = lax.ppermute(mid, "col", swap_a)
-        near_b = lax.ppermute(mid, "col", swap_b)
         out = sweep(
             last, parity, own, mid, near_a, near_b, far_a, far_b, incident, metas, tiles, prev, nxt, edge_a, edge_b
         )

time: 117 us -> 116 us (level)
  no operation moved by 1% of the time
where the time goes in v6:
time: 116 us
  blocking collectives  39.9 us (34%)
  starting transfers between devices  32.2 us (28%)
  Pallas kernels  27.1 us (23%)
  waiting for transfers between devices  15.7 us (14%)
    all_to_all x1, blocking collectives, per_device(): rows = lax.all_to_all(rows, 'row', 0, 0, tiled=True)  16.2 us
    all_to_all x1, blocking collectives, per_device(): got = lax.all_to_all(partials, 'row', 0, 0, tiled=True)  12.6 us
    all_to_all x1, blocking collectives, per_device(): out = lax.all_to_all(out, 'col', 0, 0, tiled=True)  11.1 us
    pallas_call x2, Pallas kernels, sweep(): call(body, out, flops=2 * E * S * S * 4 * 52, moved=6 * MB, in_specs=[IN_...  10.9 us
    pallas_call x1, Pallas kernels, make_kernel(): call(kernel_body, (hbm((NC, U, NR * U), BF), hbm((NR, 3, E, U), BF)), flo...  8.59 us
    all_to_all x1, starting transfers between devices, per_device(): cols = lax.all_to_all(cols, 'col', 0, 0, tiled=True)  7.6 us
    ppermute x2, waiting for transfers between devices, per_device(): near_b = lax.ppermute(mid, 'col', swap_b)  6.58 us
    all_to_all x1, starting transfers between devices, per_device(): got = lax.all_to_all(partials, 'row', 0, 0, tiled=True)  6.27 us
  transfers between devices with their start and end apart: 12, of which 4 were waited for; matrix products, arithmetic and copies ran while one was open for 0% of the time, Pallas kernels for 11%

profile of v6, /device:TPU:1, one launch (start us, length us, event | category | flops | bytes accessed | tf_op | source)
XLA Modules:
  0.0 115.6 jit_solution(10747008986302507238)
XLA Ops:
  0.6 2.3 %shard_map.80 = (bf16[2064,128]{1,0:T(8,128)(2,1)}, bf16[2064,128]{1,0:T(8,128)(2,1)}, bf16[16,128]{1,0:T(8,128)(2,1)S(1)}) custom-call(s32[1,128]{1,0:T(1,128)} %bitcast.8, s32[4,4,4]{2,1,0:T(4,128)} %columns_h.1, bf16[8192,128]{1,0:T(8,128)(2,1)} %bitcast.4), custom_call_target="tpu_custom_call" | custom-call | bytes 2097152 | tf_op jit(solution)/shard_map/pallas_call | solution.py:140
  2.9 4.0 %collective-permute-start.2 = (bf16[2064,128]{1,0:T(8,128)(2,1)}, bf16[2064,128]{1,0:T(8,128)(2,1)S(1)}, u32[]{:S(2)}, u32[]{:S(2)}) collective-permute-start(bf16[2064,128]{1,0:T(8,128)(2,1)} %get-tuple-element.25), channel_id=1, source_target_pairs={{0,16},{16,32},{32,48},{48,64},{64,80},{80,96},{96,112},{1,17},{17... | collective-permute-start | bytes 1585160 | tf_op jit(solution)/shard_map/ppermute | solution.py:529
  6.9 1.3 %collective-permute-start.3 = (bf16[2064,128]{1,0:T(8,128)(2,1)}, bf16[2064,128]{1,0:T(8,128)(2,1)S(1)}, u32[]{:S(2)}, u32[]{:S(2)}) collective-permute-start(bf16[2064,128]{1,0:T(8,128)(2,1)} %get-tuple-element.26), channel_id=1, source_target_pairs={{16,0},{32,16},{48,32},{64,48},{80,64},{96,80},{112,96},{17,1},{33... | collective-permute-start | bytes 1585160 | tf_op jit(solution)/shard_map/ppermute | solution.py:530
  8.2 1.5 %shard_map.77 = (bf16[8,48,128]{2,1,0:T(8,128)(2,1)}, bf16[16,80,128]{2,1,0:T(8,128)(2,1)}) custom-call(bf16[64,128]{1,0:T(8,128)(2,1)} %traces_h.1, f32[3,128]{1,0:T(4,128)} %points_h.1), custom_call_target="tpu_custom_call" | custom-call | tf_op jit(solution)/shard_map/pallas_call | solution.py:105
  9.7 16.2 %all_to_all.25.row_ref = bf16[8,48,128]{2,1,0:T(8,128)(2,1)} all-to-all(bf16[8,48,128]{2,1,0:T(8,128)(2,1)} %get-tuple-element.21), channel_id=1, replica_groups=mesh['row'=8,'col'=16] {'row'}, dimensions={0} | all-to-all | bytes 196608 | tf_op jit(solution)/shard_map/all_to_all | solution.py:523
  25.9 7.6 %all-to-all-start = ((bf16[16,80,128]{2,1,0:T(8,128)(2,1)}), bf16[16,80,128]{2,1,0:T(8,128)(2,1)S(1)}, u32[]{:S(2)}, u32[]{:S(2)}) async-start(bf16[16,80,128]{2,1,0:T(8,128)(2,1)} %get-tuple-element.20), calls=%async_computation | async-start | bytes 655360 | tf_op jit(solution)/shard_map/all_to_all | solution.py:524
  33.5 1.3 %shard_map.82 = (bf16[2048,128]{1,0:T(8,128)(2,1)S(1)}, bf16[2048,128]{1,0:T(8,128)(2,1)S(1)}) custom-call(s32[1]{0:T(128)} %bitcast.parity.refs_0_, bf16[8192,128]{1,0:T(8,128)(2,1)} %bitcast.5), custom_call_target="tpu_custom_call" | custom-call | bytes 2097152 | tf_op jit(solution)/shard_map/pallas_call | solution.py:173
  35.1 3.5 %collective-permute-start.7 = (bf16[2048,128]{1,0:T(8,128)(2,1)S(1)}, bf16[2048,128]{1,0:T(8,128)(2,1)}, u32[]{:S(2)}, u32[]{:S(2)}) collective-permute-start(bf16[2048,128]{1,0:T(8,128)(2,1)S(1)} %get-tuple-element.32), channel_id=1, source_target_pairs={{1,2},{2,1},{3,4},{4,3},{5,6},{6,5},{7,8},{8,7},{9,10},{10,9},{11,... | collective-permute-start | bytes 1572872 | tf_op jit(solution)/shard_map/ppermute | solution.py:527
  38.6 2.9 %all-to-all-done.col_ref = bf16[16,80,128]{2,1,0:T(8,128)(2,1)S(1)} async-done(((bf16[16,80,128]{2,1,0:T(8,128)(2,1)}), bf16[16,80,128]{2,1,0:T(8,128)(2,1)S(1)}, u32[]{:S(2)}, u32[]{:S(2)}) %all-to-all-start) | async-done | bytes 327712 | tf_op jit(solution)/shard_map/all_to_all | solution.py:524
  41.5 8.6 %shard_map.78 = (bf16[16,128,1024]{2,1,0:T(8,128)(2,1)}, bf16[8,3,64,128]{3,2,1,0:T(8,128)(2,1)}) custom-call(bf16[16,80,128]{2,1,0:T(8,128)(2,1)S(1)} %all-to-all-done.col_ref, bf16[8,48,128]{2,1,0:T(8,128)(2,1)} %all_to_all.25.row_ref), custom_call_target="tpu_custom_call" | custom-call | flops 83886080 | bytes 6291456 | tf_op jit(solution)/shard_map/pallas_call | solution.py:299
  50.1 6.3 %all-to-all-start.2 = ((bf16[8,3,64,128]{3,2,1,0:T(8,128)(2,1)}), bf16[8,3,64,128]{3,2,1,0:T(8,128)(2,1)S(1)}, u32[]{:S(2)}, u32[]{:S(2)}) async-start(bf16[8,3,64,128]{3,2,1,0:T(8,128)(2,1)} %get-tuple-element.22), calls=%async_computation.2 | async-start | bytes 786432 | tf_op jit(solution)/shard_map/all_to_all | solution.py:532
  56.4 1.5 %shard_map.81 = (bf16[1072,128]{1,0:T(8,128)(2,1)}, bf16[1072,128]{1,0:T(8,128)(2,1)S(1)}, bf16[48,128]{1,0:T(8,128)(2,1)S(1)}) custom-call(s32[1]{0:T(128)} %bitcast.parity.refs_0_, bf16[2064,128]{1,0:T(8,128)(2,1)S(1)} %collective-permute-done.2.prev.refs_10_, bf16[2064,128]{1,0:T(8,128)(2,1)S(1)} %collective-permute-done.3.nxt.refs_11_, ...), custom_call_target="tpu_custom_call" | custom-call | bytes 2097152 | tf_op jit(solution)/shard_map/pallas_call | solution.py:207
  58.6 1.9 %collective-permute-start.5 = (bf16[1072,128]{1,0:T(8,128)(2,1)S(1)}, bf16[1072,128]{1,0:T(8,128)(2,1)S(1)}, u32[]{:S(2)}, u32[]{:S(2)}) collective-permute-start(bf16[1072,128]{1,0:T(8,128)(2,1)S(1)} %get-tuple-element.29), channel_id=1, source_target_pairs={{1,2},{2,1},{3,4},{4,3},{5,6},{6,5},{7,8},{8,7},{9,10},{10,9},{11,... | collective-permute-start | bytes 823304 | tf_op jit(solution)/shard_map/ppermute | solution.py:535
  60.6 6.2 %all-to-all-done.2.got = bf16[8,3,64,128]{3,2,1,0:T(8,128)(2,1)S(1)} async-done(((bf16[8,3,64,128]{3,2,1,0:T(8,128)(2,1)}), bf16[8,3,64,128]{3,2,1,0:T(8,128)(2,1)S(1)}, u32[]{:S(2)}, u32[]{:S(2)}) %all-to-all-start.2) | async-done | bytes 393248 | tf_op jit(solution)/shard_map/all_to_all | solution.py:532
  66.8 1.1 collective-permute-start
  67.9 2.1 %collective-permute-start.1 = (bf16[192,128]{1,0:T(8,128)(2,1)S(1)}, bf16[192,128]{1,0:T(8,128)(2,1)S(1)}, u32[]{:S(2)}, u32[]{:S(2)}) collective-permute-start(bf16[192,128]{1,0:T(8,128)(2,1)S(1)} %get-tuple-element.24.refs_2_), channel_id=1, source_target_pairs={{1,2},{2,1},{3,4},{4,3},{5,6},{6,5},{7,8},{8,7},{9,10},{10,9},{11,... | collective-permute-start | bytes 147464 | tf_op jit(solution)/shard_map/ppermute | solution.py:539
  70.0 3.4 %collective-permute-done.1.refs_4_ = bf16[192,128]{1,0:T(8,128)(2,1)S(1)} collective-permute-done((bf16[192,128]{1,0:T(8,128)(2,1)S(1)}, bf16[192,128]{1,0:T(8,128)(2,1)S(1)}, u32[]{:S(2)}, u32[]{:S(2)}) %collective-permute-start.1) | collective-permute-done | bytes 49184 | tf_op jit(solution)/shard_map/ppermute | solution.py:539
  73.4 5.1 %shard_map.83 = bf16[16,64,128]{2,1,0:T(8,128)(2,1)S(1)} custom-call(s32[1]{0:T(128)} %bitcast.parity.refs_0_, f32[64,128]{1,0:T(8,128)S(1)} %get-tuple-element.23.refs_1_, bf16[192,128]{1,0:T(8,128)(2,1)S(1)} %get-tuple-element.24.refs_2_, bf16[192,128]{1,0:T(8,128)(2,1)S(1)} %collective-permute-done.refs_3_, ...), custom_call_target="tpu_custom_call" | custom-call | flops 436207616 | bytes 6291456 | tf_op jit(solution)/shard_map/pallas_call | solution.py:486
  78.6 11.1 %all_to_all.26.p_ref = bf16[16,64,128]{2,1,0:T(8,128)(2,1)S(1)} all-to-all(bf16[16,64,128]{2,1,0:T(8,128)(2,1)S(1)} %shard_map.83), channel_id=1, replica_groups=mesh['row'=8,'col'=16] {'col'}, dimensions={0} | all-to-all | bytes 524288 | tf_op jit(solution)/shard_map/all_to_all | solution.py:545
  90.5 12.6 %all_to_all.27.got = bf16[8,3,64,128]{3,2,1,0:T(8,128)(2,1)S(1)} all-to-all(bf16[8,3,64,128]{3,2,1,0:T(8,128)(2,1)S(1)} %shard_map.84), channel_id=1, replica_groups=mesh['row'=8,'col'=16] {'row'}, dimensions={0} | all-to-all | bytes 786432 | tf_op jit(solution)/shard_map/all_to_all | solution.py:547
  103.2 1.3 %collective-permute-start.8 = (bf16[192,128]{1,0:T(8,128)(2,1)S(1)}, bf16[192,128]{1,0:T(8,128)(2,1)S(1)}, u32[]{:S(2)}, u32[]{:S(2)}) collective-permute-start(bf16[192,128]{1,0:T(8,128)(2,1)S(1)} %get-tuple-element.35.refs_2_), channel_id=1, source_target_pairs={{0,1},{1,0},{2,3},{3,2},{4,5},{5,4},{6,7},{7,6},{8,9},{9,8},{10,11... | collective-permute-start | bytes 147464 | tf_op jit(solution)/shard_map/ppermute | solution.py:540
  104.4 2.2 %collective-permute-start.9 = (bf16[192,128]{1,0:T(8,128)(2,1)S(1)}, bf16[192,128]{1,0:T(8,128)(2,1)S(1)}, u32[]{:S(2)}, u32[]{:S(2)}) collective-permute-start(bf16[192,128]{1,0:T(8,128)(2,1)S(1)} %get-tuple-element.35.refs_2_), channel_id=1, source_target_pairs={{1,2},{2,1},{3,4},{4,3},{5,6},{6,5},{7,8},{8,7},{9,10},{10,9},{11,... | collective-permute-start | bytes 147464 | tf_op jit(solution)/shard_map/ppermute | solution.py:539
  106.6 3.2 %collective-permute-done.9.refs_4_ = bf16[192,128]{1,0:T(8,128)(2,1)S(1)} collective-permute-done((bf16[192,128]{1,0:T(8,128)(2,1)S(1)}, bf16[192,128]{1,0:T(8,128)(2,1)S(1)}, u32[]{:S(2)}, u32[]{:S(2)}) %collective-permute-start.9) | collective-permute-done | bytes 49184 | tf_op jit(solution)/shard_map/ppermute | solution.py:539
  109.8 5.8 %shard_map.86 = (bf16[64,128]{1,0:T(8,128)(2,1)}, f32[1024,128]{1,0:T(8,128)}) custom-call(s32[1]{0:T(128)} %bitcast.parity.refs_0_, f32[64,128]{1,0:T(8,128)S(1)} %get-tuple-element.34.refs_1_, bf16[192,128]{1,0:T(8,128)(2,1)S(1)} %get-tuple-element.35.refs_2_, bf16[192,128]{1,0:T(8,128)(2,1)S(1)} %collective-permute-done.8.refs_3_, ...), custom_call_target="tpu_custom_call" | custom-call | flops 436207616 | bytes 6291456 | tf_op jit(solution)/shard_map/pallas_call | solution.py:486
  (21 shorter events, 1.9 us)
Async XLA Ops:
  0.6 72.8 %copy-start.3 = (bf16[64,128]{1,0:T(8,128)(2,1)S(1)}, bf16[64,128]{1,0:T(8,128)(2,1)}, u32[]{:S(2)}) copy-start(bf16[64,128]{1,0:T(8,128)(2,1)} %refs_7_.3) | copy-start | bytes 49156
  2.9 53.5 %collective-permute-start.2 = (bf16[2064,128]{1,0:T(8,128)(2,1)}, bf16[2064,128]{1,0:T(8,128)(2,1)S(1)}, u32[]{:S(2)}, u32[]{:S(2)}) collective-permute-start(bf16[2064,128]{1,0:T(8,128)(2,1)} %get-tuple-element.25), channel_id=1, source_target_pairs={{0,16},{16,32},{32,48},{48,64},{64,80},{80,96},{96,112},{1,17},{17... | collective-permute-start | bytes 1585160 | tf_op jit(solution)/shard_map/ppermute | solution.py:529
  6.9 49.5 %collective-permute-start.3 = (bf16[2064,128]{1,0:T(8,128)(2,1)}, bf16[2064,128]{1,0:T(8,128)(2,1)S(1)}, u32[]{:S(2)}, u32[]{:S(2)}) collective-permute-start(bf16[2064,128]{1,0:T(8,128)(2,1)} %get-tuple-element.26), channel_id=1, source_target_pairs={{16,0},{32,16},{48,32},{64,48},{80,64},{96,80},{112,96},{17,1},{33... | collective-permute-start | bytes 1585160 | tf_op jit(solution)/shard_map/ppermute | solution.py:530
  25.9 15.6 %all-to-all-start = ((bf16[16,80,128]{2,1,0:T(8,128)(2,1)}), bf16[16,80,128]{2,1,0:T(8,128)(2,1)S(1)}, u32[]{:S(2)}, u32[]{:S(2)}) async-start(bf16[16,80,128]{2,1,0:T(8,128)(2,1)} %get-tuple-element.20), calls=%async_computation | async-start | bytes 655360 | tf_op jit(solution)/shard_map/all_to_all | solution.py:524
  34.9 33.0 %collective-permute-start.6 = (bf16[2048,128]{1,0:T(8,128)(2,1)S(1)}, bf16[2048,128]{1,0:T(8,128)(2,1)}, u32[]{:S(2)}, u32[]{:S(2)}) collective-permute-start(bf16[2048,128]{1,0:T(8,128)(2,1)S(1)} %get-tuple-element.31), channel_id=1, source_target_pairs={{0,1},{1,0},{2,3},{3,2},{4,5},{5,4},{6,7},{7,6},{8,9},{9,8},{10,11... | collective-permute-start | bytes 1572872 | tf_op jit(solution)/shard_map/ppermute | solution.py:526
  35.1 34.9 %collective-permute-start.7 = (bf16[2048,128]{1,0:T(8,128)(2,1)S(1)}, bf16[2048,128]{1,0:T(8,128)(2,1)}, u32[]{:S(2)}, u32[]{:S(2)}) collective-permute-start(bf16[2048,128]{1,0:T(8,128)(2,1)S(1)} %get-tuple-element.32), channel_id=1, source_target_pairs={{1,2},{2,1},{3,4},{4,3},{5,6},{6,5},{7,8},{8,7},{9,10},{10,9},{11,... | collective-permute-start | bytes 1572872 | tf_op jit(solution)/shard_map/ppermute | solution.py:527
  50.1 16.6 %all-to-all-start.2 = ((bf16[8,3,64,128]{3,2,1,0:T(8,128)(2,1)}), bf16[8,3,64,128]{3,2,1,0:T(8,128)(2,1)S(1)}, u32[]{:S(2)}, u32[]{:S(2)}) async-start(bf16[8,3,64,128]{3,2,1,0:T(8,128)(2,1)} %get-tuple-element.22), calls=%async_computation.2 | async-start | bytes 786432 | tf_op jit(solution)/shard_map/all_to_all | solution.py:532
  56.4 17.0 %copy-start = (bf16[2064,128]{1,0:T(8,128)(2,1)}, bf16[2064,128]{1,0:T(8,128)(2,1)S(1)}, u32[]{:S(2)}) copy-start(bf16[2064,128]{1,0:T(8,128)(2,1)S(1)} %collective-permute-done.2.prev.refs_10_) | copy-start | bytes 1585156
  56.4 17.0 %copy-start.1 = (bf16[2064,128]{1,0:T(8,128)(2,1)}, bf16[2064,128]{1,0:T(8,128)(2,1)S(1)}, u32[]{:S(2)}) copy-start(bf16[2064,128]{1,0:T(8,128)(2,1)S(1)} %collective-permute-done.3.nxt.refs_11_) | copy-start | bytes 1585156
  57.9 15.5 %collective-permute-start.4 = (bf16[1072,128]{1,0:T(8,128)(2,1)}, bf16[1072,128]{1,0:T(8,128)(2,1)S(1)}, u32[]{:S(2)}, u32[]{:S(2)}) collective-permute-start(bf16[1072,128]{1,0:T(8,128)(2,1)} %get-tuple-element.28), channel_id=1, source_target_pairs={{0,1},{1,0},{2,3},{3,2},{4,5},{5,4},{6,7},{7,6},{8,9},{9,8},{10,11... | collective-permute-start | bytes 823304 | tf_op jit(solution)/shard_map/ppermute | solution.py:534
  58.6 14.8 %collective-permute-start.5 = (bf16[1072,128]{1,0:T(8,128)(2,1)S(1)}, bf16[1072,128]{1,0:T(8,128)(2,1)S(1)}, u32[]{:S(2)}, u32[]{:S(2)}) collective-permute-start(bf16[1072,128]{1,0:T(8,128)(2,1)S(1)} %get-tuple-element.29), channel_id=1, source_target_pairs={{1,2},{2,1},{3,4},{4,3},{5,6},{6,5},{7,8},{8,7},{9,10},{10,9},{11,... | collective-permute-start | bytes 823304 | tf_op jit(solution)/shard_map/ppermute | solution.py:535
  66.7 22.9 %copy-start.2 = (bf16[16,128,1024]{2,1,0:T(8,128)(2,1)S(1)}, bf16[16,128,1024]{2,1,0:T(8,128)(2,1)}, u32[]{:S(2)}) copy-start(bf16[16,128,1024]{2,1,0:T(8,128)(2,1)} %get-tuple-element.33.k_ref) | copy-start | bytes 12582916
  66.8 3.2 %collective-permute-start = (bf16[192,128]{1,0:T(8,128)(2,1)S(1)}, bf16[192,128]{1,0:T(8,128)(2,1)S(1)}, u32[]{:S(2)}, u32[]{:S(2)}) collective-permute-start(bf16[192,128]{1,0:T(8,128)(2,1)S(1)} %get-tuple-element.24.refs_2_), channel_id=1, source_target_pairs={{0,1},{1,0},{2,3},{3,2},{4,5},{5,4},{6,7},{7,6},{8,9},{9,8},{10,11... | collective-permute-start | bytes 147464 | tf_op jit(solution)/shard_map/ppermute | solution.py:540
  67.9 5.5 %collective-permute-start.1 = (bf16[192,128]{1,0:T(8,128)(2,1)S(1)}, bf16[192,128]{1,0:T(8,128)(2,1)S(1)}, u32[]{:S(2)}, u32[]{:S(2)}) collective-permute-start(bf16[192,128]{1,0:T(8,128)(2,1)S(1)} %get-tuple-element.24.refs_2_), channel_id=1, source_target_pairs={{1,2},{2,1},{3,4},{4,3},{5,6},{6,5},{7,8},{8,7},{9,10},{10,9},{11,... | collective-permute-start | bytes 147464 | tf_op jit(solution)/shard_map/ppermute | solution.py:539
  103.2 3.5 %collective-permute-start.8 = (bf16[192,128]{1,0:T(8,128)(2,1)S(1)}, bf16[192,128]{1,0:T(8,128)(2,1)S(1)}, u32[]{:S(2)}, u32[]{:S(2)}) collective-permute-start(bf16[192,128]{1,0:T(8,128)(2,1)S(1)} %get-tuple-element.35.refs_2_), channel_id=1, source_target_pairs={{0,1},{1,0},{2,3},{3,2},{4,5},{5,4},{6,7},{7,6},{8,9},{9,8},{10,11... | collective-permute-start | bytes 147464 | tf_op jit(solution)/shard_map/ppermute | solution.py:540
  104.4 5.4 %collective-permute-start.9 = (bf16[192,128]{1,0:T(8,128)(2,1)S(1)}, bf16[192,128]{1,0:T(8,128)(2,1)S(1)}, u32[]{:S(2)}, u32[]{:S(2)}) collective-permute-start(bf16[192,128]{1,0:T(8,128)(2,1)S(1)} %get-tuple-element.35.refs_2_), channel_id=1, source_target_pairs={{1,2},{2,1},{3,4},{4,3},{5,6},{6,5},{7,8},{8,7},{9,10},{10,9},{11,... | collective-permute-start | bytes 147464 | tf_op jit(solution)/shard_map/ppermute | solution.py:539
